TPU v7x, 256 devices: a whole 4x4x8 slice. The times are simulated.
256 devices in a mesh: seq: 64 (over z, y, core), dp: 4 (over x).
Axes of the slice: x: 4, y: 4, z: 8, core: 2. Of those that a mesh axis runs over, the one named last changes fastest.
Arguments:
- inputs: bfloat16 [4, 16384, 512], P('dp', 'seq'), may hold values from -16 to 16
- write_vecs: bfloat16 [4, 16384, 128], P('dp', 'seq'), may hold values from -6 to 6
- read_vecs: bfloat16 [4, 16384, 128], P('dp', 'seq'), may hold values from -0.5 to 0.5
- dt_code: int32 [4, 8, 16384], P('dp', None, 'seq'), may hold values from 1 to 81920
- a_rate: float32 [8], replicated, may hold values from 0.4 to 682.6667
- w_out: bfloat16 [512, 2560], replicated, may hold values from -0.125 to 0.125
- grad_out: bfloat16 [4, 16384, 2560], P('dp', 'seq'), may hold values from -0.59765625 to 0.59765625
Outputs:
- outputs: bfloat16 [4, 16384, 512], P('dp', 'seq')
- grad_inputs: bfloat16 [4, 16384, 512], P('dp', 'seq')
- grad_write: bfloat16 [4, 16384, 128], P('dp', 'seq')
- grad_read: bfloat16 [4, 16384, 128], P('dp', 'seq')
- grad_w_out: float32 [512, 2560], P('seq')
All inputs are finite; a program needn't handle non-finite values.
Results may differ from a plain program's by a relative error of at most 0.0055.
Values sent between devices are 32-bit elements; how exact they have to be, the bound alone decides.
No kernel may reach another device: no remote copies, remote signals or barrier semaphores. Data moves between devices by JAX's collectives and lax.ppermute only.
A program may use at most 128 MiB of HBM per device.

v0:
```python
import jax
import jax.numpy as jnp
from jax import lax
from jax.sharding import PartitionSpec as P

HEAD_DIM = 64
STATE = 128
LOCAL_HEADS = 8
GROUP = 128


highest = lax.Precision.HIGHEST


def entering(part, axis, combine, identity, reverse):
    count = lax.axis_size(axis)
    place = lax.axis_index(axis)
    ahead = count - 1 - place if reverse else place
    gathered = jax.tree.map(lambda a: lax.all_gather(a, axis), part)
    state = jax.tree.map(lambda a, e: jnp.zeros_like(a) + jnp.asarray(e, a.dtype), part, identity)

    def one(step, state):
        source = count - 1 - step if reverse else step
        return combine(
            state, jax.tree.map(lambda a: lax.dynamic_index_in_dim(a, source, 0, False), gathered)
        )

    return lax.fori_loop(0, ahead, one, state)


def combine(first_part, second_part):
    return (
        first_part[0] * second_part[0],
        second_part[0][:, None, None] * first_part[1] + second_part[1],
    )


def shards(inputs, write_vecs, read_vecs, dt_code, a_rate, w_out, grad_out):
    tokens = inputs.shape[1]
    seq_len = tokens * lax.axis_size("seq")
    blocks = tokens // GROUP
    decay_rate = a_rate / (8.0 * seq_len)
    log_decay = -(decay_rate[:, None] * dt_code[0].astype(jnp.float32))
    weight = jnp.sqrt(-jnp.expm1(2.0 * log_decay))
    weight_rows = weight.reshape(LOCAL_HEADS, blocks, GROUP).transpose(1, 2, 0)[..., None]
    cum_decay = jnp.cumsum(log_decay.reshape(LOCAL_HEADS, blocks, GROUP), axis=2)
    group_last = cum_decay[:, :, -1]
    group_edges = jnp.cumsum(group_last, axis=1)
    totals = jnp.exp(group_edges[:, -1])
    before = jnp.concatenate(
        [jnp.zeros((LOCAL_HEADS, 1), jnp.float32), group_edges[:, :-1]], axis=1
    )
    end_decay = jnp.exp(group_edges[:, -1:] - group_edges)
    start_decay = jnp.exp(before)
    weighted = (
        inputs[0].astype(jnp.float32).reshape(blocks, GROUP, LOCAL_HEADS, HEAD_DIM) * weight_rows
    )
    b_half = write_vecs[0].reshape(blocks, GROUP, STATE)
    c_half = read_vecs[0].reshape(blocks, GROUP, STATE)
    b_rows = b_half.astype(jnp.float32)
    c_rows = c_half.astype(jnp.float32)
    rows_at = lax.broadcasted_iota(jnp.int32, (GROUP, GROUP), 0)
    cols_at = lax.broadcasted_iota(jnp.int32, (GROUP, GROUP), 1)
    spread = cum_decay[:, :, :, None] - cum_decay[:, :, None, :]
    decay_mask = jnp.exp(jnp.where((rows_at >= cols_at)[None, None], spread, -jnp.inf))
    scores = jnp.einsum("kin,kjn->kij", c_half, b_half, preferred_element_type=jnp.float32)
    mixed = decay_mask * scores[None]
    tail_decay = jnp.exp(group_last[:, :, None] - cum_decay)
    tail_rows = tail_decay.transpose(1, 2, 0)[..., None]
    head_decay = jnp.exp(cum_decay).transpose(1, 2, 0)[..., None]
    tailed = weighted * tail_rows
    group_states = jnp.einsum("kjhp,kjn->khpn", tailed, b_rows, precision=highest)
    block_row = lax.broadcasted_iota(jnp.int32, (blocks, blocks), 0)
    block_col = lax.broadcasted_iota(jnp.int32, (blocks, blocks), 1)
    fwd_weights = jnp.exp(
        jnp.where(
            (block_col < block_row)[None], before[:, :, None] - group_edges[:, None, :], -jnp.inf
        )
    )
    bwd_weights = jnp.exp(
        jnp.where(
            (block_col > block_row)[None], before[:, None, :] - group_edges[:, :, None], -jnp.inf
        )
    )
    local_in = jnp.einsum("hkm,mhpn->khpn", fwd_weights, group_states, precision=highest)
    own_state = jnp.einsum("hm,mhpn->hpn", end_decay, group_states, precision=highest)
    grad_rows = grad_out[0]
    grad_y = lax.dot_general(
        grad_rows, w_out, (((1,), (1,)), ((), ())), preferred_element_type=jnp.float32
    ).astype(jnp.bfloat16)
    grad_heads = grad_y.astype(jnp.float32).reshape(blocks, GROUP, LOCAL_HEADS, HEAD_DIM)
    grad_decayed = grad_heads * head_decay
    adj_groups = jnp.einsum("kihp,kin->khpn", grad_decayed, c_rows, precision=highest)
    own_adj = jnp.einsum("hm,mhpn->hpn", start_decay, adj_groups, precision=highest)
    identity = (
        jnp.ones((LOCAL_HEADS,), jnp.float32),
        jnp.zeros((LOCAL_HEADS, HEAD_DIM, STATE), jnp.float32),
    )
    carried_in = entering((totals, own_state), "seq", combine, identity, False)[1]
    adj_later = entering((totals, own_adj), "seq", combine, identity, True)[1]
    state_in = local_in + start_decay.T[:, :, None, None] * carried_in[None]
    y_intra = jnp.einsum("hkij,kjhp->kihp", mixed, weighted, precision=highest)
    y_inter = jnp.einsum("kin,khpn->kihp", c_rows, state_in, precision=highest) * head_decay
    outputs = (y_intra + y_inter).reshape(1, tokens, LOCAL_HEADS * HEAD_DIM).astype(jnp.bfloat16)
    adj_in = (
        jnp.einsum("hkm,mhpn->khpn", bwd_weights, adj_groups, precision=highest)
        + end_decay.T[:, :, None, None] * adj_later[None]
    )
    grad_weighted = jnp.einsum("hkij,kihp->kjhp", mixed, grad_heads, precision=highest)
    grad_weighted = grad_weighted + tail_rows * jnp.einsum(
        "khpn,kjn->kjhp", adj_in, b_rows, precision=highest
    )
    grad_inputs = (
        (grad_weighted * weight_rows)
        .reshape(1, tokens, LOCAL_HEADS * HEAD_DIM)
        .astype(jnp.bfloat16)
    )
    pair_dots = decay_mask * jnp.einsum("kihp,kjhp->hkij", grad_heads, weighted, precision=highest)
    grad_read = jnp.einsum("hkij,kjn->kin", pair_dots, b_rows, precision=highest)
    grad_read = grad_read + jnp.einsum("kihp,khpn->kin", grad_decayed, state_in, precision=highest)
    grad_write = jnp.einsum("hkij,kin->kjn", pair_dots, c_rows, precision=highest)
    grad_write = grad_write + jnp.einsum("kjhp,khpn->kjn", tailed, adj_in, precision=highest)
    grad_read = grad_read.reshape(1, tokens, STATE).astype(jnp.bfloat16)
    grad_write = grad_write.reshape(1, tokens, STATE).astype(jnp.bfloat16)
    out_rows = outputs[0]
    share = lax.psum_scatter(
        lax.dot_general(
            out_rows, grad_rows, (((0,), (0,)), ((), ())), preferred_element_type=jnp.float32
        ),
        "seq",
        scatter_dimension=0,
        tiled=True,
    )
    grad_w_out = lax.psum(share, "dp")
    return (outputs, grad_inputs, grad_write, grad_read, grad_w_out)


def solution(mesh):
    placed = (
        P("dp", "seq", None),
        P("dp", "seq", None),
        P("dp", "seq", None),
        P("dp", None, "seq"),
        P(),
        P(),
        P("dp", "seq", None),
    )
    return jax.shard_map(
        shards,
        mesh=mesh,
        in_specs=placed,
        out_specs=(
            P("dp", "seq", None),
            P("dp", "seq", None),
            P("dp", "seq", None),
            P("dp", "seq", None),
            P("seq", None),
        ),
        check_vma=False,
    )
```

profile of v0, /device:TPU:32, one launch (start us, length us, event | category | flops | bytes accessed | tf_op | source)
XLA Modules:
  0.0 547.8 jit_solution(9119124222800775612)
XLA Ops:
  10.4 2.2 reshape.165
  12.6 1.5 copy.90
  15.3 2.7 fusion.29
  19.5 2.2 fusion.11
  24.8 3.4 fusion.25
  28.3 1.3 copy.95
  29.6 1.3 copy.168
  30.9 1.3 copy.91
  32.2 1.4 fusion.74
  34.8 1.3 bitcast_dynamic-update-slice_fusion
  36.1 115.3 %all-reduce.1 = f32[512]{0:T(512)} all-reduce(f32[512]{0:T(512)} %bitcast_dynamic-update-slice_fusion), channel_id=2, replica_groups=mesh['seq'=64,'dp'=4] {'seq'}, use_global_device_ids=true, to_apply=%add.1 | all-reduce | flops 512 | bytes 4096
  151.4 1.3 reshape.146
  155.6 3.9 fusion.27
  159.5 3.9 fusion.31
  163.5 14.4 %while.26 = (s32[]{:T(128)}, f32[8,64,128]{2,1,0:T(8,128)S(1)}, s32[]{:T(128)}, f32[64,8]{1,0:T(8,128)}, f32[64,8,64,128]{3,2,1,0:T(8,128)}, /*index=5*/s32[]{:T(128)}, s32[]{:T(128)}, s32[]{:T(128)}) while((s32[]{:T(128)}, f32[8,64,128]{2,1,0:T(8,128)S(1)}, s32[]{:T(128)}, f32[64,8]{1,0:T(8,128)}, f32[64,8,64,128]{3,2,1,0:T(8,128)}, ...), condition=%wide.region_3.4_spmd, body=%wide.region_2.3_spmd.sunk | while | flops 131077 | bytes 786663 | solution.py:28
  164.2 1.1 bitcast_add_fusion.10
  166.0 1.1 bitcast_add_fusion.10
  167.7 1.1 bitcast_add_fusion.10
  169.5 1.1 bitcast_add_fusion.10
  171.3 1.1 bitcast_add_fusion.10
  173.1 1.1 bitcast_add_fusion.10
  174.9 1.1 bitcast_add_fusion.10
  176.7 1.1 bitcast_add_fusion.10
  177.9 1.6 fusion.8
  179.5 3.1 fusion.10
  183.6 3.2 fusion
  186.9 2.5 fusion.4
  189.4 2.8 convolution_bitcast_fusion.4
  192.2 27.6 %all-gather.8.cloned.1.call-done = f32[512,64,128]{2,1,0:T(8,128)} async-done(((f32[8,64,128]{2,1,0:T(8,128)}), f32[512,64,128]{2,1,0:T(8,128)}) %all-gather.8.cloned.1.call-update) | async-done | bytes 16777232 | tf_op jit(solution)/shard_map/all_gather | solution.py:19
  219.8 97.7 %while.27 = (s32[]{:T(128)}, f32[8,64,128]{2,1,0:T(8,128)S(1)}, s32[]{:T(128)}, f32[64,8]{1,0:T(8,128)}, f32[64,8,64,128]{3,2,1,0:T(8,128)}, /*index=5*/s32[]{:T(128)}, s32[]{:T(128)}, s32[]{:T(128)}, s32[]{:T(128)}) while((s32[]{:T(128)}, f32[8,64,128]{2,1,0:T(8,128)S(1)}, s32[]{:T(128)}, f32[64,8]{1,0:T(8,128)}, ...), condition=%wide.region_5.6_spmd, body=%wide.region_4.5_spmd.sunk | while | flops 131078 | bytes 786683 | solution.py:28
  220.5 1.1 bitcast_add_fusion.11
  222.3 1.1 bitcast_add_fusion.11
  224.1 1.1 bitcast_add_fusion.11
  225.9 1.1 bitcast_add_fusion.11
  227.6 1.1 bitcast_add_fusion.11
  229.4 1.1 bitcast_add_fusion.11
  231.2 1.1 bitcast_add_fusion.11
  233.0 1.1 bitcast_add_fusion.11
  234.7 1.1 bitcast_add_fusion.11
  236.5 1.1 bitcast_add_fusion.11
  238.3 1.1 bitcast_add_fusion.11
  240.1 1.1 bitcast_add_fusion.11
  241.8 1.1 bitcast_add_fusion.11
  248.9 1.1 bitcast_add_fusion.11
  259.6 1.1 bitcast_add_fusion.11
  261.4 1.1 bitcast_add_fusion.11
  272.0 1.1 bitcast_add_fusion.11
  282.7 1.1 bitcast_add_fusion.11
  293.3 1.1 bitcast_add_fusion.11
  295.1 1.1 bitcast_add_fusion.11
  305.8 1.1 bitcast_add_fusion.11
  311.1 1.1 bitcast_add_fusion.11
  312.9 1.1 bitcast_add_fusion.11
  316.4 1.1 bitcast_add_fusion.11
  317.6 2.2 convolution_bitcast_fusion.5
  319.8 1.9 fusion.15
  321.6 1.5 fusion.9
  324.1 166.4 %all-reduce.8.cloned.1.call-done = f32[512,2560]{1,0:T(8,128)} async-done(((f32[512,2560]{1,0:T(8,128)}), f32[512,2560]{1,0:T(8,128)}) %all-reduce.8.cloned.1.call-update) | async-done | bytes 5242896
  490.4 1.5 constant_dynamic-slice_fusion
  492.8 1.2 copy.127
  494.1 1.1 copy.128
  495.2 2.1 reshape.167
  498.3 41.5 %all-reduce.6.cloned.1.call-done = f32[8,2560]{1,0:T(8,128)} async-done(((f32[8,2560]{1,0:T(8,128)}), f32[8,2560]{1,0:T(8,128)}) %all-reduce.6.cloned.1.call-update) | async-done | bytes 81936 | tf_op jit(solution)/shard_map/psum | solution.py:134
  539.8 1.5 copy.187
  (168 shorter events, 92.1 us)
Async XLA Ops:
  7.2 12.3 %copy-start = (bf16[512,2560]{1,0:T(8,128)(2,1)S(1)}, bf16[512,2560]{1,0:T(8,128)(2,1)}, u32[]{:S(2)}) copy-start(bf16[512,2560]{1,0:T(8,128)(2,1)} %param.16) | copy-start | bytes 7864324
  7.2 6.9 %copy-start.7 = (bf16[1,256,128]{2,1,0:T(8,128)(2,1)S(1)}, bf16[1,256,128]{2,1,0:T(8,128)(2,1)}, u32[]{:S(2)}) copy-start(bf16[1,256,128]{2,1,0:T(8,128)(2,1)} %param.12) | copy-start | bytes 196612
  7.2 156.3 %all-gather.6.cloned.1.call-start = ((), (), s32[]{:S(2)}) async-start(), calls=%async_computation.1 | async-start | bytes 17039360 | tf_op jit(solution)/shard_map/all_gather | solution.py:19
  8.8 9.3 %copy-start.13 = (f32[2,128,8]{1,2,0:T(8,128)}, f32[2,128,8]{1,2,0:T(8,128)S(1)}, u32[]{:S(2)}) copy-start(f32[2,128,8]{1,2,0:T(8,128)S(1)} %get-tuple-element.170) | copy-start | bytes 24580
  9.4 8.7 %copy-start.11 = (f32[8,2,128]{2,0,1:T(8,128)}, f32[8,2,128]{2,0,1:T(8,128)S(1)}, u32[]{:S(2)}) copy-start(f32[8,2,128]{2,0,1:T(8,128)S(1)} %reduce_window_sum.24) | copy-start | bytes 24580
  9.6 8.5 %copy-start.15 = (f32[8,2]{0,1:T(2,128)}, f32[8,2]{0,1:T(2,128)S(1)}, u32[]{:S(2)}) copy-start(f32[8,2]{0,1:T(2,128)S(1)} %reduce_window_sum.26) | copy-start | bytes 196
  9.6 8.5 %copy-start.18 = (f32[8,1]{0,1:T(1,128)}, f32[8,1]{0,1:T(1,128)S(1)}, u32[]{:S(2)}) copy-start(f32[8,1]{0,1:T(1,128)S(1)} %get-tuple-element.179) | copy-start | bytes 100
  14.5 0.8 copy-start.3
  18.1 201.7 %all-gather.8.cloned.1.call-start = ((), (), s32[]{:S(2)}) async-start(), calls=%async_computation.2 | async-start | bytes 17039360 | tf_op jit(solution)/shard_map/all_gather | solution.py:19
  19.5 4.1 copy-start.8
  23.6 139.9 %copy-start.1 = (bf16[2,128,8,64]{1,0,3,2:T(2,128)(2,1)}, bf16[2,128,8,64]{1,0,3,2:T(2,128)(2,1)S(1)}, u32[]{:S(2)}) copy-start(bf16[2,128,8,64]{1,0,3,2:T(2,128)(2,1)S(1)} %reshape.143) | copy-start | bytes 786436
  24.0 0.8 copy-start.4
  28.2 462.2 %all-reduce.8.cloned.1.call-start = ((), (), s32[]{:S(2)}) async-start(), calls=%async_computation.3 | async-start | bytes 10485760
  177.9 5.7 %copy-start.5 = (bf16[1,256,2560]{2,1,0:T(8,128)(2,1)S(1)}, bf16[1,256,2560]{2,1,0:T(8,128)(2,1)}, u32[]{:S(2)}) copy-start(bf16[1,256,2560]{2,1,0:T(8,128)(2,1)} %param.17) | copy-start | bytes 3932164
  182.6 0.7 copy-start.6
  186.8 352.9 %all-reduce.6.cloned.1.call-start = ((), (), s32[]{:S(2)}) async-start(), calls=%async_computation | async-start | bytes 163840 | tf_op jit(solution)/shard_map/psum | solution.py:134
  192.2 125.3 %copy-start.14 = (f32[2,128,8]{1,2,0:T(8,128)S(1)}, f32[2,128,8]{1,2,0:T(8,128)}, u32[]{:S(2)}) copy-start(f32[2,128,8]{1,2,0:T(8,128)} %copy-done.13) | copy-start | bytes 24580
  317.5 5.6 %copy-start.2 = (bf16[2,128,8,64]{1,0,3,2:T(2,128)(2,1)S(1)}, bf16[2,128,8,64]{1,0,3,2:T(2,128)(2,1)}, u32[]{:S(2)}) copy-start(bf16[2,128,8,64]{1,0,3,2:T(2,128)(2,1)} %copy-done.1) | copy-start | bytes 786436
  317.5 5.6 %copy-start.12 = (f32[2,128,128]{2,1,0:T(8,128)S(1)}, f32[2,128,128]{2,1,0:T(8,128)}, u32[]{:S(2)}) copy-start(f32[2,128,128]{2,1,0:T(8,128)} %fusion.75) | copy-start | bytes 393220
  317.5 5.6 %copy-start.16 = (pred[128,128]{1,0:T(8,128)(4,1)S(1)}, pred[128,128]{1,0:T(8,128)(4,1)}, u32[]{:S(2)}) copy-start(pred[128,128]{1,0:T(8,128)(4,1)} %iota_compare_fusion) | copy-start | bytes 49156
  317.5 5.6 %copy-start.17 = (f32[8,2,128]{2,1,0:T(2,128)S(1)}, f32[8,2,128]{2,1,0:T(2,128)}, u32[]{:S(2)}) copy-start(f32[8,2,128]{2,1,0:T(2,128)} %copy.91) | copy-start | bytes 24580
  319.7 172.3 %copy-start.9 = (f32[2,128,128]{2,1,0:T(8,128)S(1)}, f32[2,128,128]{2,1,0:T(8,128)}, u32[]{:S(2)}) copy-start(f32[2,128,128]{2,1,0:T(8,128)} %fusion.4) | copy-start | bytes 393220
  319.7 172.3 %copy-start.10 = (f32[2,128,128]{2,1,0:T(8,128)S(1)}, f32[2,128,128]{2,1,0:T(8,128)}, u32[]{:S(2)}) copy-start(f32[2,128,128]{2,1,0:T(8,128)} %convolution_bitcast_fusion.4) | copy-start | bytes 393220
Sparse Core Ops, SparseCore 0:
  18.2 101.2 all-gather.5
  122.8 96.9 all-gather.7
  223.4 266.9 all-reduce.7
  493.2 46.5 all-reduce.5
where the time goes:
time: 553 us; the launch traced here: 548 us
  waiting for transfers between devices  235 us (42%)
  blocking collectives  115 us (21%)
  local copies, waits for them, and re-layouts  71.4 us (13%)
  other arithmetic  70 us (13%)
  matrix products  38.3 us (7%)
  between operations  15.4 us (3%)
    unnamed x5, waiting for transfers between devices  166 us
    unnamed x1, blocking collectives  115 us
    add x63, other arithmetic, combine(): second_part[0][:, None, None] * first_part[1] + second_part[1]  66.4 us
    mul x63, local copies, waits for them, and re-layouts, combine(): second_part[0][:, None, None] * first_part[1] + second_part[1]  43.9 us
    psum x1, waiting for transfers between devices, shards(): grad_w_out = lax.psum(share, 'dp')  41.5 us
    all_gather x2, waiting for transfers between devices, entering(): gathered = jax.tree.map(lambda a: lax.all_gather(a, axis), part)  27.6 us
    unnamed x48, local copies, waits for them, and re-layouts  15.5 us
  transfers between devices with their start and end apart: 4, of which 3 were waited for; matrix products, arithmetic and copies ran while one was open for 30% of the time, Pallas kernels for 0%

commit v1 on v0

v1 whole, which is shorter than its diff:
```python
import jax
import jax.numpy as jnp
from jax import lax
from jax.experimental import pallas as pl
from jax.experimental.pallas import tpu as pltpu
from jax.sharding import PartitionSpec as P

HEAD_DIM = 64
STATE = 128
HEADS = 8
TOK = 256
CH = HEADS * HEAD_DIM
D = 2560
NX, NY, NZ = 4, 4, 8
CHIPS = NY * NZ
PIECE = CH // CHIPS
BLK = D // NX
BOTH = ("seq", "dp")

f32, bf16 = jnp.float32, jnp.bfloat16
HI = lax.Precision.HIGHEST
NT = (((1,), (1,)), ((), ()))
TN = (((0,), (0,)), ((), ()))
NN = (((1,), (0,)), ((), ()))


def mm(a, b, dims):
    return lax.dot_general(a, b, dims, preferred_element_type=f32)


def permute(v, target):
    pairs = []
    for z in range(NZ):
        for y in range(NY):
            for c in range(2):
                for x in range(NX):
                    tz, ty, tc, tx = target(z, y, c, x)
                    src = ((z * NY + y) * 2 + c) * NX + x
                    dst = ((tz * NY + ty) * 2 + tc) * NX + tx
                    pairs.append((src, dst))
    return lax.ppermute(v, BOTH, pairs)


def swap_core(z, y, c, x):
    return z, y, 1 - c, x


def first_axis(k):
    return lambda z, y, c, x: (z, y, c, (x + k) % NX) if c == 0 else (z, (y + k) % NY, c, x)


def second_axis(k):
    return lambda z, y, c, x: (z, (y + k) % NY, c, x) if c == 0 else (z, y, c, (x + k) % NX)


def x_axis(k):
    return lambda z, y, c, x: (z, y, c, (x + k) % NX)


def rate_lanes(rate_ref, width):
    lane = lax.broadcasted_iota(jnp.int32, (1, width), 1) // (width // HEADS)
    rates = jnp.zeros((1, width), f32)
    for h in range(HEADS):
        rates = jnp.where(lane == h, rate_ref[h] * (1.0 / (8.0 * TOK * 64)), rates)
    return rates


def signed_tri():
    t = lax.broadcasted_iota(jnp.int32, (TOK, TOK), 0)
    s = lax.broadcasted_iota(jnp.int32, (TOK, TOK), 1)
    half = TOK // 2
    plus = (s >= half) & (s <= t)
    minus = (s < half) & (s > t)
    return jnp.where(plus, 1.0, jnp.where(minus, -1.0, 0.0)).astype(f32)


def gate(v):
    s = 1.0 - v * (1.0 / 8.0)
    for n in (7.0, 6.0, 5.0, 4.0, 3.0, 2.0):
        s = 1.0 - v * (1.0 / n) * s
    return jnp.sqrt(jnp.where(v < 0.25, v * s, 1.0 - jnp.exp(-v)))


def local_states(pos_ref, rate_ref, x_ref, b_ref, c_ref, dt_ref, w_ref, g_ref,
                 keep_ref, send_ref, tot_ref, gy_ref, gyd_ref, xw_ref, xt_ref, cum_ref):
    dt = dt_ref[...].astype(f32)
    dt_lanes = jnp.broadcast_to(dt[:, None, :], (HEADS, HEAD_DIM, TOK)).reshape(CH, TOK)
    cum = lax.dot_general(signed_tri(), dt_lanes, NT, precision=HI, preferred_element_type=f32)
    cum_ref[...] = cum
    steps = cum - pltpu.roll(cum, 1, 0)
    row = lax.broadcasted_iota(jnp.int32, (TOK, CH), 0)
    ones = jnp.ones((8, TOK // 2), f32)
    start = -lax.dot_general(ones, dt_lanes[:, : TOK // 2], NT, precision=HI, preferred_element_type=f32)[:1]
    steps = jnp.where(row == 0, cum - start, steps)
    rate = rate_lanes(rate_ref, CH)
    last = cum[TOK - 1:]
    xw = x_ref[...].astype(f32) * gate(steps * (2.0 * rate))
    xw_ref[...] = xw.astype(bf16)
    xt = (xw * jnp.exp((cum - last) * rate)).astype(bf16)
    xt_ref[...] = xt
    own = mm(xt, b_ref[...], TN)
    gy = mm(g_ref[...], w_ref[...], NT).astype(bf16)
    gy_ref[...] = gy
    gyd = (gy.astype(f32) * jnp.exp((start - cum) * rate)).astype(bf16)
    gyd_ref[...] = gyd
    adj = mm(gyd, c_ref[...], TN)
    total = jnp.sum(dt, axis=1, keepdims=True)
    head = lax.broadcasted_iota(jnp.int32, (HEADS, 1), 0)
    rate_col = jnp.zeros((HEADS, 1), f32)
    for h in range(HEADS):
        rate_col = jnp.where(head == h, rate_ref[h] * (1.0 / (8.0 * TOK * 64)), rate_col)
    tot = jnp.broadcast_to(-(total * rate_col), (HEADS, STATE))
    tot_ref[...] = tot
    send_ref[CH:, :] = tot
    core = pos_ref[2]

    @pl.when(core == 0)
    def _():
        keep_ref[...] = own
        send_ref[:CH, :] = adj

    @pl.when(core == 1)
    def _():
        keep_ref[...] = adj
        send_ref[:CH, :] = own


def per_head(rows):
    return jnp.broadcast_to(rows[:, None, :], (HEADS, HEAD_DIM, STATE)).reshape(CH, STATE)


def chip_states(keep_ref, recv_ref, tot_ref, out_ref):
    tot2 = recv_ref[CH:, :]
    chip = keep_ref[...] * per_head(jnp.exp(tot2)) + recv_ref[:CH, :]
    out_ref[:, :PIECE, :] = chip.reshape(CHIPS, PIECE, STATE)
    tots = (tot2 + tot_ref[...])[:, None, None, :]
    tots = jnp.broadcast_to(tots, (HEADS, CHIPS // HEADS, 8, STATE))
    out_ref[:, PIECE:, :] = tots.reshape(CHIPS, 8, STATE)


def scan_chips(pos_ref, in_ref, out_ref):
    core = pos_ref[2]

    def run(order):
        acc = jnp.zeros((PIECE, STATE), f32)
        for k in order:
            out_ref[k] = acc
            acc = acc * jnp.exp(in_ref[k, PIECE:PIECE + 1, :]) + in_ref[k, :PIECE, :]

    @pl.when(core == 0)
    def _():
        run(range(CHIPS))

    @pl.when(core == 1)
    def _():
        run(range(CHIPS - 1, -1, -1))


def core_states(carry_ref, keep_ref, tot_ref, out_ref):
    out_ref[...] = carry_ref[...] * per_head(jnp.exp(tot_ref[...])) + keep_ref[...]


def intra(rate_ref, dt_ref, cum_ref, b_ref, c_ref, gy_ref, xw_ref,
          y_ref, gin_ref, wt_ref, hd_ref, gr_ref, gw_ref):
    dt = dt_ref[...].astype(f32)
    tri = signed_tri()
    cum_rows = lax.dot_general(dt, tri, NT, precision=HI, preferred_element_type=f32)
    ones = jnp.ones((8, TOK), f32)
    rate = rate_lanes(rate_ref, CH)
    cum = cum_ref[...]
    i = lax.broadcasted_iota(jnp.int32, (TOK, TOK), 0)
    j = lax.broadcasted_iota(jnp.int32, (TOK, TOK), 1)
    lower = i >= j
    b = b_ref[...]
    c = c_ref[...]
    scores = mm(c, b, NT)
    pairs = jnp.zeros((TOK, TOK), f32)
    for h in range(HEADS):
        lanes = slice(h * HEAD_DIM, (h + 1) * HEAD_DIM)
        r = rate_ref[h] * (1.0 / (8.0 * TOK * 64))
        gap = cum_rows[h:h + 1, :] - cum[:, h * HEAD_DIM:h * HEAD_DIM + 1]
        mask = jnp.exp(jnp.where(lower, gap * r, -jnp.inf))
        mixed = (mask * scores).astype(bf16)
        xw = xw_ref[:, lanes]
        gy = gy_ref[:, lanes]
        y_ref[:, lanes] = mm(mixed, xw, NN)
        gin_ref[:, lanes] = mm(mixed, gy, TN)
        pairs = pairs + mask * mm(gy, xw, NT)
    pairs = pairs.astype(bf16)
    gr_ref[...] = mm(pairs, b, NN)
    gw_ref[...] = mm(pairs, c, TN)
    row = lax.broadcasted_iota(jnp.int32, (TOK, CH), 0)
    dt_lanes = jnp.broadcast_to(dt[:, None, :], (HEADS, HEAD_DIM, TOK)).reshape(CH, TOK)
    start = -lax.dot_general(ones[:, : TOK // 2], dt_lanes[:, : TOK // 2], NT, precision=HI,
                             preferred_element_type=f32)[:1]
    steps = jnp.where(row == 0, cum - start, cum - pltpu.roll(cum, 1, 0))
    w = gate(steps * (2.0 * rate))
    gin_ref[...] = gin_ref[...] * w
    wt_ref[...] = w * jnp.exp((cum - cum[TOK - 1:]) * rate)
    hd_ref[...] = jnp.exp((start - cum) * rate)


def select_rows(core, y_at):
    row = lax.broadcasted_iota(jnp.int32, (CH // 2, CH), 0)
    lane = lax.broadcasted_iota(jnp.int32, (CH // 2, CH), 1)
    y = (y_at + row // 64) % NY
    z = (row // 8) % NZ
    return jnp.where(lane == ((z * NY + y) * 2 + core) * 8 + row % 8, 1.0, 0.0).astype(bf16)


def forward_out(pos_ref, carry_ref, recv_ref, c_ref, y_ref, hd_ref, out_ref, mine_ref, other_ref):
    y_at, core = pos_ref[1], pos_ref[2]
    state = jnp.where(core == 0, carry_ref[...], recv_ref[...]).astype(bf16)
    out = (y_ref[...] + hd_ref[...] * mm(c_ref[...], state, NT)).astype(bf16)
    out_ref[...] = out
    mine_ref[...] = mm(select_rows(core, y_at), out, NT).astype(bf16)
    other_ref[...] = mm(select_rows(1 - core, y_at), out, NT)


def partial_grad(pos_ref, mine_ref, peer_ref, g_ref, gp_ref, s0_ref, s1_ref, s2_ref, s3_ref):
    core, x_at = pos_ref[2], pos_ref[3]
    outs = (s0_ref, s1_ref, s2_ref, s3_ref)
    mine = mine_ref[...]
    peer = peer_ref[...].astype(bf16)
    for xr in range(NX):
        at = pl.multiple_of(((x_at + xr) % NX) * BLK, 128)
        tile = mm(mine, g_ref[:, pl.ds(at, BLK)], NN)
        tile = tile + mm(peer, gp_ref[:, pl.ds(at, BLK)].astype(bf16), NN)

        @pl.when(core == 0)
        def _():
            for yr in range(NY):
                outs[xr][yr] = tile[yr * 64:(yr + 1) * 64]

        @pl.when(core == 1)
        def _():
            for yr in range(NY):
                outs[yr][xr] = tile[yr * 64:(yr + 1) * 64]


def other_grads(pos_ref, carry_ref, recv_ref, b_ref, gin_ref, wt_ref, gyd_ref, xt_ref, gr_ref, gw_ref,
                gi_ref, gwr_ref, grd_ref):
    core = pos_ref[2]
    carry, recv = carry_ref[...], recv_ref[...]
    state = jnp.where(core == 0, carry, recv).astype(bf16)
    adj = jnp.where(core == 0, recv, carry).astype(bf16)
    gi_ref[...] = (gin_ref[...] + wt_ref[...] * mm(b_ref[...], adj, NT)).astype(bf16)
    grd_ref[...] = (gr_ref[...] + mm(gyd_ref[...], state, NN)).astype(bf16)
    gwr_ref[...] = (gw_ref[...] + mm(xt_ref[...], adj, NN)).astype(bf16)


def place(pos_ref, r0_ref, r1_ref, r2_ref, r3_ref, out_ref):
    x_at = pos_ref[3]
    for k, ref in enumerate((r0_ref, r1_ref, r2_ref, r3_ref)):
        at = pl.multiple_of(((x_at + NX - k) % NX) * BLK, 128)
        out_ref[:, pl.ds(at, BLK)] = ref[...]


def call(body, outs, scalars, *args, flops=0):
    specs = [pl.BlockSpec(memory_space=pltpu.SMEM)] * scalars
    specs += [pl.BlockSpec(memory_space=pltpu.VMEM)] * (len(args) - scalars)
    shapes = [jax.ShapeDtypeStruct(s, d) for s, d in outs]
    moved = sum(a.size * a.dtype.itemsize for a in args) + sum(s.size * s.dtype.itemsize for s in shapes)
    got = pl.pallas_call(
        body,
        out_shape=shapes,
        in_specs=specs,
        out_specs=[pl.BlockSpec(memory_space=pltpu.VMEM)] * len(shapes),
        cost_estimate=pl.CostEstimate(flops=flops, bytes_accessed=moved, transcendentals=0),
        compiler_params=pltpu.CompilerParams(vmem_limit_bytes=48 << 20),
        name=body.__name__,
    )(*args)
    return got if len(got) > 1 else got[0]


def shards(inputs, write_vecs, read_vecs, dt_code, a_rate, w_out, grad_out):
    place_seq = lax.axis_index("seq")
    pos = jnp.stack([place_seq // 8, (place_seq // 2) % NY, place_seq % 2, lax.axis_index("dp")]).astype(jnp.int32)
    x, b, c, dt, g = inputs[0], write_vecs[0], read_vecs[0], dt_code[0], grad_out[0]
    chips = [[q * 2 + core for q in range(CHIPS)] for core in range(2)]
    depth = [[(z * NY + y) * 2 + core for z in range(NZ)] for y in range(NY) for core in range(2)]

    keep, send, tot, gy, gyd, xw, xt, cum = call(
        local_states,
        [((CH, STATE), f32), ((CH + 8, STATE), f32), ((HEADS, STATE), f32), ((TOK, CH), bf16), ((TOK, CH), bf16),
         ((TOK, CH), bf16), ((TOK, CH), bf16), ((TOK, CH), f32)],
        2, pos, a_rate, x, b, c, dt, w_out, g, flops=2 * TOK * D * CH)
    recv = permute(send, swap_core)
    chip = call(chip_states, [((CHIPS, PIECE + 8, STATE), f32)], 0, keep, recv, tot)
    pieces = lax.all_to_all(chip, "seq", 0, 0, axis_index_groups=chips, tiled=True)
    scanned = call(scan_chips, [((CHIPS, PIECE, STATE), f32)], 1, pos, pieces)
    carry = lax.all_to_all(scanned, "seq", 0, 0, axis_index_groups=chips, tiled=True).reshape(CH, STATE)
    recv2 = permute(call(core_states, [((CH, STATE), f32)], 0, carry, keep, tot), swap_core)

    g_peer = permute(g.astype(f32), swap_core)
    y_in, gin, wt, hd, gr, gw = call(
        intra,
        [((TOK, CH), f32), ((TOK, CH), f32), ((TOK, CH), f32), ((TOK, CH), f32), ((TOK, STATE), f32),
         ((TOK, STATE), f32)],
        1, a_rate, dt, cum, b, c, gy, xw, flops=2 * TOK * TOK * CH * 3)

    out, mine, other = call(
        forward_out, [((TOK, CH), bf16), ((CH // 2, TOK), bf16), ((CH // 2, TOK), f32)],
        1, pos, carry, recv2, c, y_in, hd, flops=2 * TOK * CH * 768)
    peer = permute(other, swap_core)
    tile = ((NY, 64, BLK), f32)
    s = call(partial_grad, [tile] * 4, 1, pos, mine, peer, g, g_peer, flops=2 * TOK * D * CH)
    s = s[0] + permute(s[2], first_axis(2)) + permute(s[1], first_axis(1)) + permute(s[3], first_axis(3))
    s = s[0] + permute(s[2], second_axis(2)) + permute(s[1], second_axis(1)) + permute(s[3], second_axis(3))
    s = lax.all_to_all(s.reshape(NZ, 8, BLK), "seq", 0, 0, axis_index_groups=depth, tiled=True)
    s = jnp.sum(s, axis=0)
    grad_w_out = call(place, [((8, D), f32)], 1, pos, s, permute(s, x_axis(1)), permute(s, x_axis(2)),
                      permute(s, x_axis(3)))
    gi, gwr, grd = call(
        other_grads, [((TOK, CH), bf16), ((TOK, STATE), bf16), ((TOK, STATE), bf16)],
        1, pos, carry, recv2, b, gin, wt, gyd, xt, gr, gw, flops=2 * TOK * CH * STATE * 3)
    return out[None], gi[None], gwr[None], grd[None], grad_w_out


def solution(mesh):
    rows = P("dp", "seq", None)
    return jax.shard_map(
        shards,
        mesh=mesh,
        in_specs=(rows, rows, rows, P("dp", None, "seq"), P(), P(), rows),
        out_specs=(rows, rows, rows, rows, P("seq", None)),
        check_vma=False,
    )
```

time: 553 us -> 114 us (0.21)
  waiting for transfers between devices: 235 us -> 25.1 us
  local copies, waits for them, and re-layouts: 71.4 us -> 0.08 us
  other arithmetic: 70 us -> 3.51 us
  blocking collectives: 115 us -> 54 us
  matrix products: 38.3 us -> 0 us
  Pallas kernels: 0 us -> 16.1 us
  between operations: 15.4 us -> 0.81 us
  starting transfers between devices: 0.16 us -> 14.5 us
    unnamed x5 -> x0, waiting for transfers between devices: 166 us -> none
    unnamed x1 -> x0, blocking collectives: 115 us -> none
    add x63 -> x1, other arithmetic: 66.4 us -> 0.13 us  [shards(): s[0] + permute(s[2], first_axis(2)) + permute(s[1], first_axis(1))]
    all_to_all x0 -> x3, blocking collectives: none -> 54 us  [the longest x1 26.3 us: shards(): lax.all_to_all(chip, 'seq', 0, 0, axis_index_groups=chips, tiled=True)]
    mul x63 -> x0, local copies, waits for them, and re-layouts: 43.9 us -> none  [combine(): second_part[0][:, None, None] * first_part[1] + second_part[1]]
    psum x1 -> x0, waiting for transfers between devices: 41.5 us -> none  [shards(): grad_w_out = lax.psum(share, 'dp')]
    dot_general x18 -> x0, matrix products: 38.3 us -> none  [the longest x1 3.94 us: shards(): jnp.einsum('hkm,mhpn->khpn', fwd_weights, group_states, precision=highest)]
    all_gather x2 -> x0, waiting for transfers between devices: 27.6 us -> none  [entering(): gathered = jax.tree.map(lambda a: lax.all_gather(a, axis), part)]
  transfers between devices with their start and end apart: 4 -> 13, of which waited for: 3 -> 10; matrix products, arithmetic and copies ran while one was open for 30% -> 0% of each run, Pallas kernels for 0% -> 10%
where the time goes in v1:
time: 114 us
  blocking collectives  54 us (47%)
  waiting for transfers between devices  25.1 us (22%)
  Pallas kernels  16.1 us (14%)
  starting transfers between devices  14.5 us (13%)
  other arithmetic  3.51 us (3%)
    all_to_all x1, blocking collectives, shards(): lax.all_to_all(chip, 'seq', 0, 0, axis_index_groups=chips, tiled=True)  26.3 us
    ppermute x13, waiting for transfers between devices, permute(): return lax.ppermute(v, BOTH, pairs)  25.1 us
    all_to_all x1, blocking collectives, shards(): lax.all_to_all(scanned, 'seq', 0, 0, axis_index_groups=chips, tiled=True)  16.1 us
    pallas_call x9, Pallas kernels, call(): pl.pallas_call(body, out_shape=shapes, in_specs=specs, out_specs=[pl.Bloc...  16.1 us
    ppermute x13, starting transfers between devices, permute(): return lax.ppermute(v, BOTH, pairs)  14.5 us
    all_to_all x1, blocking collectives, shards(): lax.all_to_all(s.reshape(NZ, 8, BLK), 'seq', 0, 0, axis_index_groups=dept...  11.6 us
    convert_element_type x1, other arithmetic, shards(): g_peer = permute(g.astype(f32), swap_core)  3.24 us
  transfers between devices with their start and end apart: 13, of which 10 were waited for; matrix products, arithmetic and copies ran while one was open for 0% of the time, Pallas kernels for 10%

profile of v1, /device:TPU:32, one launch (start us, length us, event | category | flops | bytes accessed | tf_op | source)
XLA Modules:
  0.0 114.1 jit_solution(13843665970737083983)
XLA Ops:
  0.6 0.0 copy-start
  0.6 0.0 copy-start.9
  0.7 0.0 copy-start.8
  0.7 0.0 copy-start.1
  0.7 0.0 copy-start.2
  0.7 0.0 copy-start.3
  0.7 3.2 %bitcast_convert_fusion = f32[256,2560]{1,0:T(8,128)} fusion(bf16[1,256,2560]{2,1,0:T(8,128)(2,1)} %param.13), kind=kLoop, calls=%fused_computation.10 | loop fusion | flops 655360 | bytes 3932160 | tf_op jit(solution)/shard_map/convert_element_type | solution.py:295
  3.9 0.0 collective-permute-start.3
  3.9 0.1 pad_add_fusion.pos_ref
  4.0 0.0 copy-done
  4.0 0.0 copy-done.9
  4.0 0.0 copy-done.8
  4.0 0.0 copy-done.1
  4.0 0.0 copy-done.2
  4.0 0.0 copy-done.3
  4.1 4.4 %local_states.1 = (f32[512,128]{1,0:T(8,128)S(1)}, f32[520,128]{1,0:T(8,128)S(1)}, f32[8,128]{1,0:T(8,128)S(1)}, bf16[256,512]{1,0:T(8,128)(2,1)S(1)}, bf16[256,...) custom-call(s32[4]{0:T(128)S(1)} %pad_add_fusion.pos_ref, ...), custom_call_target="tpu_custom_call" | custom-call | flops 671088640 | bytes 6438960 | tf_op jit(solution)/shard_map/local_states/pallas_call | solution.py:264
  8.5 0.6 collective-permute-start
  9.1 1.2 %collective-permute-done.recv_ref = f32[520,128]{1,0:T(8,128)S(1)} collective-permute-done((f32[520,128]{1,0:T(8,128)S(1)}, f32[520,128]{1,0:T(8,128)S(1)}, u32[]{:S(2)}, u32[]{:S(2)}) %collective-permute-start) | collective-permute-done | bytes 266272 | tf_op jit(solution)/shard_map/ppermute | solution.py:41
  10.3 26.3 %all_to_all.15.in_ref = f32[32,24,128]{2,1,0:T(8,128)S(1)} all-to-all(f32[32,24,128]{2,1,0:T(8,128)S(1)} %chip_states.1), channel_id=1, replica_groups={{0,8,16,24,32,40,48,56,64,72,80,88,96,104,112,120,128,136,144,152,160,1..., dimensions={0} | all-to-all | bytes 786432 | tf_op jit(solution)/shard_map/all_to_all | solution.py:290
  36.6 0.6 scan_chips.1
  37.2 16.1 %all_to_all.16 = f32[32,16,128]{2,1,0:T(8,128)S(1)} all-to-all(f32[32,16,128]{2,1,0:T(8,128)S(1)} %scan_chips.1), channel_id=1, replica_groups={{0,8,16,24,32,40,48,56,64,72,80,88,96,104,112,120,128,136,144,152,160,1..., dimensions={0} | all-to-all | bytes 524288 | tf_op jit(solution)/shard_map/all_to_all | solution.py:292
  53.4 0.1 collective-permute-start.1
  53.5 3.2 %intra.1 = (f32[256,512]{1,0:T(8,128)S(1)}, f32[256,512]{1,0:T(8,128)S(1)}, f32[256,512]{1,0:T(8,128)S(1)}, f32[256,512]{1,0:T(8,128)S(1)}, f32[256,128]{1,0:T(8,128)S(1)}, /*index=5*/f32[256,128]{1,0:T(8,128)S(1)}) custom-call(f32[8]{0:T(128)S(1)} %copy-done.9, s32[8,256]{1,0:T(8,128)S(1)} %bitcast.46, f32[256,512]{1,0:T(8,128)S(1)} %get-tuple-element.32.cum_ref, ...), custom_call_target="tpu_custom_call" | custom-call | flops 201326592 | bytes 3547168 | tf_op jit(solution)/shard_map/intra/pallas_call | solution.py:264
  56.7 0.0 copy-start.4
  56.7 0.0 copy-start.6
  56.7 0.0 collective-permute-done.1.recv_ref
  56.7 1.6 %forward_out.1 = (bf16[256,512]{1,0:T(8,128)(2,1)}, bf16[256,256]{1,0:T(8,128)(2,1)S(1)}, f32[256,256]{1,0:T(8,128)S(1)}) custom-call(s32[4]{0:T(128)S(1)} %pad_add_fusion.pos_ref, f32[512,128]{1,0:T(8,128)S(1)} %bitcast.36, f32[512,128]{1,0:T(8,128)S(1)} %collective-permute-done.1.recv_ref, bf16[256,128]{1,0:T(8,128)(2,1)S(1)} %bitcast.40, ...), custom_call_target="tpu_custom_call" | custom-call | flops 201326592 | bytes 2293776 | tf_op jit(solution)/shard_map/forward_out/pallas_call | solution.py:264
  58.3 0.0 copy-done.4
  58.4 0.5 collective-permute-start.2
  58.8 1.2 %collective-permute-done.2.peer_ref = f32[256,256]{1,0:T(8,128)S(1)} collective-permute-done((f32[256,256]{1,0:T(8,128)S(1)}, f32[256,256]{1,0:T(8,128)S(1)}, u32[]{:S(2)}, u32[]{:S(2)}) %collective-permute-start.2) | collective-permute-done | bytes 262176 | tf_op jit(solution)/shard_map/ppermute | solution.py:41
  60.0 0.0 collective-permute-done.3.gp_ref
  60.0 0.0 copy-done.6
  60.0 3.4 %partial_grad.1 = (f32[4,64,640]{2,1,0:T(8,128)S(1)}, f32[4,64,640]{2,1,0:T(8,128)S(1)}, f32[4,64,640]{2,1,0:T(8,128)S(1)}, f32[4,64,640]{2,1,0:T(8,128)S(1)}) custom-call(s32[4]{0:T(128)S(1)} %pad_add_fusion.pos_ref, bf16[256,256]{1,0:T(8,128)(2,1)S(1)} %get-tuple-element.47.mine_ref, f32[256,256]{1,0:T(8,128)S(1)} %collective-permute-done.2.peer_ref, ...), custom_call_target="tpu_custom_call" | custom-call | flops 671088640 | bytes 6946832 | tf_op jit(solution)/shard_map/partial_grad/pallas_call | solution.py:264
  63.4 3.1 %collective-permute-start.4 = (f32[4,64,640]{2,1,0:T(8,128)S(1)}, f32[4,64,640]{2,1,0:T(8,128)S(1)}, u32[]{:S(2)}, u32[]{:S(2)}) collective-permute-start(f32[4,64,640]{2,1,0:T(8,128)S(1)} %get-tuple-element.50), channel_id=1, source_target_pairs={{0,2},{1,3},{2,0},{3,1},{4,20},{5,21},{6,22},{7,23},{8,10},{9,11},... | collective-permute-start | bytes 1966088 | tf_op jit(solution)/shard_map/ppermute | solution.py:41
  66.5 0.6 collective-permute-start.5
  67.1 2.6 %collective-permute-start.6 = (f32[4,64,640]{2,1,0:T(8,128)S(1)}, f32[4,64,640]{2,1,0:T(8,128)S(1)}, u32[]{:S(2)}, u32[]{:S(2)}) collective-permute-start(f32[4,64,640]{2,1,0:T(8,128)S(1)} %get-tuple-element.52), channel_id=1, source_target_pairs={{0,3},{1,0},{2,1},{3,2},{4,28},{5,29},{6,30},{7,31},{8,11},{9,8},{... | collective-permute-start | bytes 1966088 | tf_op jit(solution)/shard_map/ppermute | solution.py:41
  69.8 5.9 %collective-permute-done.4 = f32[4,64,640]{2,1,0:T(8,128)S(1)} collective-permute-done((f32[4,64,640]{2,1,0:T(8,128)S(1)}, f32[4,64,640]{2,1,0:T(8,128)S(1)}, u32[]{:S(2)}, u32[]{:S(2)}) %collective-permute-start.4) | collective-permute-done | bytes 655392 | tf_op jit(solution)/shard_map/ppermute | solution.py:41
  75.7 6.9 %collective-permute-done.5 = f32[4,64,640]{2,1,0:T(8,128)S(1)} collective-permute-done((f32[4,64,640]{2,1,0:T(8,128)S(1)}, f32[4,64,640]{2,1,0:T(8,128)S(1)}, u32[]{:S(2)}, u32[]{:S(2)}) %collective-permute-start.5) | collective-permute-done | bytes 655392 | tf_op jit(solution)/shard_map/ppermute | solution.py:41
  82.6 0.1 collective-permute-done.6
  82.8 0.0 copy-start.5
  82.8 0.0 copy-start.7
  82.8 0.1 add_add_fusion
  82.9 1.3 %collective-permute-start.7 = (f32[64,640]{1,0:T(8,128)S(1)}, f32[64,640]{1,0:T(8,128)S(1)}, u32[]{:S(2)}, u32[]{:S(2)}) collective-permute-start(f32[64,640]{1,0:T(8,128)S(1)} %get-tuple-element.53), channel_id=1, source_target_pairs={{0,16},{1,17},{2,18},{3,19},{4,6},{5,7},{6,4},{7,5},{8,24},{9,25},... | collective-permute-start | bytes 491528 | tf_op jit(solution)/shard_map/ppermute | solution.py:41
  84.2 1.9 %collective-permute-start.9 = (f32[64,640]{1,0:T(8,128)S(1)}, f32[64,640]{1,0:T(8,128)S(1)}, u32[]{:S(2)}, u32[]{:S(2)}) collective-permute-start(f32[64,640]{1,0:T(8,128)S(1)} %get-tuple-element.54), channel_id=1, source_target_pairs={{0,24},{1,25},{2,26},{3,27},{4,7},{5,4},{6,5},{7,6},{8,0},{9,1},{1... | collective-permute-start | bytes 491528 | tf_op jit(solution)/shard_map/ppermute | solution.py:41
  86.1 0.1 collective-permute-start.8
  86.2 3.6 %collective-permute-done.7 = f32[64,640]{1,0:T(8,128)S(1)} collective-permute-done((f32[64,640]{1,0:T(8,128)S(1)}, f32[64,640]{1,0:T(8,128)S(1)}, u32[]{:S(2)}, u32[]{:S(2)}) %collective-permute-start.7) | collective-permute-done | bytes 163872 | tf_op jit(solution)/shard_map/ppermute | solution.py:41
  89.8 0.4 collective-permute-done.9
  90.2 2.4 %collective-permute-done.8 = f32[64,640]{1,0:T(8,128)S(1)} collective-permute-done((f32[64,640]{1,0:T(8,128)S(1)}, f32[64,640]{1,0:T(8,128)S(1)}, u32[]{:S(2)}, u32[]{:S(2)}) %collective-permute-start.8) | collective-permute-done | bytes 163872 | tf_op jit(solution)/shard_map/ppermute | solution.py:41
  92.7 0.1 fusion.3
  92.7 11.6 %all_to_all.17 = f32[8,8,640]{2,1,0:T(8,128)S(1)} all-to-all(f32[8,8,640]{2,1,0:T(8,128)S(1)} %fusion.3), channel_id=1, replica_groups={{0,32,64,96,128,160,192,224},{4,36,68,100,132,164,196,228},{8,40,72,104..., dimensions={0} | all-to-all | bytes 327680 | tf_op jit(solution)/shard_map/all_to_all | solution.py:310
  104.3 2.7 %collective-permute-start.12 = (f32[8,640]{1,0:T(8,128)S(1)}, f32[8,640]{1,0:T(8,128)S(1)}, u32[]{:S(2)}, u32[]{:S(2)}) collective-permute-start(f32[8,640]{1,0:T(8,128)S(1)} %reduce_sum.9.r0_ref), channel_id=1, source_target_pairs={{0,3},{1,0},{2,1},{3,2},{4,7},{5,4},{6,5},{7,6},{8,11},{9,8},{10,9... | collective-permute-start | bytes 61448 | tf_op jit(solution)/shard_map/ppermute | solution.py:41
  107.0 0.9 collective-permute-start.11
  107.9 0.1 collective-permute-start.10
  108.0 0.0 copy-done.5
  108.0 0.0 copy-done.7
  108.0 1.6 %other_grads.1 = (bf16[256,512]{1,0:T(8,128)(2,1)}, bf16[256,128]{1,0:T(8,128)(2,1)}, bf16[256,128]{1,0:T(8,128)(2,1)}) custom-call(s32[4]{0:T(128)S(1)} %pad_add_fusion.pos_ref, f32[512,128]{1,0:T(8,128)S(1)} %bitcast.37, f32[512,128]{1,0:T(8,128)S(1)} %collective-permute-done.1.recv_ref, bf16[256,128]{1,0:T(8,128)(2,1)S(1)} %bitcast.43, ...), custom_call_target="tpu_custom_call" | custom-call | flops 100663296 | bytes 2818064 | tf_op jit(solution)/shard_map/other_grads/pallas_call | solution.py:264
  109.6 0.0 collective-permute-done.12.r3_ref
  109.6 2.7 %collective-permute-done.11.r2_ref = f32[8,640]{1,0:T(8,128)S(1)} collective-permute-done((f32[8,640]{1,0:T(8,128)S(1)}, f32[8,640]{1,0:T(8,128)S(1)}, u32[]{:S(2)}, u32[]{:S(2)}) %collective-permute-start.11) | collective-permute-done | bytes 20512 | tf_op jit(solution)/shard_map/ppermute | solution.py:41
  112.3 0.6 collective-permute-done.10.r1_ref
  112.9 1.2 %place.1 = f32[8,2560]{1,0:T(8,128)} custom-call(s32[4]{0:T(128)S(1)} %pad_add_fusion.pos_ref, f32[8,640]{1,0:T(8,128)S(1)} %reduce_sum.9.r0_ref, f32[8,640]{1,0:T(8,128)S(1)} %collective-permute-done.10.r1_ref, f32[8,640]{1,0:T(8,128)S(1)} %collective-permute-done.11.r2_ref, f32[8,640]{1,0:T(8,128)S(1)} %collective-permute-done.12.r3_ref), custom_call_target="tpu_custom_call" | custom-call | bytes 163856 | tf_op jit(solution)/shard_map/place/pallas_call | solution.py:264
  (4 shorter events, 0.1 us)
Async XLA Ops:
  0.6 3.4 %copy-start = (bf16[1,256,2560]{2,1,0:T(8,128)(2,1)S(1)}, bf16[1,256,2560]{2,1,0:T(8,128)(2,1)}, u32[]{:S(2)}) copy-start(bf16[1,256,2560]{2,1,0:T(8,128)(2,1)} %param.13) | copy-start | bytes 3932164
  0.6 3.4 %copy-start.9 = (f32[8]{0:T(128)S(1)}, f32[8]{0:T(128)}, u32[]{:S(2)}) copy-start(f32[8]{0:T(128)} %rate_ref.3) | copy-start | bytes 100
  0.7 3.4 %copy-start.8 = (s32[1,8,256]{2,1,0:T(8,128)S(1)}, s32[1,8,256]{2,1,0:T(8,128)}, u32[]{:S(2)}) copy-start(s32[1,8,256]{2,1,0:T(8,128)} %param.10) | copy-start | bytes 24580
  0.7 3.4 %copy-start.1 = (bf16[1,256,128]{2,1,0:T(8,128)(2,1)S(1)}, bf16[1,256,128]{2,1,0:T(8,128)(2,1)}, u32[]{:S(2)}) copy-start(bf16[1,256,128]{2,1,0:T(8,128)(2,1)} %param.9) | copy-start | bytes 196612
  0.7 3.4 %copy-start.2 = (bf16[1,256,128]{2,1,0:T(8,128)(2,1)S(1)}, bf16[1,256,128]{2,1,0:T(8,128)(2,1)}, u32[]{:S(2)}) copy-start(bf16[1,256,128]{2,1,0:T(8,128)(2,1)} %param.8) | copy-start | bytes 196612
  0.7 3.4 %copy-start.3 = (bf16[1,256,512]{2,1,0:T(8,128)(2,1)S(1)}, bf16[1,256,512]{2,1,0:T(8,128)(2,1)}, u32[]{:S(2)}) copy-start(bf16[1,256,512]{2,1,0:T(8,128)(2,1)} %param.7) | copy-start | bytes 786436
  3.9 56.1 %collective-permute-start.3 = (f32[256,2560]{1,0:T(8,128)}, f32[256,2560]{1,0:T(8,128)}, u32[]{:S(2)}, u32[]{:S(2)}) collective-permute-start(f32[256,2560]{1,0:T(8,128)} %bitcast_convert_fusion), channel_id=1, source_target_pairs={{0,4},{1,5},{2,6},{3,7},{4,0},{5,1},{6,2},{7,3},{8,12},{9,13},{10,... | collective-permute-start | bytes 7864328 | tf_op jit(solution)/shard_map/ppermute | solution.py:41
  8.5 1.8 %collective-permute-start = (f32[520,128]{1,0:T(8,128)S(1)}, f32[520,128]{1,0:T(8,128)S(1)}, u32[]{:S(2)}, u32[]{:S(2)}) collective-permute-start(f32[520,128]{1,0:T(8,128)S(1)} %get-tuple-element.30), channel_id=1, source_target_pairs={{0,4},{1,5},{2,6},{3,7},{4,0},{5,1},{6,2},{7,3},{8,12},{9,13},{10,... | collective-permute-start | bytes 798728 | tf_op jit(solution)/shard_map/ppermute | solution.py:41
  53.4 3.3 %collective-permute-start.1 = (f32[512,128]{1,0:T(8,128)S(1)}, f32[512,128]{1,0:T(8,128)S(1)}, u32[]{:S(2)}, u32[]{:S(2)}) collective-permute-start(f32[512,128]{1,0:T(8,128)S(1)} %core_states.1), channel_id=1, source_target_pairs={{0,4},{1,5},{2,6},{3,7},{4,0},{5,1},{6,2},{7,3},{8,12},{9,13},{10,... | collective-permute-start | bytes 786440 | tf_op jit(solution)/shard_map/ppermute | solution.py:41
  56.7 1.6 %copy-start.4 = (f32[256,128]{1,0:T(8,128)}, f32[256,128]{1,0:T(8,128)S(1)}, u32[]{:S(2)}) copy-start(f32[256,128]{1,0:T(8,128)S(1)} %get-tuple-element.42.gr_ref) | copy-start | bytes 393220
  56.7 3.3 %copy-start.6 = (f32[256,128]{1,0:T(8,128)}, f32[256,128]{1,0:T(8,128)S(1)}, u32[]{:S(2)}) copy-start(f32[256,128]{1,0:T(8,128)S(1)} %get-tuple-element.43.gw_ref) | copy-start | bytes 393220
  58.4 1.7 %collective-permute-start.2 = (f32[256,256]{1,0:T(8,128)S(1)}, f32[256,256]{1,0:T(8,128)S(1)}, u32[]{:S(2)}, u32[]{:S(2)}) collective-permute-start(f32[256,256]{1,0:T(8,128)S(1)} %get-tuple-element.48), channel_id=1, source_target_pairs={{0,4},{1,5},{2,6},{3,7},{4,0},{5,1},{6,2},{7,3},{8,12},{9,13},{10,... | collective-permute-start | bytes 786440 | tf_op jit(solution)/shard_map/ppermute | solution.py:41
  63.4 12.3 %collective-permute-start.4 = (f32[4,64,640]{2,1,0:T(8,128)S(1)}, f32[4,64,640]{2,1,0:T(8,128)S(1)}, u32[]{:S(2)}, u32[]{:S(2)}) collective-permute-start(f32[4,64,640]{2,1,0:T(8,128)S(1)} %get-tuple-element.50), channel_id=1, source_target_pairs={{0,2},{1,3},{2,0},{3,1},{4,20},{5,21},{6,22},{7,23},{8,10},{9,11},... | collective-permute-start | bytes 1966088 | tf_op jit(solution)/shard_map/ppermute | solution.py:41
  66.5 16.1 %collective-permute-start.5 = (f32[4,64,640]{2,1,0:T(8,128)S(1)}, f32[4,64,640]{2,1,0:T(8,128)S(1)}, u32[]{:S(2)}, u32[]{:S(2)}) collective-permute-start(f32[4,64,640]{2,1,0:T(8,128)S(1)} %get-tuple-element.51), channel_id=1, source_target_pairs={{0,1},{1,2},{2,3},{3,0},{4,12},{5,13},{6,14},{7,15},{8,9},{9,10},{... | collective-permute-start | bytes 1966088 | tf_op jit(solution)/shard_map/ppermute | solution.py:41
  67.1 15.6 %collective-permute-start.6 = (f32[4,64,640]{2,1,0:T(8,128)S(1)}, f32[4,64,640]{2,1,0:T(8,128)S(1)}, u32[]{:S(2)}, u32[]{:S(2)}) collective-permute-start(f32[4,64,640]{2,1,0:T(8,128)S(1)} %get-tuple-element.52), channel_id=1, source_target_pairs={{0,3},{1,0},{2,1},{3,2},{4,28},{5,29},{6,30},{7,31},{8,11},{9,8},{... | collective-permute-start | bytes 1966088 | tf_op jit(solution)/shard_map/ppermute | solution.py:41
  82.8 25.2 %copy-start.5 = (f32[256,128]{1,0:T(8,128)S(1)}, f32[256,128]{1,0:T(8,128)}, u32[]{:S(2)}) copy-start(f32[256,128]{1,0:T(8,128)} %copy-done.4) | copy-start | bytes 393220
  82.8 25.2 %copy-start.7 = (f32[256,128]{1,0:T(8,128)S(1)}, f32[256,128]{1,0:T(8,128)}, u32[]{:S(2)}) copy-start(f32[256,128]{1,0:T(8,128)} %copy-done.6) | copy-start | bytes 393220
  82.9 6.9 %collective-permute-start.7 = (f32[64,640]{1,0:T(8,128)S(1)}, f32[64,640]{1,0:T(8,128)S(1)}, u32[]{:S(2)}, u32[]{:S(2)}) collective-permute-start(f32[64,640]{1,0:T(8,128)S(1)} %get-tuple-element.53), channel_id=1, source_target_pairs={{0,16},{1,17},{2,18},{3,19},{4,6},{5,7},{6,4},{7,5},{8,24},{9,25},... | collective-permute-start | bytes 491528 | tf_op jit(solution)/shard_map/ppermute | solution.py:41
  84.2 6.0 %collective-permute-start.9 = (f32[64,640]{1,0:T(8,128)S(1)}, f32[64,640]{1,0:T(8,128)S(1)}, u32[]{:S(2)}, u32[]{:S(2)}) collective-permute-start(f32[64,640]{1,0:T(8,128)S(1)} %get-tuple-element.54), channel_id=1, source_target_pairs={{0,24},{1,25},{2,26},{3,27},{4,7},{5,4},{6,5},{7,6},{8,0},{9,1},{1... | collective-permute-start | bytes 491528 | tf_op jit(solution)/shard_map/ppermute | solution.py:41
  86.1 6.5 %collective-permute-start.8 = (f32[64,640]{1,0:T(8,128)S(1)}, f32[64,640]{1,0:T(8,128)S(1)}, u32[]{:S(2)}, u32[]{:S(2)}) collective-permute-start(f32[64,640]{1,0:T(8,128)S(1)} %get-tuple-element.55), channel_id=1, source_target_pairs={{0,8},{1,9},{2,10},{3,11},{4,5},{5,6},{6,7},{7,4},{8,16},{9,17},{1... | collective-permute-start | bytes 491528 | tf_op jit(solution)/shard_map/ppermute | solution.py:41
  104.3 5.2 %collective-permute-start.12 = (f32[8,640]{1,0:T(8,128)S(1)}, f32[8,640]{1,0:T(8,128)S(1)}, u32[]{:S(2)}, u32[]{:S(2)}) collective-permute-start(f32[8,640]{1,0:T(8,128)S(1)} %reduce_sum.9.r0_ref), channel_id=1, source_target_pairs={{0,3},{1,0},{2,1},{3,2},{4,7},{5,4},{6,5},{7,6},{8,11},{9,8},{10,9... | collective-permute-start | bytes 61448 | tf_op jit(solution)/shard_map/ppermute | solution.py:41
  107.0 5.3 %collective-permute-start.11 = (f32[8,640]{1,0:T(8,128)S(1)}, f32[8,640]{1,0:T(8,128)S(1)}, u32[]{:S(2)}, u32[]{:S(2)}) collective-permute-start(f32[8,640]{1,0:T(8,128)S(1)} %reduce_sum.9.r0_ref), channel_id=1, source_target_pairs={{0,2},{1,3},{2,0},{3,1},{4,6},{5,7},{6,4},{7,5},{8,10},{9,11},{10,... | collective-permute-start | bytes 61448 | tf_op jit(solution)/shard_map/ppermute | solution.py:41
  107.9 5.0 %collective-permute-start.10 = (f32[8,640]{1,0:T(8,128)S(1)}, f32[8,640]{1,0:T(8,128)S(1)}, u32[]{:S(2)}, u32[]{:S(2)}) collective-permute-start(f32[8,640]{1,0:T(8,128)S(1)} %reduce_sum.9.r0_ref), channel_id=1, source_target_pairs={{0,1},{1,2},{2,3},{3,0},{4,5},{5,6},{6,7},{7,4},{8,9},{9,10},{10,1... | collective-permute-start | bytes 61448 | tf_op jit(solution)/shard_map/ppermute | solution.py:41

commit v2 on v1

v2 whole, which is shorter than its diff:
```python
import jax
import jax.numpy as jnp
from jax import lax
from jax.experimental import pallas as pl
from jax.experimental.pallas import tpu as pltpu
from jax.sharding import PartitionSpec as P

HEAD_DIM = 64
STATE = 128
HEADS = 8
TOK = 256
CH = HEADS * HEAD_DIM
D = 2560
NX, NY, NZ = 4, 4, 8
CHIPS = NY * NZ
HALF = CH // 2
PIECE = HALF // CHIPS
BLK = D // NX
BOTH = ("seq", "dp")

f32, bf16 = jnp.float32, jnp.bfloat16
RATE_UNIT = 1.0 / (8.0 * TOK * 64)
HI = lax.Precision.HIGHEST
NT = (((1,), (1,)), ((), ()))
TN = (((0,), (0,)), ((), ()))
NN = (((1,), (0,)), ((), ()))


def mm(a, b, dims):
    return lax.dot_general(a, b, dims, preferred_element_type=f32)


def permute(v, target):
    pairs = []
    for z in range(NZ):
        for y in range(NY):
            for c in range(2):
                for x in range(NX):
                    tz, ty, tc, tx = target(z, y, c, x)
                    src = ((z * NY + y) * 2 + c) * NX + x
                    dst = ((tz * NY + ty) * 2 + tc) * NX + tx
                    pairs.append((src, dst))
    return lax.ppermute(v, BOTH, pairs)


def swap_core(z, y, c, x):
    return z, y, 1 - c, x


def first_axis(k):
    return lambda z, y, c, x: (z, y, c, (x + k) % NX) if c == 0 else (z, (y + k) % NY, c, x)


def second_axis(k):
    return lambda z, y, c, x: (z, (y + k) % NY, c, x) if c == 0 else (z, y, c, (x + k) % NX)


def x_axis(k):
    return lambda z, y, c, x: (z, y, c, (x + k) % NX)


def rate_lanes(rate_ref, width):
    lane = lax.broadcasted_iota(jnp.int32, (1, width), 1) // (width // HEADS)
    rates = jnp.zeros((1, width), f32)
    for h in range(HEADS):
        rates = jnp.where(lane == h, rate_ref[h] * RATE_UNIT, rates)
    return rates


def signed_tri():
    t = lax.broadcasted_iota(jnp.int32, (TOK, TOK), 0)
    s = lax.broadcasted_iota(jnp.int32, (TOK, TOK), 1)
    half = TOK // 2
    plus = (s >= half) & (s <= t)
    minus = (s < half) & (s > t)
    return jnp.where(plus, 1.0, jnp.where(minus, -1.0, 0.0)).astype(f32)


def step_lanes(cum, dt_lanes):
    ones = jnp.ones((8, TOK // 2), f32)
    start = -lax.dot_general(ones, dt_lanes[:, : TOK // 2], NT, precision=HI, preferred_element_type=f32)[:1]
    row = lax.broadcasted_iota(jnp.int32, (TOK, CH), 0)
    return jnp.where(row == 0, cum - start, cum - pltpu.roll(cum, 1, 0)), start


def gate(v):
    s = 1.0 - v * (1.0 / 8.0)
    for n in (7.0, 6.0, 5.0, 4.0, 3.0, 2.0):
        s = 1.0 - v * (1.0 / n) * s
    return jnp.sqrt(jnp.where(v < 0.25, v * s, 1.0 - jnp.exp(-v)))


def local_forward(pos_ref, rate_ref, x_ref, b_ref, dt_ref, mine_ref, send_ref, tot_ref, xw_ref, xt_ref, cum_ref):
    dt = dt_ref[...].astype(f32)
    dt_lanes = jnp.broadcast_to(dt[:, None, :], (HEADS, HEAD_DIM, TOK)).reshape(CH, TOK)
    cum = lax.dot_general(signed_tri(), dt_lanes, NT, precision=HI, preferred_element_type=f32)
    cum_ref[...] = cum
    rate = rate_lanes(rate_ref, CH)
    xw = x_ref[...].astype(f32) * gate(step_lanes(cum, dt_lanes)[0] * (2.0 * rate))
    xw_ref[...] = xw.astype(bf16)
    xt = (xw * jnp.exp((cum - cum[TOK - 1:]) * rate)).astype(bf16)
    xt_ref[...] = xt
    own = mm(xt, b_ref[...], TN)
    head = lax.broadcasted_iota(jnp.int32, (HEADS, 1), 0)
    rate_col = jnp.zeros((HEADS, 1), f32)
    for h in range(HEADS):
        rate_col = jnp.where(head == h, rate_ref[h] * RATE_UNIT, rate_col)
    tot = jnp.broadcast_to(-(jnp.sum(dt, axis=1, keepdims=True) * rate_col), (HEADS, STATE))
    tot_ref[...] = tot
    send_ref[HALF:, :] = tot
    core = pos_ref[2]

    @pl.when(core == 0)
    def _():
        mine_ref[...] = own[:HALF]
        send_ref[:HALF, :] = own[HALF:]

    @pl.when(core == 1)
    def _():
        mine_ref[...] = own[HALF:]
        send_ref[:HALF, :] = own[:HALF]


def local_backward(pos_ref, rate_ref, cum_ref, dt_ref, c_ref, w_ref, g_ref, mine_ref, send_ref, gy_ref, gyd_ref, wide_ref):
    dt = dt_ref[...].astype(f32)
    dt_lanes = jnp.broadcast_to(dt[:, None, :], (HEADS, HEAD_DIM, TOK)).reshape(CH, TOK)
    rate = rate_lanes(rate_ref, CH)
    cum = cum_ref[...]
    start = step_lanes(cum, dt_lanes)[1]
    wide_ref[...] = g_ref[...].astype(f32)
    gy = mm(g_ref[...], w_ref[...], NT).astype(bf16)
    gy_ref[...] = gy
    gyd = (gy.astype(f32) * jnp.exp((start - cum) * rate)).astype(bf16)
    gyd_ref[...] = gyd
    adj = mm(gyd, c_ref[...], TN)
    core = pos_ref[2]

    @pl.when(core == 0)
    def _():
        mine_ref[...] = adj[:HALF]
        send_ref[...] = adj[HALF:]

    @pl.when(core == 1)
    def _():
        mine_ref[...] = adj[HALF:]
        send_ref[...] = adj[:HALF]


def my_heads(core, tots):
    return jnp.where(core == 0, tots[:HEADS // 2], tots[HEADS // 2:])


def decay_rows(tots):
    rows = jnp.exp(tots)
    return jnp.broadcast_to(rows[:, None, :], (HEADS // 2, HEAD_DIM, STATE)).reshape(HALF, STATE)


def chip_forward(pos_ref, mine_ref, peer_ref, tot_ref, out_ref):
    core = pos_ref[2]
    own = my_heads(core, tot_ref[...])
    other = my_heads(core, peer_ref[HALF:, :])
    mine, peer = mine_ref[...], peer_ref[:HALF, :]
    second = decay_rows(jnp.where(core == 0, other, own))
    chip = jnp.where(core == 0, mine, peer) * second + jnp.where(core == 0, peer, mine)
    out_ref[:, :PIECE, :] = chip.reshape(CHIPS, PIECE, STATE)
    tots = jnp.broadcast_to((own + other)[:, None, None, :], (HEADS // 2, CHIPS // (HEADS // 2), PIECE, STATE))
    out_ref[:, PIECE:, :] = tots.reshape(CHIPS, PIECE, STATE)


def scan_forward(pos_ref, in_ref, mine_ref, peer_ref, tot_ref, fpeer_ref, out_ref):
    core = pos_ref[2]
    first = decay_rows(my_heads(core, jnp.where(core == 0, tot_ref[...], fpeer_ref[HALF:, :])))
    mine, peer = mine_ref[...], peer_ref[...]
    chip = jnp.where(core == 0, mine, peer) + jnp.where(core == 0, peer, mine) * first
    out_ref[:, PIECE:, :] = chip.reshape(CHIPS, PIECE, STATE)
    acc = jnp.zeros((PIECE, STATE), f32)
    for k in range(CHIPS):
        out_ref[k, :PIECE, :] = acc
        acc = acc * jnp.exp(in_ref[k, PIECE:, :]) + in_ref[k, :PIECE, :]


def scan_backward(dec_ref, in_ref, out_ref):
    acc = jnp.zeros((PIECE, STATE), f32)
    for k in range(CHIPS - 1, -1, -1):
        out_ref[k] = acc
        acc = acc * jnp.exp(dec_ref[k, PIECE:, :]) + in_ref[k, PIECE:, :]


def core_forward(pos_ref, got_ref, mine_ref, peer_ref, tot_ref, keep_ref, send_ref):
    core = pos_ref[2]
    into = got_ref[:, :PIECE, :].reshape(HALF, STATE)
    first = decay_rows(my_heads(core, jnp.where(core == 0, tot_ref[...], peer_ref[HALF:, :])))
    after = into * first + jnp.where(core == 0, mine_ref[...], peer_ref[:HALF, :])
    keep_ref[...] = jnp.where(core == 0, into, after)
    send_ref[...] = jnp.where(core == 0, after, into)


def core_backward(pos_ref, got_ref, mine_ref, peer_ref, tot_ref, fpeer_ref, keep_ref, send_ref):
    core = pos_ref[2]
    after = got_ref[...].reshape(HALF, STATE)
    second = decay_rows(my_heads(core, jnp.where(core == 0, fpeer_ref[HALF:, :], tot_ref[...])))
    into = after * second + jnp.where(core == 0, peer_ref[...], mine_ref[...])
    keep_ref[...] = jnp.where(core == 0, into, after)
    send_ref[...] = jnp.where(core == 0, after, into)


def both_halves(core, keep, recv):
    low = jnp.where(core == 0, keep, recv)
    high = jnp.where(core == 0, recv, keep)
    return jnp.concatenate([low, high], axis=0).astype(bf16)


def intra(rate_ref, dt_ref, cum_ref, b_ref, c_ref, gy_ref, xw_ref,
          y_ref, gin_ref, wt_ref, hd_ref, gr_ref, gw_ref):
    dt = dt_ref[...].astype(f32)
    tri = signed_tri()
    cum_rows = lax.dot_general(dt, tri, NT, precision=HI, preferred_element_type=f32)
    rate = rate_lanes(rate_ref, CH)
    cum = cum_ref[...]
    i = lax.broadcasted_iota(jnp.int32, (TOK, TOK), 0)
    j = lax.broadcasted_iota(jnp.int32, (TOK, TOK), 1)
    lower = i >= j
    b = b_ref[...]
    c = c_ref[...]
    scores = mm(c, b, NT)
    pairs = jnp.zeros((TOK, TOK), f32)
    for h in range(HEADS):
        lanes = slice(h * HEAD_DIM, (h + 1) * HEAD_DIM)
        r = rate_ref[h] * RATE_UNIT
        gap = cum_rows[h:h + 1, :] - cum[:, h * HEAD_DIM:h * HEAD_DIM + 1]
        mask = jnp.exp(jnp.where(lower, gap * r, -jnp.inf))
        mixed = (mask * scores).astype(bf16)
        xw = xw_ref[:, lanes]
        gy = gy_ref[:, lanes]
        y_ref[:, lanes] = mm(mixed, xw, NN)
        gin_ref[:, lanes] = mm(mixed, gy, TN)
        pairs = pairs + mask * mm(gy, xw, NT)
    pairs = pairs.astype(bf16)
    gr_ref[...] = mm(pairs, b, NN)
    gw_ref[...] = mm(pairs, c, TN)
    dt_lanes = jnp.broadcast_to(dt[:, None, :], (HEADS, HEAD_DIM, TOK)).reshape(CH, TOK)
    steps, start = step_lanes(cum, dt_lanes)
    w = gate(steps * (2.0 * rate))
    gin_ref[...] = gin_ref[...] * w
    wt_ref[...] = w * jnp.exp((cum - cum[TOK - 1:]) * rate)
    hd_ref[...] = jnp.exp((start - cum) * rate)


def select_rows(core, y_at):
    row = lax.broadcasted_iota(jnp.int32, (CH // 2, CH), 0)
    lane = lax.broadcasted_iota(jnp.int32, (CH // 2, CH), 1)
    y = (y_at + row // 64) % NY
    z = (row // 8) % NZ
    return jnp.where(lane == ((z * NY + y) * 2 + core) * 8 + row % 8, 1.0, 0.0).astype(bf16)


def forward_out(pos_ref, carry_ref, recv_ref, c_ref, y_ref, hd_ref, out_ref, mine_ref, other_ref):
    y_at, core = pos_ref[1], pos_ref[2]
    state = both_halves(core, carry_ref[...], recv_ref[...])
    out = (y_ref[...] + hd_ref[...] * mm(c_ref[...], state, NT)).astype(bf16)
    out_ref[...] = out
    mine_ref[...] = mm(select_rows(core, y_at), out, NT).astype(bf16)
    other_ref[...] = mm(select_rows(1 - core, y_at), out, NT)


def partial_grad(pos_ref, mine_ref, peer_ref, g_ref, gp_ref, s0_ref, s1_ref, s2_ref, s3_ref):
    core, x_at = pos_ref[2], pos_ref[3]
    outs = (s0_ref, s1_ref, s2_ref, s3_ref)
    mine = mine_ref[...]
    peer = peer_ref[...].astype(bf16)
    for xr in range(NX):
        at = pl.multiple_of(((x_at + xr) % NX) * BLK, 128)
        tile = mm(mine, g_ref[:, pl.ds(at, BLK)], NN)
        tile = tile + mm(peer, gp_ref[:, pl.ds(at, BLK)].astype(bf16), NN)

        @pl.when(core == 0)
        def _():
            for yr in range(NY):
                outs[xr][yr] = tile[yr * 64:(yr + 1) * 64]

        @pl.when(core == 1)
        def _():
            for yr in range(NY):
                outs[yr][xr] = tile[yr * 64:(yr + 1) * 64]


def other_grads(pos_ref, carry_ref, recv_ref, after_ref, recv2_ref, b_ref, gin_ref, wt_ref, gyd_ref, xt_ref, gr_ref, gw_ref,
                gi_ref, gwr_ref, grd_ref):
    core = pos_ref[2]
    state = both_halves(core, carry_ref[...], recv_ref[...])
    adj = both_halves(core, after_ref[...], recv2_ref[...])
    gi_ref[...] = (gin_ref[...] + wt_ref[...] * mm(b_ref[...], adj, NT)).astype(bf16)
    grd_ref[...] = (gr_ref[...] + mm(gyd_ref[...], state, NN)).astype(bf16)
    gwr_ref[...] = (gw_ref[...] + mm(xt_ref[...], adj, NN)).astype(bf16)


def place(pos_ref, r0_ref, r1_ref, r2_ref, r3_ref, out_ref):
    x_at = pos_ref[3]
    for k, ref in enumerate((r0_ref, r1_ref, r2_ref, r3_ref)):
        at = pl.multiple_of(((x_at + NX - k) % NX) * BLK, 128)
        out_ref[:, pl.ds(at, BLK)] = ref[...]


def call(body, outs, scalars, *args, us=1):
    specs = [pl.BlockSpec(memory_space=pltpu.SMEM)] * scalars
    specs += [pl.BlockSpec(memory_space=pltpu.VMEM)] * (len(args) - scalars)
    shapes = [jax.ShapeDtypeStruct(s, d) for s, d in outs]
    moved = sum(a.size * a.dtype.itemsize for a in args) + sum(s.size * s.dtype.itemsize for s in shapes)
    got = pl.pallas_call(
        body,
        out_shape=shapes,
        in_specs=specs,
        out_specs=[pl.BlockSpec(memory_space=pltpu.VMEM)] * len(shapes),
        cost_estimate=pl.CostEstimate(flops=us * 1_000_000_000, bytes_accessed=moved, transcendentals=0),
        compiler_params=pltpu.CompilerParams(vmem_limit_bytes=48 << 20),
        name=body.__name__,
    )(*args)
    return got if len(got) > 1 else got[0]


def shards(inputs, write_vecs, read_vecs, dt_code, a_rate, w_out, grad_out):
    at = lax.axis_index("seq")
    pos = jnp.stack([at >> 3, (at >> 1) & 3, at & 1, lax.axis_index("dp")]).astype(jnp.int32)
    x, b, c, dt, g = inputs[0], write_vecs[0], read_vecs[0], dt_code[0], grad_out[0]
    chips = [[q * 2 + core for q in range(CHIPS)] for core in range(2)]
    depth = [[(z * NY + y) * 2 + core for z in range(NZ)] for y in range(NY) for core in range(2)]

    def over(v, groups):
        return lax.all_to_all(v, "seq", 0, 0, axis_index_groups=groups, tiled=True)

    half, wide = ((HALF, STATE), f32), ((TOK, CH), f32)
    tokens, narrow = ((TOK, CH), bf16), ((TOK, STATE), f32)
    mine, send, tot, xw, xt, cum = call(
        local_forward, [half, ((HALF + 8, STATE), f32), ((HEADS, STATE), f32), tokens, tokens, wide],
        2, pos, a_rate, x, b, dt, us=2)
    peer = permute(send, swap_core)
    chip = call(chip_forward, [((CHIPS, 2 * PIECE, STATE), f32)], 1, pos, mine, peer, tot)
    pieces = over(chip, chips)

    cum2, g2 = lax.optimization_barrier((cum, g, chip))[:2]
    bmine, bsend, gy, gyd, g_wide = call(local_backward, [half, half, tokens, tokens, ((TOK, D), f32)], 2, pos, a_rate, cum2, dt, c, w_out, g2, us=4)
    bpeer = permute(bsend, swap_core)
    y_in, gin, wt, hd, gr, gw = call(intra, [wide, wide, wide, wide, narrow, narrow], 1, a_rate, dt, cum2, b, c, gy, xw, us=3)
    pieces, bpeer, y_in, g_wide = lax.optimization_barrier((pieces, bpeer, y_in, g_wide))
    g_peer = permute(g_wide, swap_core)

    got = over(call(scan_forward, [((CHIPS, 2 * PIECE, STATE), f32)], 1, pos, pieces, bmine, bpeer, tot, peer), chips)
    carry, send = call(core_forward, [half, half], 1, pos, got, mine, peer, tot)
    recv = permute(send, swap_core)
    out, rows, send = call(
        forward_out, [tokens, ((CH // 2, TOK), bf16), ((CH // 2, TOK), f32)], 1, pos, carry, recv, c, y_in, hd, us=2)
    s = call(partial_grad, [((NY, 64, BLK), f32)] * 4, 1, pos, rows, permute(send, swap_core), g, g_peer, us=4)

    got2, pieces2 = lax.optimization_barrier((got, pieces, s[1]))[:2]
    back = over(call(scan_backward, [((CHIPS, PIECE, STATE), f32)], 0, pieces2, got2), chips)
    s1, s2, s3 = permute(s[1], first_axis(1)), permute(s[2], first_axis(2)), permute(s[3], first_axis(3))
    s1, s2, s3, back = lax.optimization_barrier((s1, s2, s3, back))
    s = s[0] + s2 + s1 + s3
    after, send = call(core_backward, [half, half], 1, pos, back, bmine, bpeer, tot, peer)
    recv2 = permute(send, swap_core)
    s = s[0] + permute(s[2], second_axis(2)) + permute(s[1], second_axis(1)) + permute(s[3], second_axis(3))
    s = jnp.sum(over(s.reshape(NZ, 8, BLK), depth), axis=0)
    grad_w_out = call(place, [((8, D), f32)], 1, pos, s, permute(s, x_axis(1)), permute(s, x_axis(2)),
                      permute(s, x_axis(3)))
    gi, gwr, grd = call(
        other_grads, [tokens, ((TOK, STATE), bf16), ((TOK, STATE), bf16)],
        1, pos, carry, recv, after, recv2, b, gin, wt, gyd, xt, gr, gw, us=2)
    return out[None], gi[None], gwr[None], grd[None], grad_w_out


def solution(mesh):
    rows = P("dp", "seq", None)
    return jax.shard_map(
        shards,
        mesh=mesh,
        in_specs=(rows, rows, rows, P("dp", None, "seq"), P(), P(), rows),
        out_specs=(rows, rows, rows, rows, P("seq", None)),
        check_vma=False,
    )
```

time: 114 us -> 124 us (1.088)
  blocking collectives: 54 us -> 36 us
  local copies, waits for them, and re-layouts: 0.08 us -> 16.2 us
  starting transfers between devices: 14.5 us -> 28.3 us
  waiting for transfers between devices: 25.1 us -> 21.2 us
  Pallas kernels: 16.1 us -> 19.6 us
  other arithmetic: 3.51 us -> 0.95 us
    all_to_all x3 -> x2, blocking collectives: 54 us -> 36 us  [over(): return lax.all_to_all(v, 'seq', 0, 0, axis_index_groups=groups, tiled=True)]
    unnamed x20 -> x74, local copies, waits for them, and re-layouts: 0.04 us -> 16.2 us
    all_to_all x0 -> x2, starting transfers between devices: none -> 15.3 us  [over(): return lax.all_to_all(v, 'seq', 0, 0, axis_index_groups=groups, tiled=True)]
    ppermute x13 -> x15, waiting for transfers between devices: 25.1 us -> 13.3 us  [permute(): return lax.ppermute(v, BOTH, pairs)]
    all_to_all x0 -> x2, waiting for transfers between devices: none -> 7.93 us  [over(): return lax.all_to_all(v, 'seq', 0, 0, axis_index_groups=groups, tiled=True)]
    pallas_call x9 -> x12, Pallas kernels: 16.1 us -> 19.6 us  [call(): pl.pallas_call(body, out_shape=shapes, in_specs=specs, out_specs=[pl.Bloc...]
    convert_element_type x1 -> x0, other arithmetic: 3.24 us -> none  [shards(): g_peer = permute(g.astype(f32), swap_core)]
    ppermute x13 -> x15, starting transfers between devices: 14.5 us -> 13 us  [permute(): return lax.ppermute(v, BOTH, pairs)]
  transfers between devices with their start and end apart: 13 -> 17, of which waited for: 10 -> 10; matrix products, arithmetic and copies ran while one was open for 0% -> 0% of each run, Pallas kernels for 10% -> 9%
where the time goes in v2:
time: 124 us; the launch traced here: 123 us
  blocking collectives  36 us (29%)
  starting transfers between devices  28.3 us (23%)
  waiting for transfers between devices  21.2 us (17%)
  Pallas kernels  19.6 us (16%)
  local copies, waits for them, and re-layouts  16.2 us (13%)
    all_to_all x2, blocking collectives, over(): return lax.all_to_all(v, 'seq', 0, 0, axis_index_groups=groups, tiled=True)  36 us
    pallas_call x12, Pallas kernels, call(): pl.pallas_call(body, out_shape=shapes, in_specs=specs, out_specs=[pl.Bloc...  19.6 us
    unnamed x74, local copies, waits for them, and re-layouts  16.2 us
    all_to_all x2, starting transfers between devices, over(): return lax.all_to_all(v, 'seq', 0, 0, axis_index_groups=groups, tiled=True)  15.3 us
    ppermute x15, waiting for transfers between devices, permute(): return lax.ppermute(v, BOTH, pairs)  13.3 us
    ppermute x15, starting transfers between devices, permute(): return lax.ppermute(v, BOTH, pairs)  13 us
    all_to_all x2, waiting for transfers between devices, over(): return lax.all_to_all(v, 'seq', 0, 0, axis_index_groups=groups, tiled=True)  7.93 us
  transfers between devices with their start and end apart: 17, of which 10 were waited for; matrix products, arithmetic and copies ran while one was open for 0% of the time, Pallas kernels for 9%

profile of v2, /device:TPU:32, one launch (start us, length us, event | category | flops | bytes accessed | tf_op | source)
XLA Modules:
  0.0 123.2 jit_solution(9482665708004762674)
XLA Ops:
  0.6 0.1 pad_add_fusion.pos_ref
  0.7 0.9 copy-done.2
  1.7 0.8 copy-done.4
  2.5 0.7 copy-done.6
  3.2 0.7 copy-done.8
  3.9 2.1 %local_forward.1 = (f32[256,128]{1,0:T(8,128)S(1)}, f32[264,128]{1,0:T(8,128)S(1)}, f32[8,128]{1,0:T(8,128)S(1)}, bf16[256,512]{1,0:T(8,128)(2,1)S(1)}, bf16[256...) custom-call(s32[4]{0:T(128)S(1)} %pad_add_fusion.pos_ref, f32[8]{0:T(128)S(1)} %copy-done.8, bf16[256,512]{1,0:T(8,128)(2,1)S(1)} %bitcast.33, ...), custom_call_target="tpu_custom_call" | custom-call | flops 2000000000 | bytes 1654832 | tf_op jit(solution)/shard_map/local_forward/pallas_call | solution.py:309
  6.0 0.7 copy-done.23
  6.7 0.7 copy-done.34
  7.4 0.0 copy-start.9
  7.4 0.1 collective-permute-start
  7.5 1.3 %collective-permute-done.peer_ref.fpeer_ref = f32[264,128]{1,0:T(8,128)S(1)} collective-permute-done((f32[264,128]{1,0:T(8,128)S(1)}, f32[264,128]{1,0:T(8,128)S(1)}, u32[]{:S(2)}, u32[]{:S(2)}) %collective-permute-start) | collective-permute-done | bytes 135200 | tf_op jit(solution)/shard_map/ppermute | solution.py:43
  8.9 1.3 %chip_forward.1 = f32[32,16,128]{2,1,0:T(8,128)} custom-call(s32[4]{0:T(128)S(1)} %pad_add_fusion.pos_ref, f32[256,128]{1,0:T(8,128)S(1)} %get-tuple-element.48.mine_ref, f32[264,128]{1,0:T(8,128)S(1)} %collective-permute-done.peer_ref.fpeer_ref, f32[8,128]{1,0:T(8,128)S(1)} %get-tuple-element.50.tot_ref), custom_call_target="tpu_custom_call" | custom-call | flops 1000000000 | bytes 532496 | tf_op jit(solution)/shard_map/chip_forward/pallas_call | solution.py:309
  10.2 11.4 %all-to-all-start = ((f32[32,16,128]{2,1,0:T(8,128)}), f32[32,16,128]{2,1,0:T(8,128)S(1)}, u32[]{:S(2)}, u32[]{:S(2)}) async-start(f32[32,16,128]{2,1,0:T(8,128)} %chip_forward.1), calls=%async_computation | async-start | bytes 524288 | tf_op jit(solution)/shard_map/all_to_all | solution.py:329
  21.6 0.0 copy-start
  21.6 1.3 %copy-done = bf16[1,256,2560]{2,1,0:T(8,128)(2,1)S(1)} copy-done((bf16[1,256,2560]{2,1,0:T(8,128)(2,1)S(1)}, bf16[1,256,2560]{2,1,0:T(8,128)(2,1)}, u32[]{:S(2)}) %copy-start) | copy-done | bytes 1310744
  22.9 1.0 copy-done.28
  24.0 3.3 %local_backward.1 = (f32[256,128]{1,0:T(8,128)S(1)}, f32[256,128]{1,0:T(8,128)S(1)}, bf16[256,512]{1,0:T(8,128)(2,1)S(1)}, bf16[256,512]{1,0:T(8,128)(2,1)S(1)}, f32[256,2560]{1,0:T(8,128)S(1)}) custom-call(s32[4]{0:T(128)S(1)} %pad_add_fusion.pos_ref, f32[8]{0:T(128)S(1)} %copy-done.9, f32[256,512]{1,0:T(8,128)S(1)} %copy-done.28, s32[8,256]{1,0:T(8,128)S(1)} %bitcast.41, ...), custom_call_target="tpu_custom_call" | custom-call | flops 4000000000 | bytes 7938096 | tf_op jit(solution)/shard_map/local_backward/pallas_call | solution.py:309
  27.2 0.7 copy-done.14
  27.9 0.7 copy-done.25
  28.6 0.0 collective-permute-start.1
  28.6 3.2 %intra.1 = (f32[256,512]{1,0:T(8,128)S(1)}, f32[256,512]{1,0:T(8,128)S(1)}, f32[256,512]{1,0:T(8,128)S(1)}, f32[256,512]{1,0:T(8,128)S(1)}, f32[256,128]{1,0:T(8,128)S(1)}, /*index=5*/f32[256,128]{1,0:T(8,128)S(1)}) custom-call(f32[8]{0:T(128)S(1)} %copy-done.9, s32[8,256]{1,0:T(8,128)S(1)} %bitcast.42, f32[256,512]{1,0:T(8,128)S(1)} %copy-done.29, ...), custom_call_target="tpu_custom_call" | custom-call | flops 3000000000 | bytes 3547168 | tf_op jit(solution)/shard_map/intra/pallas_call | solution.py:309
  31.9 0.8 copy-done.10
  32.7 0.8 copy-done.12
  33.5 0.8 copy-done.17
  34.3 0.8 copy-done.19
  35.1 0.7 copy-done.30
  35.8 0.7 copy-done.32
  36.4 0.5 collective-permute-start.4
  36.9 0.9 copy-done.15
  37.8 0.6 scan_forward.1
  38.5 22.0 %all_to_all.20.got_ref.in_ref = f32[32,16,128]{2,1,0:T(8,128)S(1)} all-to-all(f32[32,16,128]{2,1,0:T(8,128)S(1)} %scan_forward.1), channel_id=1, replica_groups={{0,8,16,24,32,40,48,56,64,72,80,88,96,104,112,120,128,136,144,152,160,1..., dimensions={0} | all-to-all | bytes 524288 | tf_op jit(solution)/shard_map/all_to_all | solution.py:329
  60.5 0.9 copy-done.22
  61.4 0.6 core_forward.1
  62.0 0.1 collective-permute-start.2
  62.1 1.3 %collective-permute-done.2.recv_ref = f32[256,128]{1,0:T(8,128)S(1)} collective-permute-done((f32[256,128]{1,0:T(8,128)S(1)}, f32[256,128]{1,0:T(8,128)S(1)}, u32[]{:S(2)}, u32[]{:S(2)}) %collective-permute-start.2) | collective-permute-done | bytes 131104 | tf_op jit(solution)/shard_map/ppermute | solution.py:43
  63.5 1.6 %forward_out.1 = (bf16[256,512]{1,0:T(8,128)(2,1)}, bf16[256,256]{1,0:T(8,128)(2,1)S(1)}, f32[256,256]{1,0:T(8,128)S(1)}) custom-call(s32[4]{0:T(128)S(1)} %pad_add_fusion.pos_ref, f32[256,128]{1,0:T(8,128)S(1)} %get-tuple-element.62.carry_ref, f32[256,128]{1,0:T(8,128)S(1)} %collective-permute-done.2.recv_ref, bf16[256,128]{1,0:T(8,128)(2,1)S(1)} %bitcast.36, ...), custom_call_target="tpu_custom_call" | custom-call | flops 2000000000 | bytes 2031632 | tf_op jit(solution)/shard_map/forward_out/pallas_call | solution.py:309
  65.1 0.1 collective-permute-start.3
  65.2 1.4 %collective-permute-done.3.peer_ref = f32[256,256]{1,0:T(8,128)S(1)} collective-permute-done((f32[256,256]{1,0:T(8,128)S(1)}, f32[256,256]{1,0:T(8,128)S(1)}, u32[]{:S(2)}, u32[]{:S(2)}) %collective-permute-start.3) | collective-permute-done | bytes 262176 | tf_op jit(solution)/shard_map/ppermute | solution.py:43
  66.6 1.5 %copy-done.36 = f32[256,2560]{1,0:T(8,128)} copy-done((f32[256,2560]{1,0:T(8,128)}, f32[256,2560]{1,0:T(8,128)S(1)}, u32[]{:S(2)}) %copy-start.36) | copy-done | bytes 2621464
  68.1 3.4 %partial_grad.1 = (f32[4,64,640]{2,1,0:T(8,128)S(1)}, f32[4,64,640]{2,1,0:T(8,128)S(1)}, f32[4,64,640]{2,1,0:T(8,128)S(1)}, f32[4,64,640]{2,1,0:T(8,128)S(1)}) custom-call(s32[4]{0:T(128)S(1)} %pad_add_fusion.pos_ref, bf16[256,256]{1,0:T(8,128)(2,1)S(1)} %get-tuple-element.67.mine_ref, f32[256,256]{1,0:T(8,128)S(1)} %collective-permute-done.3.peer_ref, ...), custom_call_target="tpu_custom_call" | custom-call | flops 4000000000 | bytes 6946832 | tf_op jit(solution)/shard_map/partial_grad/pallas_call | solution.py:309
  71.5 3.1 %collective-permute-start.6 = (f32[4,64,640]{2,1,0:T(8,128)S(1)}, f32[4,64,640]{2,1,0:T(8,128)S(1)}, u32[]{:S(2)}, u32[]{:S(2)}) collective-permute-start(f32[4,64,640]{2,1,0:T(8,128)S(1)} %get-tuple-element.71), channel_id=1, source_target_pairs={{0,2},{1,3},{2,0},{3,1},{4,20},{5,21},{6,22},{7,23},{8,10},{9,11},... | collective-permute-start | bytes 1966088 | tf_op jit(solution)/shard_map/ppermute | solution.py:43
  74.6 1.1 collective-permute-start.7
  75.8 0.9 collective-permute-start.5
  76.7 0.1 scan_backward.1
  76.7 14.0 %all_to_all.21.got_ref = f32[32,8,128]{2,1,0:T(8,128)S(1)} all-to-all(f32[32,8,128]{2,1,0:T(8,128)S(1)} %scan_backward.1), channel_id=1, replica_groups={{0,8,16,24,32,40,48,56,64,72,80,88,96,104,112,120,128,136,144,152,160,1..., dimensions={0} | all-to-all | bytes 262144 | tf_op jit(solution)/shard_map/all_to_all | solution.py:329
  90.7 0.2 collective-permute-done.7
  90.9 0.2 add_add_fusion
  91.1 1.2 collective-permute-start.9
  92.3 2.1 %collective-permute-start.11 = (f32[64,640]{1,0:T(8,128)S(1)}, f32[64,640]{1,0:T(8,128)S(1)}, u32[]{:S(2)}, u32[]{:S(2)}) collective-permute-start(f32[64,640]{1,0:T(8,128)S(1)} %get-tuple-element.92), channel_id=1, source_target_pairs={{0,24},{1,25},{2,26},{3,27},{4,7},{5,4},{6,5},{7,6},{8,0},{9,1},{1... | collective-permute-start | bytes 491528 | tf_op jit(solution)/shard_map/ppermute | solution.py:43
  94.4 3.6 %collective-permute-done.9 = f32[64,640]{1,0:T(8,128)S(1)} collective-permute-done((f32[64,640]{1,0:T(8,128)S(1)}, f32[64,640]{1,0:T(8,128)S(1)}, u32[]{:S(2)}, u32[]{:S(2)}) %collective-permute-start.9) | collective-permute-done | bytes 163872 | tf_op jit(solution)/shard_map/ppermute | solution.py:43
  98.0 0.4 collective-permute-done.11
  98.4 2.6 %collective-permute-done.10 = f32[64,640]{1,0:T(8,128)S(1)} collective-permute-done((f32[64,640]{1,0:T(8,128)S(1)}, f32[64,640]{1,0:T(8,128)S(1)}, u32[]{:S(2)}, u32[]{:S(2)}) %collective-permute-start.10) | collective-permute-done | bytes 163872 | tf_op jit(solution)/shard_map/ppermute | solution.py:43
  101.0 0.7 fusion.3
  101.7 3.9 %all-to-all-start.3 = ((f32[8,8,640]{2,1,0:T(8,128)}), f32[8,8,640]{2,1,0:T(8,128)S(1)}, u32[]{:S(2)}, u32[]{:S(2)}) async-start(f32[8,8,640]{2,1,0:T(8,128)} %fusion.3), calls=%async_computation.3 | async-start | bytes 327680 | tf_op jit(solution)/shard_map/all_to_all | solution.py:329
  105.6 0.6 core_backward.1
  106.2 0.1 collective-permute-start.8
  106.3 7.9 %all-to-all-done.3 = f32[8,8,640]{2,1,0:T(8,128)S(1)} async-done(((f32[8,8,640]{2,1,0:T(8,128)}), f32[8,8,640]{2,1,0:T(8,128)S(1)}, u32[]{:S(2)}, u32[]{:S(2)}) %all-to-all-start.3) | async-done | bytes 163872 | tf_op jit(solution)/shard_map/all_to_all | solution.py:329
  114.2 2.0 %collective-permute-start.14 = (f32[8,640]{1,0:T(8,128)S(1)}, f32[8,640]{1,0:T(8,128)S(1)}, u32[]{:S(2)}, u32[]{:S(2)}) collective-permute-start(f32[8,640]{1,0:T(8,128)S(1)} %reduce_sum.9.r0_ref), channel_id=1, source_target_pairs={{0,3},{1,0},{2,1},{3,2},{4,7},{5,4},{6,5},{7,6},{8,11},{9,8},{10,9... | collective-permute-start | bytes 61448 | tf_op jit(solution)/shard_map/ppermute | solution.py:43
  116.2 0.9 collective-permute-start.13
  117.1 0.8 collective-permute-start.12
  117.9 1.6 %other_grads.1 = (bf16[256,512]{1,0:T(8,128)(2,1)}, bf16[256,128]{1,0:T(8,128)(2,1)}, bf16[256,128]{1,0:T(8,128)(2,1)}) custom-call(s32[4]{0:T(128)S(1)} %pad_add_fusion.pos_ref, f32[256,128]{1,0:T(8,128)S(1)} %get-tuple-element.62.carry_ref, f32[256,128]{1,0:T(8,128)S(1)} %collective-permute-done.2.recv_ref, f32[256,128]{1,0:T(8,128)S(1)} %get-tuple-element.76.after_ref, ...), custom_call_target="tpu_custom_call" | custom-call | flops 2000000000 | bytes 2818064 | tf_op jit(solution)/shard_map/other_grads/pallas_call | solution.py:309
  119.5 2.0 %collective-permute-done.13.r2_ref = f32[8,640]{1,0:T(8,128)S(1)} collective-permute-done((f32[8,640]{1,0:T(8,128)S(1)}, f32[8,640]{1,0:T(8,128)S(1)}, u32[]{:S(2)}, u32[]{:S(2)}) %collective-permute-start.13) | collective-permute-done | bytes 20512 | tf_op jit(solution)/shard_map/ppermute | solution.py:43
  121.5 0.6 collective-permute-done.12.r1_ref
  122.0 1.2 place.1
  (63 shorter events, 0.2 us)
Async XLA Ops:
  0.7 1.0 copy-start.2
  1.7 0.8 copy-start.4
  2.5 0.7 copy-start.6
  3.2 0.7 copy-start.8
  6.0 0.7 copy-start.23
  6.7 0.7 copy-start.34
  7.4 14.1 %copy-start.21 = (f32[256,128]{1,0:T(8,128)}, f32[256,128]{1,0:T(8,128)S(1)}, u32[]{:S(2)}) copy-start(f32[256,128]{1,0:T(8,128)S(1)} %get-tuple-element.48.mine_ref) | copy-start | bytes 393220
  7.4 14.1 %copy-start.27 = (f32[256,512]{1,0:T(8,128)}, f32[256,512]{1,0:T(8,128)S(1)}, u32[]{:S(2)}) copy-start(f32[256,512]{1,0:T(8,128)S(1)} %get-tuple-element.52.cum_ref) | copy-start | bytes 1572868
  7.4 14.1 %copy-start.3 = (bf16[1,256,128]{2,1,0:T(8,128)(2,1)S(1)}, bf16[1,256,128]{2,1,0:T(8,128)(2,1)}, u32[]{:S(2)}) copy-start(bf16[1,256,128]{2,1,0:T(8,128)(2,1)} %param.9) | copy-start | bytes 196612
  7.4 14.1 %copy-start.7 = (s32[1,8,256]{2,1,0:T(8,128)S(1)}, s32[1,8,256]{2,1,0:T(8,128)}, u32[]{:S(2)}) copy-start(s32[1,8,256]{2,1,0:T(8,128)} %param.10) | copy-start | bytes 24580
  7.4 14.1 %copy-start.9 = (f32[8]{0:T(128)S(1)}, f32[8]{0:T(128)}, u32[]{:S(2)}) copy-start(f32[8]{0:T(128)} %rate_ref.5) | copy-start | bytes 100
  7.4 1.4 %collective-permute-start = (f32[264,128]{1,0:T(8,128)S(1)}, f32[264,128]{1,0:T(8,128)S(1)}, u32[]{:S(2)}, u32[]{:S(2)}) collective-permute-start(f32[264,128]{1,0:T(8,128)S(1)} %get-tuple-element.49), channel_id=1, source_target_pairs={{0,4},{1,5},{2,6},{3,7},{4,0},{5,1},{6,2},{7,3},{8,12},{9,13},{10,... | collective-permute-start | bytes 405512 | tf_op jit(solution)/shard_map/ppermute | solution.py:43
  10.2 26.3 %all-to-all-start = ((f32[32,16,128]{2,1,0:T(8,128)}), f32[32,16,128]{2,1,0:T(8,128)S(1)}, u32[]{:S(2)}, u32[]{:S(2)}) async-start(f32[32,16,128]{2,1,0:T(8,128)} %chip_forward.1), calls=%async_computation | async-start | bytes 524288 | tf_op jit(solution)/shard_map/all_to_all | solution.py:329
  21.6 1.3 %copy-start = (bf16[1,256,2560]{2,1,0:T(8,128)(2,1)S(1)}, bf16[1,256,2560]{2,1,0:T(8,128)(2,1)}, u32[]{:S(2)}) copy-start(bf16[1,256,2560]{2,1,0:T(8,128)(2,1)} %param.13) | copy-start | bytes 3932164
  22.9 1.0 copy-start.28
  24.0 4.7 %copy-start.5 = (bf16[1,256,128]{2,1,0:T(8,128)(2,1)S(1)}, bf16[1,256,128]{2,1,0:T(8,128)(2,1)}, u32[]{:S(2)}) copy-start(bf16[1,256,128]{2,1,0:T(8,128)(2,1)} %param.8) | copy-start | bytes 196612
  24.0 4.7 %copy-start.29 = (f32[256,512]{1,0:T(8,128)S(1)}, f32[256,512]{1,0:T(8,128)}, u32[]{:S(2)}) copy-start(f32[256,512]{1,0:T(8,128)} %copy-done.27) | copy-start | bytes 1572868
  24.0 4.7 %copy-start.35 = (bf16[256,512]{1,0:T(8,128)(2,1)S(1)}, bf16[256,512]{1,0:T(8,128)(2,1)}, u32[]{:S(2)}) copy-start(bf16[256,512]{1,0:T(8,128)(2,1)} %copy-done.34) | copy-start | bytes 786436
  27.2 0.7 copy-start.14
  27.9 0.7 copy-start.25
  28.6 7.8 %collective-permute-start.1 = (f32[256,128]{1,0:T(8,128)S(1)}, f32[256,128]{1,0:T(8,128)S(1)}, u32[]{:S(2)}, u32[]{:S(2)}) collective-permute-start(f32[256,128]{1,0:T(8,128)S(1)} %get-tuple-element.54), channel_id=1, source_target_pairs={{0,4},{1,5},{2,6},{3,7},{4,0},{5,1},{6,2},{7,3},{8,12},{9,13},{10,... | collective-permute-start | bytes 393224 | tf_op jit(solution)/shard_map/ppermute | solution.py:43
  31.9 0.8 copy-start.10
  32.7 0.8 copy-start.12
  33.5 0.8 copy-start.17
  34.3 0.8 copy-start.19
  35.1 0.7 copy-start.30
  35.8 0.7 copy-start.32
  36.4 30.2 %collective-permute-start.4 = (f32[256,2560]{1,0:T(8,128)S(1)}, f32[256,2560]{1,0:T(8,128)S(1)}, u32[]{:S(2)}, u32[]{:S(2)}) collective-permute-start(f32[256,2560]{1,0:T(8,128)S(1)} %get-tuple-element.69), channel_id=1, source_target_pairs={{0,4},{1,5},{2,6},{3,7},{4,0},{5,1},{6,2},{7,3},{8,12},{9,13},{10,... | collective-permute-start | bytes 7864328 | tf_op jit(solution)/shard_map/ppermute | solution.py:43
  36.9 0.9 copy-start.15
  38.5 25.0 %copy-start.18 = (f32[256,512]{1,0:T(8,128)S(1)}, f32[256,512]{1,0:T(8,128)}, u32[]{:S(2)}) copy-start(f32[256,512]{1,0:T(8,128)} %copy-done.17) | copy-start | bytes 1572868
  38.5 25.0 %copy-start.20 = (f32[256,512]{1,0:T(8,128)S(1)}, f32[256,512]{1,0:T(8,128)}, u32[]{:S(2)}) copy-start(f32[256,512]{1,0:T(8,128)} %copy-done.19) | copy-start | bytes 1572868
  60.5 0.9 copy-start.22
  62.0 1.4 %collective-permute-start.2 = (f32[256,128]{1,0:T(8,128)S(1)}, f32[256,128]{1,0:T(8,128)S(1)}, u32[]{:S(2)}, u32[]{:S(2)}) collective-permute-start(f32[256,128]{1,0:T(8,128)S(1)} %get-tuple-element.63), channel_id=1, source_target_pairs={{0,4},{1,5},{2,6},{3,7},{4,0},{5,1},{6,2},{7,3},{8,12},{9,13},{10,... | collective-permute-start | bytes 393224 | tf_op jit(solution)/shard_map/ppermute | solution.py:43
  63.5 4.6 %copy-start.1 = (bf16[1,256,2560]{2,1,0:T(8,128)(2,1)S(1)}, bf16[1,256,2560]{2,1,0:T(8,128)(2,1)}, u32[]{:S(2)}) copy-start(bf16[1,256,2560]{2,1,0:T(8,128)(2,1)} %param.13) | copy-start | bytes 3932164
  65.1 1.5 %collective-permute-start.3 = (f32[256,256]{1,0:T(8,128)S(1)}, f32[256,256]{1,0:T(8,128)S(1)}, u32[]{:S(2)}, u32[]{:S(2)}) collective-permute-start(f32[256,256]{1,0:T(8,128)S(1)} %get-tuple-element.68), channel_id=1, source_target_pairs={{0,4},{1,5},{2,6},{3,7},{4,0},{5,1},{6,2},{7,3},{8,12},{9,13},{10,... | collective-permute-start | bytes 786440 | tf_op jit(solution)/shard_map/ppermute | solution.py:43
  66.6 1.5 %copy-start.36 = (f32[256,2560]{1,0:T(8,128)}, f32[256,2560]{1,0:T(8,128)S(1)}, u32[]{:S(2)}) copy-start(f32[256,2560]{1,0:T(8,128)S(1)} %collective-permute-done.4.gp_ref) | copy-start | bytes 7864324
  71.5 19.2 %collective-permute-start.6 = (f32[4,64,640]{2,1,0:T(8,128)S(1)}, f32[4,64,640]{2,1,0:T(8,128)S(1)}, u32[]{:S(2)}, u32[]{:S(2)}) collective-permute-start(f32[4,64,640]{2,1,0:T(8,128)S(1)} %get-tuple-element.71), channel_id=1, source_target_pairs={{0,2},{1,3},{2,0},{3,1},{4,20},{5,21},{6,22},{7,23},{8,10},{9,11},... | collective-permute-start | bytes 1966088 | tf_op jit(solution)/shard_map/ppermute | solution.py:43
  74.6 16.2 %collective-permute-start.7 = (f32[4,64,640]{2,1,0:T(8,128)S(1)}, f32[4,64,640]{2,1,0:T(8,128)S(1)}, u32[]{:S(2)}, u32[]{:S(2)}) collective-permute-start(f32[4,64,640]{2,1,0:T(8,128)S(1)} %get-tuple-element.72), channel_id=1, source_target_pairs={{0,3},{1,0},{2,1},{3,2},{4,28},{5,29},{6,30},{7,31},{8,11},{9,8},{... | collective-permute-start | bytes 1966088 | tf_op jit(solution)/shard_map/ppermute | solution.py:43
  75.8 15.1 %collective-permute-start.5 = (f32[4,64,640]{2,1,0:T(8,128)S(1)}, f32[4,64,640]{2,1,0:T(8,128)S(1)}, u32[]{:S(2)}, u32[]{:S(2)}) collective-permute-start(f32[4,64,640]{2,1,0:T(8,128)S(1)} %get-tuple-element.70), channel_id=1, source_target_pairs={{0,1},{1,2},{2,3},{3,0},{4,12},{5,13},{6,14},{7,15},{8,9},{9,10},{... | collective-permute-start | bytes 1966088 | tf_op jit(solution)/shard_map/ppermute | solution.py:43
  90.9 14.7 %copy-start.16 = (f32[256,128]{1,0:T(8,128)S(1)}, f32[256,128]{1,0:T(8,128)}, u32[]{:S(2)}) copy-start(f32[256,128]{1,0:T(8,128)} %copy-done.14) | copy-start | bytes 393220
  91.1 26.8 %copy-start.11 = (f32[256,512]{1,0:T(8,128)S(1)}, f32[256,512]{1,0:T(8,128)}, u32[]{:S(2)}) copy-start(f32[256,512]{1,0:T(8,128)} %copy-done.10) | copy-start | bytes 1572868
  91.1 26.8 %copy-start.13 = (f32[256,512]{1,0:T(8,128)S(1)}, f32[256,512]{1,0:T(8,128)}, u32[]{:S(2)}) copy-start(f32[256,512]{1,0:T(8,128)} %copy-done.12) | copy-start | bytes 1572868
  91.1 26.8 %copy-start.24 = (bf16[256,512]{1,0:T(8,128)(2,1)S(1)}, bf16[256,512]{1,0:T(8,128)(2,1)}, u32[]{:S(2)}) copy-start(bf16[256,512]{1,0:T(8,128)(2,1)} %copy-done.23) | copy-start | bytes 786436
  91.1 26.8 %copy-start.26 = (bf16[256,512]{1,0:T(8,128)(2,1)S(1)}, bf16[256,512]{1,0:T(8,128)(2,1)}, u32[]{:S(2)}) copy-start(bf16[256,512]{1,0:T(8,128)(2,1)} %copy-done.25) | copy-start | bytes 786436
  91.1 26.8 %copy-start.31 = (f32[256,128]{1,0:T(8,128)S(1)}, f32[256,128]{1,0:T(8,128)}, u32[]{:S(2)}) copy-start(f32[256,128]{1,0:T(8,128)} %copy-done.30) | copy-start | bytes 393220
  91.1 26.8 %copy-start.33 = (f32[256,128]{1,0:T(8,128)S(1)}, f32[256,128]{1,0:T(8,128)}, u32[]{:S(2)}) copy-start(f32[256,128]{1,0:T(8,128)} %copy-done.32) | copy-start | bytes 393220
  91.1 6.9 %collective-permute-start.9 = (f32[64,640]{1,0:T(8,128)S(1)}, f32[64,640]{1,0:T(8,128)S(1)}, u32[]{:S(2)}, u32[]{:S(2)}) collective-permute-start(f32[64,640]{1,0:T(8,128)S(1)} %get-tuple-element.91), channel_id=1, source_target_pairs={{0,16},{1,17},{2,18},{3,19},{4,6},{5,7},{6,4},{7,5},{8,24},{9,25},... | collective-permute-start | bytes 491528 | tf_op jit(solution)/shard_map/ppermute | solution.py:43
  92.3 6.0 %collective-permute-start.11 = (f32[64,640]{1,0:T(8,128)S(1)}, f32[64,640]{1,0:T(8,128)S(1)}, u32[]{:S(2)}, u32[]{:S(2)}) collective-permute-start(f32[64,640]{1,0:T(8,128)S(1)} %get-tuple-element.92), channel_id=1, source_target_pairs={{0,24},{1,25},{2,26},{3,27},{4,7},{5,4},{6,5},{7,6},{8,0},{9,1},{1... | collective-permute-start | bytes 491528 | tf_op jit(solution)/shard_map/ppermute | solution.py:43
  94.4 6.5 %collective-permute-start.10 = (f32[64,640]{1,0:T(8,128)S(1)}, f32[64,640]{1,0:T(8,128)S(1)}, u32[]{:S(2)}, u32[]{:S(2)}) collective-permute-start(f32[64,640]{1,0:T(8,128)S(1)} %get-tuple-element.93), channel_id=1, source_target_pairs={{0,8},{1,9},{2,10},{3,11},{4,5},{5,6},{6,7},{7,4},{8,16},{9,17},{1... | collective-permute-start | bytes 491528 | tf_op jit(solution)/shard_map/ppermute | solution.py:43
  101.7 12.5 %all-to-all-start.3 = ((f32[8,8,640]{2,1,0:T(8,128)}), f32[8,8,640]{2,1,0:T(8,128)S(1)}, u32[]{:S(2)}, u32[]{:S(2)}) async-start(f32[8,8,640]{2,1,0:T(8,128)} %fusion.3), calls=%async_computation.3 | async-start | bytes 327680 | tf_op jit(solution)/shard_map/all_to_all | solution.py:329
  106.2 11.7 %collective-permute-start.8 = (f32[256,128]{1,0:T(8,128)S(1)}, f32[256,128]{1,0:T(8,128)S(1)}, u32[]{:S(2)}, u32[]{:S(2)}) collective-permute-start(f32[256,128]{1,0:T(8,128)S(1)} %get-tuple-element.77), channel_id=1, source_target_pairs={{0,4},{1,5},{2,6},{3,7},{4,0},{5,1},{6,2},{7,3},{8,12},{9,13},{10,... | collective-permute-start | bytes 393224 | tf_op jit(solution)/shard_map/ppermute | solution.py:43
  114.2 5.3 %collective-permute-start.14 = (f32[8,640]{1,0:T(8,128)S(1)}, f32[8,640]{1,0:T(8,128)S(1)}, u32[]{:S(2)}, u32[]{:S(2)}) collective-permute-start(f32[8,640]{1,0:T(8,128)S(1)} %reduce_sum.9.r0_ref), channel_id=1, source_target_pairs={{0,3},{1,0},{2,1},{3,2},{4,7},{5,4},{6,5},{7,6},{8,11},{9,8},{10,9... | collective-permute-start | bytes 61448 | tf_op jit(solution)/shard_map/ppermute | solution.py:43
  116.2 5.3 %collective-permute-start.13 = (f32[8,640]{1,0:T(8,128)S(1)}, f32[8,640]{1,0:T(8,128)S(1)}, u32[]{:S(2)}, u32[]{:S(2)}) collective-permute-start(f32[8,640]{1,0:T(8,128)S(1)} %reduce_sum.9.r0_ref), channel_id=1, source_target_pairs={{0,2},{1,3},{2,0},{3,1},{4,6},{5,7},{6,4},{7,5},{8,10},{9,11},{10,... | collective-permute-start | bytes 61448 | tf_op jit(solution)/shard_map/ppermute | solution.py:43
  117.1 5.0 %collective-permute-start.12 = (f32[8,640]{1,0:T(8,128)S(1)}, f32[8,640]{1,0:T(8,128)S(1)}, u32[]{:S(2)}, u32[]{:S(2)}) collective-permute-start(f32[8,640]{1,0:T(8,128)S(1)} %reduce_sum.9.r0_ref), channel_id=1, source_target_pairs={{0,1},{1,2},{2,3},{3,0},{4,5},{5,6},{6,7},{7,4},{8,9},{9,10},{10,1... | collective-permute-start | bytes 61448 | tf_op jit(solution)/shard_map/ppermute | solution.py:43

commit v3 on v2

v3 whole, which is shorter than its diff:
```python
import jax
import jax.numpy as jnp
from jax import lax
from jax.experimental import pallas as pl
from jax.experimental.pallas import tpu as pltpu
from jax.sharding import PartitionSpec as P

HEAD_DIM = 64
STATE = 128
HEADS = 8
TOK = 256
CH = HEADS * HEAD_DIM
D = 2560
NX, NY, NZ = 4, 4, 8
CHIPS = NY * NZ
HALF = CH // 2
PIECE = HALF // CHIPS
BLK = D // NX
BOTH = ("seq", "dp")

f32, bf16 = jnp.float32, jnp.bfloat16
RATE_UNIT = 1.0 / (8.0 * TOK * 64)
HI = lax.Precision.HIGHEST
NT = (((1,), (1,)), ((), ()))
TN = (((0,), (0,)), ((), ()))
NN = (((1,), (0,)), ((), ()))


def mm(a, b, dims):
    return lax.dot_general(a, b, dims, preferred_element_type=f32)


def permute(v, target):
    pairs = []
    for z in range(NZ):
        for y in range(NY):
            for c in range(2):
                for x in range(NX):
                    tz, ty, tc, tx = target(z, y, c, x)
                    src = ((z * NY + y) * 2 + c) * NX + x
                    dst = ((tz * NY + ty) * 2 + tc) * NX + tx
                    pairs.append((src, dst))
    return lax.ppermute(v, BOTH, pairs)


def swap_core(z, y, c, x):
    return z, y, 1 - c, x


def first_axis(k):
    return lambda z, y, c, x: (z, y, c, (x + k) % NX) if c == 0 else (z, (y + k) % NY, c, x)


def second_axis(k):
    return lambda z, y, c, x: (z, (y + k) % NY, c, x) if c == 0 else (z, y, c, (x + k) % NX)


def x_axis(k):
    return lambda z, y, c, x: (z, y, c, (x + k) % NX)


def place_of():
    at = lax.axis_index("seq")
    return at >> 3, (at >> 1) & 3, at & 1, lax.axis_index("dp")


def rate_lanes(rate_ref, width):
    lane = lax.broadcasted_iota(jnp.int32, (1, width), 1) // (width // HEADS)
    rates = jnp.zeros((1, width), f32)
    for h in range(HEADS):
        rates = jnp.where(lane == h, rate_ref[h] * RATE_UNIT, rates)
    return rates


def signed_tri():
    t = lax.broadcasted_iota(jnp.int32, (TOK, TOK), 0)
    s = lax.broadcasted_iota(jnp.int32, (TOK, TOK), 1)
    half = TOK // 2
    plus = (s >= half) & (s <= t)
    minus = (s < half) & (s > t)
    return jnp.where(plus, 1.0, jnp.where(minus, -1.0, 0.0)).astype(f32)


def step_lanes(cum, dt_lanes):
    ones = jnp.ones((8, TOK // 2), f32)
    start = -lax.dot_general(ones, dt_lanes[:, : TOK // 2], NT, precision=HI, preferred_element_type=f32)[:1]
    row = lax.broadcasted_iota(jnp.int32, (TOK, CH), 0)
    return jnp.where(row == 0, cum - start, cum - pltpu.roll(cum, 1, 0)), start


def gate(v):
    s = 1.0 - v * (1.0 / 8.0)
    for n in (7.0, 6.0, 5.0, 4.0, 3.0, 2.0):
        s = 1.0 - v * (1.0 / n) * s
    return jnp.sqrt(jnp.where(v < 0.25, v * s, 1.0 - jnp.exp(-v)))


def lanes_of(dt):
    return jnp.broadcast_to(dt[:, None, :], (HEADS, HEAD_DIM, TOK)).reshape(CH, TOK)


def local_forward(rate_ref, dt_ref, x_ref, b_ref, mine_ref, send_ref, tot_ref):
    core = place_of()[2]
    dt = dt_ref[...].astype(f32)
    rate = rate_lanes(rate_ref, CH)
    dt_lanes = lanes_of(dt)
    cum = lax.dot_general(signed_tri(), dt_lanes, NT, precision=HI, preferred_element_type=f32)
    w = gate(step_lanes(cum, dt_lanes)[0] * (2.0 * rate))
    xt = (x_ref[...].astype(f32) * w * jnp.exp((cum - cum[TOK - 1:]) * rate)).astype(bf16)
    own = mm(xt, b_ref[...], TN)
    head = lax.broadcasted_iota(jnp.int32, (HEADS, 1), 0)
    rate_col = jnp.zeros((HEADS, 1), f32)
    for h in range(HEADS):
        rate_col = jnp.where(head == h, rate_ref[h] * RATE_UNIT, rate_col)
    tot = jnp.broadcast_to(-(jnp.sum(dt, axis=1, keepdims=True) * rate_col), (HEADS, STATE))
    tot_ref[...] = tot
    send_ref[HALF:, :] = tot

    @pl.when(core == 0)
    def _():
        mine_ref[...] = own[:HALF]
        send_ref[:HALF, :] = own[HALF:]

    @pl.when(core == 1)
    def _():
        mine_ref[...] = own[HALF:]
        send_ref[:HALF, :] = own[:HALF]


def local_backward(rate_ref, dt_ref, c_ref, g_ref, w_ref, mine_ref, send_ref, gy_ref, wide_ref):
    core = place_of()[2]
    rate = rate_lanes(rate_ref, CH)
    dt_lanes = lanes_of(dt_ref[...].astype(f32))
    cum = lax.dot_general(signed_tri(), dt_lanes, NT, precision=HI, preferred_element_type=f32)
    decay = jnp.exp((step_lanes(cum, dt_lanes)[1] - cum) * rate)
    g = g_ref[...]
    gy = mm(g, w_ref[...], NT).astype(bf16)
    gy_ref[...] = gy
    wide_ref[...] = g.astype(f32)
    adj = mm((gy.astype(f32) * decay).astype(bf16), c_ref[...], TN)

    @pl.when(core == 0)
    def _():
        mine_ref[...] = adj[:HALF]
        send_ref[...] = adj[HALF:]

    @pl.when(core == 1)
    def _():
        mine_ref[...] = adj[HALF:]
        send_ref[...] = adj[:HALF]


def my_heads(core, tots):
    return jnp.where(core == 0, tots[:HEADS // 2], tots[HEADS // 2:])


def decay_rows(tots):
    rows = jnp.exp(tots)
    return jnp.broadcast_to(rows[:, None, :], (HEADS // 2, HEAD_DIM, STATE)).reshape(HALF, STATE)


def chip_forward(mine_ref, peer_ref, tot_ref, out_ref):
    core = place_of()[2]
    own = my_heads(core, tot_ref[...])
    other = my_heads(core, peer_ref[HALF:, :])
    mine, peer = mine_ref[...], peer_ref[:HALF, :]
    second = decay_rows(jnp.where(core == 0, other, own))
    chip = jnp.where(core == 0, mine, peer) * second + jnp.where(core == 0, peer, mine)
    out_ref[:, :PIECE, :] = chip.reshape(CHIPS, PIECE, STATE)
    tots = jnp.broadcast_to((own + other)[:, None, None, :], (HEADS // 2, CHIPS // (HEADS // 2), PIECE, STATE))
    out_ref[:, PIECE:, :] = tots.reshape(CHIPS, PIECE, STATE)


def scan_forward(in_ref, mine_ref, peer_ref, tot_ref, fpeer_ref, out_ref):
    core = place_of()[2]
    first = decay_rows(my_heads(core, jnp.where(core == 0, tot_ref[...], fpeer_ref[HALF:, :])))
    mine, peer = mine_ref[...], peer_ref[...]
    chip = jnp.where(core == 0, mine, peer) + jnp.where(core == 0, peer, mine) * first
    out_ref[:, PIECE:, :] = chip.reshape(CHIPS, PIECE, STATE)
    acc = jnp.zeros((PIECE, STATE), f32)
    for k in range(CHIPS):
        out_ref[k, :PIECE, :] = acc
        acc = acc * jnp.exp(in_ref[k, PIECE:, :]) + in_ref[k, :PIECE, :]


def scan_backward(dec_ref, in_ref, out_ref):
    acc = jnp.zeros((PIECE, STATE), f32)
    for k in range(CHIPS - 1, -1, -1):
        out_ref[k] = acc
        acc = acc * jnp.exp(dec_ref[k, PIECE:, :]) + in_ref[k, PIECE:, :]


def core_forward(got_ref, mine_ref, peer_ref, tot_ref, keep_ref, send_ref):
    core = place_of()[2]
    into = got_ref[:, :PIECE, :].reshape(HALF, STATE)
    first = decay_rows(my_heads(core, jnp.where(core == 0, tot_ref[...], peer_ref[HALF:, :])))
    after = into * first + jnp.where(core == 0, mine_ref[...], peer_ref[:HALF, :])
    keep_ref[...] = jnp.where(core == 0, into, after)
    send_ref[...] = jnp.where(core == 0, after, into)


def core_backward(got_ref, mine_ref, peer_ref, tot_ref, fpeer_ref, keep_ref, send_ref):
    core = place_of()[2]
    after = got_ref[...].reshape(HALF, STATE)
    second = decay_rows(my_heads(core, jnp.where(core == 0, fpeer_ref[HALF:, :], tot_ref[...])))
    into = after * second + jnp.where(core == 0, peer_ref[...], mine_ref[...])
    keep_ref[...] = jnp.where(core == 0, into, after)
    send_ref[...] = jnp.where(core == 0, after, into)


def both_halves(core, keep, recv):
    low = jnp.where(core == 0, keep, recv)
    high = jnp.where(core == 0, recv, keep)
    return jnp.concatenate([low, high], axis=0).astype(bf16)


def head_masks(rate_ref, dt, cum):
    cum_rows = lax.dot_general(dt, signed_tri(), NT, precision=HI, preferred_element_type=f32)
    i = lax.broadcasted_iota(jnp.int32, (TOK, TOK), 0)
    j = lax.broadcasted_iota(jnp.int32, (TOK, TOK), 1)
    for h in range(HEADS):
        gap = cum_rows[h:h + 1, :] - cum[:, h * HEAD_DIM:h * HEAD_DIM + 1]
        mask = jnp.exp(jnp.where(i >= j, gap * (rate_ref[h] * RATE_UNIT), -jnp.inf))
        yield slice(h * HEAD_DIM, (h + 1) * HEAD_DIM), mask


def intra_forward(rate_ref, dt_ref, x_ref, b_ref, c_ref, out_ref):
    dt = dt_ref[...].astype(f32)
    rate = rate_lanes(rate_ref, CH)
    dt_lanes = lanes_of(dt)
    cum = lax.dot_general(signed_tri(), dt_lanes, NT, precision=HI, preferred_element_type=f32)
    steps, start = step_lanes(cum, dt_lanes)
    xw = (x_ref[...].astype(f32) * gate(steps * (2.0 * rate))).astype(bf16)
    scores = mm(c_ref[...], b_ref[...], NT)
    for lanes, mask in head_masks(rate_ref, dt, cum):
        out_ref[:, lanes] = mm((mask * scores).astype(bf16), xw[:, lanes], NN)
    out_ref[:, CH:] = jnp.exp((start - cum) * rate)


def select_rows(core, y_at):
    row = lax.broadcasted_iota(jnp.int32, (CH // 2, CH), 0)
    lane = lax.broadcasted_iota(jnp.int32, (CH // 2, CH), 1)
    y = (y_at + row // 64) % NY
    z = (row // 8) % NZ
    return jnp.where(lane == ((z * NY + y) * 2 + core) * 8 + row % 8, 1.0, 0.0).astype(bf16)


def forward_out(keep_ref, recv_ref, c_ref, y_ref, out_ref, mine_ref, other_ref):
    _, y_at, core, _ = place_of()
    state = both_halves(core, keep_ref[...], recv_ref[...])
    out = (y_ref[:, :CH] + y_ref[:, CH:] * mm(c_ref[...], state, NT)).astype(bf16)
    out_ref[...] = out
    mine_ref[...] = mm(select_rows(core, y_at), out, NT).astype(bf16)
    other_ref[...] = mm(select_rows(1 - core, y_at), out, NT)


def partial_grad(rows_ref, peer_ref, g_ref, gp_ref, s0_ref, s1_ref, s2_ref, s3_ref):
    _, _, core, x_at = place_of()
    outs = (s0_ref, s1_ref, s2_ref, s3_ref)
    mine = rows_ref[...]
    peer = peer_ref[...].astype(bf16)
    for xr in range(NX):
        at = pl.multiple_of(((x_at + xr) % NX) * BLK, 128)
        tile = mm(mine, g_ref[:, pl.ds(at, BLK)], NN)
        tile = tile + mm(peer, gp_ref[:, pl.ds(at, BLK)].astype(bf16), NN)

        @pl.when(core == 0)
        def _():
            for yr in range(NY):
                outs[xr][yr] = tile[yr * 64:(yr + 1) * 64]

        @pl.when(core == 1)
        def _():
            for yr in range(NY):
                outs[yr][xr] = tile[yr * 64:(yr + 1) * 64]


def gradients(rate_ref, dt_ref, x_ref, b_ref, c_ref, gy_ref, keep_ref, recv_ref, after_ref, recv2_ref,
              gi_ref, gwr_ref, grd_ref):
    core = place_of()[2]
    dt = dt_ref[...].astype(f32)
    rate = rate_lanes(rate_ref, CH)
    dt_lanes = lanes_of(dt)
    cum = lax.dot_general(signed_tri(), dt_lanes, NT, precision=HI, preferred_element_type=f32)
    steps, start = step_lanes(cum, dt_lanes)
    w = gate(steps * (2.0 * rate))
    tail = jnp.exp((cum - cum[TOK - 1:]) * rate)
    xw = x_ref[...].astype(f32) * w
    xt = (xw * tail).astype(bf16)
    xw = xw.astype(bf16)
    gy = gy_ref[...]
    gyd = (gy.astype(f32) * jnp.exp((start - cum) * rate)).astype(bf16)
    b = b_ref[...]
    c = c_ref[...]
    scores = mm(c, b, NT)
    state = both_halves(core, keep_ref[...], recv_ref[...])
    adj = both_halves(core, after_ref[...], recv2_ref[...])
    inter = tail * mm(b, adj, NT)
    pairs = jnp.zeros((TOK, TOK), f32)
    for lanes, mask in head_masks(rate_ref, dt, cum):
        intra = mm((mask * scores).astype(bf16), gy[:, lanes], TN)
        gi_ref[:, lanes] = (w[:, lanes] * (intra + inter[:, lanes])).astype(bf16)
        pairs = pairs + mask * mm(gy[:, lanes], xw[:, lanes], NT)
    pairs = pairs.astype(bf16)
    grd_ref[...] = (mm(pairs, b, NN) + mm(gyd, state, NN)).astype(bf16)
    gwr_ref[...] = (mm(pairs, c, TN) + mm(xt, adj, NN)).astype(bf16)


def place(r0_ref, r1_ref, r2_ref, r3_ref, out_ref):
    x_at = place_of()[3]
    for k, ref in enumerate((r0_ref, r1_ref, r2_ref, r3_ref)):
        at = pl.multiple_of(((x_at + NX - k) % NX) * BLK, 128)
        out_ref[:, pl.ds(at, BLK)] = ref[...]


class Fetched:
    def __init__(self, copy, buffer):
        self.copy, self.buffer, self.here = copy, buffer, False

    def wait(self):
        if not self.here:
            self.copy.wait()
            self.here = True

    def __getitem__(self, at):
        self.wait()
        return self.buffer[at]


def call(body, outs, fetch, *args, us=1):
    shapes = [jax.ShapeDtypeStruct(s, d) for s, d in outs]
    moved = sum(a.size * a.dtype.itemsize for a in args) + sum(s.size * s.dtype.itemsize for s in shapes)
    scratch = [(pltpu.SMEM if a.ndim == 1 else pltpu.VMEM)(a.shape, a.dtype) for a in args[:fetch]]
    if fetch:
        scratch.append(pltpu.SemaphoreType.DMA((fetch,)))

    def kernel(*refs):
        left = refs[len(args) + len(outs):]
        held = [Fetched(pltpu.make_async_copy(refs[n], left[n], left[fetch].at[n]), left[n]) for n in range(fetch)]
        for one in held:
            one.copy.start()
        body(*held, *refs[fetch:len(args) + len(outs)])
        for one in held:
            one.wait()

    got = pl.pallas_call(
        kernel,
        out_shape=shapes,
        in_specs=[pl.BlockSpec(memory_space=pltpu.HBM)] * fetch
        + [pl.BlockSpec(memory_space=pltpu.VMEM)] * (len(args) - fetch),
        out_specs=[pl.BlockSpec(memory_space=pltpu.VMEM)] * len(shapes),
        scratch_shapes=scratch,
        cost_estimate=pl.CostEstimate(flops=us * 1_000_000_000, bytes_accessed=moved, transcendentals=0),
        compiler_params=pltpu.CompilerParams(vmem_limit_bytes=(54 << 20) if fetch else (8 << 20)),
        name=body.__name__,
    )(*args)
    return got if len(got) > 1 else got[0]


def shards(inputs, write_vecs, read_vecs, dt_code, a_rate, w_out, grad_out):
    x, b, c, dt, g = inputs[0], write_vecs[0], read_vecs[0], dt_code[0], grad_out[0]
    chips = [[q * 2 + core for q in range(CHIPS)] for core in range(2)]
    depth = [[(z * NY + y) * 2 + core for z in range(NZ)] for y in range(NY) for core in range(2)]

    def over(v, groups):
        return lax.all_to_all(v, "seq", 0, 0, axis_index_groups=groups, tiled=True)

    half = ((HALF, STATE), f32)
    tokens, narrow = ((TOK, CH), bf16), ((TOK, STATE), bf16)
    mine, send, tot = call(local_forward, [half, ((HALF + 8, STATE), f32), ((HEADS, STATE), f32)], 4,
                           a_rate, dt, x, b, us=2)
    peer = permute(send, swap_core)
    chip = call(chip_forward, [((CHIPS, 2 * PIECE, STATE), f32)], 0, mine, peer, tot)
    pieces = over(chip, chips)

    g2, x2 = lax.optimization_barrier((g, x, chip))[:2]
    bmine, bsend, gy, g_wide = call(local_backward, [half, half, tokens, ((TOK, D), f32)], 5,
                                    a_rate, dt, c, g2, w_out, us=4)
    bpeer = permute(bsend, swap_core)
    y_in = call(intra_forward, [((TOK, 2 * CH), f32)], 5, a_rate, dt, x2, b, c, us=3)
    pieces, bpeer, y_in, g_wide = lax.optimization_barrier((pieces, bpeer, y_in, g_wide))
    g_peer = permute(g_wide, swap_core)

    got = over(call(scan_forward, [((CHIPS, 2 * PIECE, STATE), f32)], 0, pieces, bmine, bpeer, tot, peer), chips)
    keep, send = call(core_forward, [half, half], 0, got, mine, peer, tot)
    recv = permute(send, swap_core)
    out, rows, send = call(
        forward_out, [tokens, ((HALF, TOK), bf16), ((HALF, TOK), f32)], 0, keep, recv, c, y_in, us=2)
    s = call(partial_grad, [((NY, 64, BLK), f32)] * 4, 0, rows, permute(send, swap_core), g, g_peer, us=4)

    got2, pieces2 = lax.optimization_barrier((got, pieces, s[1]))[:2]
    back = over(call(scan_backward, [((CHIPS, PIECE, STATE), f32)], 0, pieces2, got2), chips)
    s1, s2, s3 = permute(s[1], first_axis(1)), permute(s[2], first_axis(2)), permute(s[3], first_axis(3))
    s1, s2, s3, back = lax.optimization_barrier((s1, s2, s3, back))
    s = s[0] + s2 + s1 + s3
    after, send = call(core_backward, [half, half], 0, back, bmine, bpeer, tot, peer)
    recv2 = permute(send, swap_core)
    s = s[0] + permute(s[2], second_axis(2)) + permute(s[1], second_axis(1)) + permute(s[3], second_axis(3))
    s = over(s.reshape(NZ, 8, BLK), depth)
    gi, gwr, grd = call(gradients, [tokens, narrow, narrow], 5, a_rate, dt, x2, b, c, gy, keep, recv, after, recv2, us=5)
    s, gi = lax.optimization_barrier((s, gi))
    s = jnp.sum(s, axis=0)
    grad_w_out = call(place, [((8, D), f32)], 0, s, permute(s, x_axis(1)), permute(s, x_axis(2)), permute(s, x_axis(3)))
    return out[None], gi[None], gwr[None], grd[None], grad_w_out


def solution(mesh):
    rows = P("dp", "seq", None)
    return jax.shard_map(
        shards,
        mesh=mesh,
        in_specs=(rows, rows, rows, P("dp", None, "seq"), P(), P(), rows),
        out_specs=(rows, rows, rows, rows, P("seq", None)),
        check_vma=False,
    )
```

time: 124 us -> 110 us (0.89)
  local copies, waits for them, and re-layouts: 16.2 us -> 2.95 us
  Pallas kernels: 19.6 us -> 23.8 us
  waiting for transfers between devices: 21.2 us -> 17 us
  blocking collectives: 36 us -> 34.3 us
    unnamed x74 -> x26, local copies, waits for them, and re-layouts: 16.2 us -> 2.92 us
    pallas_call x12, Pallas kernels: 19.6 us -> 23.8 us  [call(): pl.pallas_call(kernel, out_shape=shapes, in_specs=[pl.BlockSpec(memory_sp...]
    all_to_all x2, waiting for transfers between devices: 7.93 us -> 3.94 us  [over(): return lax.all_to_all(v, 'seq', 0, 0, axis_index_groups=groups, tiled=True)]
    all_to_all x2, blocking collectives: 36 us -> 34.3 us  [over(): return lax.all_to_all(v, 'seq', 0, 0, axis_index_groups=groups, tiled=True)]
  transfers between devices with their start and end apart: 17 -> 17, of which waited for: 10 -> 12; matrix products, arithmetic and copies ran while one was open for 0% -> 1% of each run, Pallas kernels for 9% -> 16%
where the time goes in v3:
time: 110 us; the launch traced here: 109 us
  blocking collectives  34.3 us (31%)
  starting transfers between devices  29.4 us (27%)
  Pallas kernels  23.8 us (22%)
  waiting for transfers between devices  17 us (15%)
  local copies, waits for them, and re-layouts  2.95 us (3%)
    all_to_all x2, blocking collectives, over(): return lax.all_to_all(v, 'seq', 0, 0, axis_index_groups=groups, tiled=True)  34.3 us
    pallas_call x12, Pallas kernels, call(): pl.pallas_call(kernel, out_shape=shapes, in_specs=[pl.BlockSpec(memory_sp...  23.8 us
    all_to_all x2, starting transfers between devices, over(): return lax.all_to_all(v, 'seq', 0, 0, axis_index_groups=groups, tiled=True)  15.3 us
    ppermute x15, starting transfers between devices, permute(): return lax.ppermute(v, BOTH, pairs)  14.1 us
    ppermute x15, waiting for transfers between devices, permute(): return lax.ppermute(v, BOTH, pairs)  13.1 us
    all_to_all x2, waiting for transfers between devices, over(): return lax.all_to_all(v, 'seq', 0, 0, axis_index_groups=groups, tiled=True)  3.94 us
    unnamed x26, local copies, waits for them, and re-layouts  2.92 us
  transfers between devices with their start and end apart: 17, of which 12 were waited for; matrix products, arithmetic and copies ran while one was open for 1% of the time, Pallas kernels for 16%

profile of v3, /device:TPU:32, one launch (start us, length us, event | category | flops | bytes accessed | tf_op | source)
XLA Modules:
  0.0 109.2 jit_solution(10678436522884956897)
XLA Ops:
  0.6 3.1 %local_forward.1 = (f32[256,128]{1,0:T(8,128)}, f32[264,128]{1,0:T(8,128)}, f32[8,128]{1,0:T(8,128)}) custom-call(f32[8]{0:T(128)} %refs_0_.7, s32[8,256]{1,0:T(8,128)} %bitcast.39, bf16[256,512]{1,0:T(8,128)(2,1)} %bitcast.33, bf16[256,128]{1,0:T(8,128)(2,1)} %bitcast.36), custom_call_target="tpu_custom_call" | custom-call | flops 2000000000 | bytes 606240 | tf_op jit(solution)/shard_map/local_forward/pallas_call | solution.py:346
  3.8 0.1 collective-permute-start
  3.9 1.6 %collective-permute-done.refs_1_.refs_4_.refs_2_ = f32[264,128]{1,0:T(8,128)S(1)} collective-permute-done((f32[264,128]{1,0:T(8,128)}, f32[264,128]{1,0:T(8,128)S(1)}, u32[]{:S(2)}, u32[]{:S(2)}) %collective-permute-start) | collective-permute-done | bytes 135200 | tf_op jit(solution)/shard_map/ppermute | solution.py:43
  5.4 0.9 copy-done.6
  6.3 0.7 copy-done.9
  7.0 0.7 chip_forward.1
  7.7 11.4 %all-to-all-start = ((f32[32,16,128]{2,1,0:T(8,128)}), f32[32,16,128]{2,1,0:T(8,128)S(1)}, u32[]{:S(2)}, u32[]{:S(2)}) async-start(f32[32,16,128]{2,1,0:T(8,128)} %chip_forward.1), calls=%async_computation | async-start | bytes 524288 | tf_op jit(solution)/shard_map/all_to_all | solution.py:366
  19.1 5.2 %local_backward.1 = (f32[256,128]{1,0:T(8,128)}, f32[256,128]{1,0:T(8,128)}, bf16[256,512]{1,0:T(8,128)(2,1)}, f32[256,2560]{1,0:T(8,128)}) custom-call(f32[8]{0:T(128)} %refs_0_.7, s32[8,256]{1,0:T(8,128)} %bitcast.40, bf16[256,128]{1,0:T(8,128)(2,1)} %bitcast.29, bf16[256,2560]{1,0:T(8,128)(2,1)} %bitcast.27, bf16[512,2560]{1,0:T(8,128)(2,1)} %refs_4_.1), custom_call_target="tpu_custom_call" | custom-call | flops 4000000000 | bytes 7151648 | tf_op jit(solution)/shard_map/local_backward/pallas_call | solution.py:346
  24.3 0.0 copy-start.11
  24.3 0.0 copy-start.4
  24.3 0.0 copy-start.10
  24.3 0.1 collective-permute-start.1
  24.4 4.9 %intra_forward.1.refs_3_ = f32[256,1024]{1,0:T(8,128)} custom-call(f32[8]{0:T(128)} %refs_0_.7, s32[8,256]{1,0:T(8,128)} %bitcast.41, bf16[256,512]{1,0:T(8,128)(2,1)} %bitcast.34, bf16[256,128]{1,0:T(8,128)(2,1)} %bitcast.37, bf16[256,128]{1,0:T(8,128)(2,1)} %bitcast.30), custom_call_target="tpu_custom_call" | custom-call | flops 3000000000 | bytes 1450016 | tf_op jit(solution)/shard_map/intra_forward/pallas_call | solution.py:346
  29.3 0.0 copy-start.7
  29.3 0.0 collective-permute-done.1.refs_2_
  29.3 2.2 %all-to-all-done.refs_0_ = f32[32,16,128]{2,1,0:T(8,128)S(1)} async-done(((f32[32,16,128]{2,1,0:T(8,128)}), f32[32,16,128]{2,1,0:T(8,128)S(1)}, u32[]{:S(2)}, u32[]{:S(2)}) %all-to-all-start) | async-done | bytes 262176 | tf_op jit(solution)/shard_map/all_to_all | solution.py:366
  31.6 0.0 copy-done.11
  31.6 0.0 collective-permute-start.4
  31.6 0.0 copy-done.4
  31.6 0.0 copy-done.10
  31.6 0.1 scan_forward.1
  31.7 0.0 copy-start.3
  31.7 20.4 %all_to_all.20.refs_0_.refs_1_ = f32[32,16,128]{2,1,0:T(8,128)S(1)} all-to-all(f32[32,16,128]{2,1,0:T(8,128)S(1)} %scan_forward.1), channel_id=1, replica_groups={{0,8,16,24,32,40,48,56,64,72,80,88,96,104,112,120,128,136,144,152,160,1..., dimensions={0} | all-to-all | bytes 524288 | tf_op jit(solution)/shard_map/all_to_all | solution.py:366
  52.1 0.0 copy-done.7
  52.2 0.0 copy-start.5
  52.2 0.1 collective-permute-start.2
  52.3 1.3 %collective-permute-done.2.refs_1_.refs_7_ = f32[256,128]{1,0:T(8,128)S(1)} collective-permute-done((f32[256,128]{1,0:T(8,128)S(1)}, f32[256,128]{1,0:T(8,128)S(1)}, u32[]{:S(2)}, u32[]{:S(2)}) %collective-permute-start.2) | collective-permute-done | bytes 131104 | tf_op jit(solution)/shard_map/ppermute | solution.py:43
  53.6 0.0 copy-done.2
  53.6 0.0 copy-done.3
  53.6 1.1 forward_out.1
  54.7 0.1 collective-permute-start.3
  54.9 1.4 %collective-permute-done.3.refs_1_ = f32[256,256]{1,0:T(8,128)S(1)} collective-permute-done((f32[256,256]{1,0:T(8,128)S(1)}, f32[256,256]{1,0:T(8,128)S(1)}, u32[]{:S(2)}, u32[]{:S(2)}) %collective-permute-start.3) | collective-permute-done | bytes 262176 | tf_op jit(solution)/shard_map/ppermute | solution.py:43
  56.2 0.0 collective-permute-done.4.refs_3_
  56.3 1.7 %partial_grad.1 = (f32[4,64,640]{2,1,0:T(8,128)S(1)}, f32[4,64,640]{2,1,0:T(8,128)S(1)}, f32[4,64,640]{2,1,0:T(8,128)S(1)}, f32[4,64,640]{2,1,0:T(8,128)S(1)}) custom-call(bf16[256,256]{1,0:T(8,128)(2,1)S(1)} %get-tuple-element.54.refs_0_, f32[256,256]{1,0:T(8,128)S(1)} %collective-permute-done.3.refs_1_, bf16[256,2560]{1,0:T(8,128)(2,1)S(1)} %bitcast.28, ...), custom_call_target="tpu_custom_call" | custom-call | flops 4000000000 | bytes 6946816 | tf_op jit(solution)/shard_map/partial_grad/pallas_call | solution.py:346
  57.9 3.3 %collective-permute-start.6 = (f32[4,64,640]{2,1,0:T(8,128)S(1)}, f32[4,64,640]{2,1,0:T(8,128)S(1)}, u32[]{:S(2)}, u32[]{:S(2)}) collective-permute-start(f32[4,64,640]{2,1,0:T(8,128)S(1)} %get-tuple-element.59), channel_id=1, source_target_pairs={{0,2},{1,3},{2,0},{3,1},{4,20},{5,21},{6,22},{7,23},{8,10},{9,11},... | collective-permute-start | bytes 1966088 | tf_op jit(solution)/shard_map/ppermute | solution.py:43
  61.2 1.1 %collective-permute-start.7 = (f32[4,64,640]{2,1,0:T(8,128)S(1)}, f32[4,64,640]{2,1,0:T(8,128)S(1)}, u32[]{:S(2)}, u32[]{:S(2)}) collective-permute-start(f32[4,64,640]{2,1,0:T(8,128)S(1)} %get-tuple-element.60), channel_id=1, source_target_pairs={{0,3},{1,0},{2,1},{3,2},{4,28},{5,29},{6,30},{7,31},{8,11},{9,8},{... | collective-permute-start | bytes 1966088 | tf_op jit(solution)/shard_map/ppermute | solution.py:43
  62.4 0.9 collective-permute-start.5
  63.3 0.1 scan_backward.1
  63.3 14.0 %all_to_all.21.refs_0_ = f32[32,8,128]{2,1,0:T(8,128)S(1)} all-to-all(f32[32,8,128]{2,1,0:T(8,128)S(1)} %scan_backward.1), channel_id=1, replica_groups={{0,8,16,24,32,40,48,56,64,72,80,88,96,104,112,120,128,136,144,152,160,1..., dimensions={0} | all-to-all | bytes 262144 | tf_op jit(solution)/shard_map/all_to_all | solution.py:366
  77.3 0.0 collective-permute-done.6
  77.3 0.1 collective-permute-done.7
  77.4 0.0 collective-permute-done.5
  77.4 0.1 add_add_fusion
  77.6 1.2 %collective-permute-start.8 = (f32[64,640]{1,0:T(8,128)S(1)}, f32[64,640]{1,0:T(8,128)S(1)}, u32[]{:S(2)}, u32[]{:S(2)}) collective-permute-start(f32[64,640]{1,0:T(8,128)S(1)} %get-tuple-element.75), channel_id=1, source_target_pairs={{0,16},{1,17},{2,18},{3,19},{4,6},{5,7},{6,4},{7,5},{8,24},{9,25},... | collective-permute-start | bytes 491528 | tf_op jit(solution)/shard_map/ppermute | solution.py:43
  78.8 2.1 %collective-permute-start.10 = (f32[64,640]{1,0:T(8,128)S(1)}, f32[64,640]{1,0:T(8,128)S(1)}, u32[]{:S(2)}, u32[]{:S(2)}) collective-permute-start(f32[64,640]{1,0:T(8,128)S(1)} %get-tuple-element.76), channel_id=1, source_target_pairs={{0,24},{1,25},{2,26},{3,27},{4,7},{5,4},{6,5},{7,6},{8,0},{9,1},{1... | collective-permute-start | bytes 491528 | tf_op jit(solution)/shard_map/ppermute | solution.py:43
  80.9 0.0 collective-permute-start.9
  81.0 0.6 copy-done.8
  81.6 1.4 %collective-permute-start.11 = (f32[256,128]{1,0:T(8,128)S(1)}, f32[256,128]{1,0:T(8,128)S(1)}, u32[]{:S(2)}, u32[]{:S(2)}) collective-permute-start(f32[256,128]{1,0:T(8,128)S(1)} %get-tuple-element.69), channel_id=1, source_target_pairs={{0,4},{1,5},{2,6},{3,7},{4,0},{5,1},{6,2},{7,3},{8,12},{9,13},{10,... | collective-permute-start | bytes 393224 | tf_op jit(solution)/shard_map/ppermute | solution.py:43
  83.0 1.5 %collective-permute-done.8 = f32[64,640]{1,0:T(8,128)S(1)} collective-permute-done((f32[64,640]{1,0:T(8,128)S(1)}, f32[64,640]{1,0:T(8,128)S(1)}, u32[]{:S(2)}, u32[]{:S(2)}) %collective-permute-start.8) | collective-permute-done | bytes 163872 | tf_op jit(solution)/shard_map/ppermute | solution.py:43
  84.5 0.4 collective-permute-done.10
  84.9 2.6 %collective-permute-done.9 = f32[64,640]{1,0:T(8,128)S(1)} collective-permute-done((f32[64,640]{1,0:T(8,128)S(1)}, f32[64,640]{1,0:T(8,128)S(1)}, u32[]{:S(2)}, u32[]{:S(2)}) %collective-permute-start.9) | collective-permute-done | bytes 163872 | tf_op jit(solution)/shard_map/ppermute | solution.py:43
  87.5 0.7 fusion.3
  88.2 3.9 %all-to-all-start.3 = ((f32[8,8,640]{2,1,0:T(8,128)}), f32[8,8,640]{2,1,0:T(8,128)S(1)}, u32[]{:S(2)}, u32[]{:S(2)}) async-start(f32[8,8,640]{2,1,0:T(8,128)} %fusion.3), calls=%async_computation.3 | async-start | bytes 327680 | tf_op jit(solution)/shard_map/all_to_all | solution.py:366
  92.1 0.0 collective-permute-done.11.refs_9_
  92.1 0.6 copy-done.12
  92.8 6.3 %gradients.1 = (bf16[256,512]{1,0:T(8,128)(2,1)}, bf16[256,128]{1,0:T(8,128)(2,1)}, bf16[256,128]{1,0:T(8,128)(2,1)}) custom-call(f32[8]{0:T(128)} %refs_0_.7, s32[8,256]{1,0:T(8,128)} %bitcast.42, bf16[256,512]{1,0:T(8,128)(2,1)} %bitcast.35, bf16[256,128]{1,0:T(8,128)(2,1)} %bitcast.38, bf16[256,128]{1,0:T(8,128)(2,1)} %bitcast.31, ...), custom_call_target="tpu_custom_call" | custom-call | flops 5000000000 | bytes 1581088 | tf_op jit(solution)/shard_map/gradients/pallas_call | solution.py:346
  99.0 1.7 %all-to-all-done.3 = f32[8,8,640]{2,1,0:T(8,128)S(1)} async-done(((f32[8,8,640]{2,1,0:T(8,128)}), f32[8,8,640]{2,1,0:T(8,128)S(1)}, u32[]{:S(2)}, u32[]{:S(2)}) %all-to-all-start.3) | async-done | bytes 163872 | tf_op jit(solution)/shard_map/all_to_all | solution.py:366
  100.7 1.9 %collective-permute-start.14 = (f32[8,640]{1,0:T(8,128)S(1)}, f32[8,640]{1,0:T(8,128)S(1)}, u32[]{:S(2)}, u32[]{:S(2)}) collective-permute-start(f32[8,640]{1,0:T(8,128)S(1)} %reduce_sum.9.refs_0_), channel_id=1, source_target_pairs={{0,3},{1,0},{2,1},{3,2},{4,7},{5,4},{6,5},{7,6},{8,11},{9,8},{10,9... | collective-permute-start | bytes 61448 | tf_op jit(solution)/shard_map/ppermute | solution.py:43
  102.7 0.9 collective-permute-start.13
  103.6 0.8 collective-permute-start.12
  104.4 0.2 collective-permute-done.14.refs_3_
  104.6 3.4 %collective-permute-done.13.refs_2_ = f32[8,640]{1,0:T(8,128)S(1)} collective-permute-done((f32[8,640]{1,0:T(8,128)S(1)}, f32[8,640]{1,0:T(8,128)S(1)}, u32[]{:S(2)}, u32[]{:S(2)}) %collective-permute-start.13) | collective-permute-done | bytes 20512 | tf_op jit(solution)/shard_map/ppermute | solution.py:43
  108.0 0.6 collective-permute-done.12.refs_1_
  108.6 0.6 place.1
  (14 shorter events, 0.2 us)
Async XLA Ops:
  3.8 1.7 %collective-permute-start = (f32[264,128]{1,0:T(8,128)}, f32[264,128]{1,0:T(8,128)S(1)}, u32[]{:S(2)}, u32[]{:S(2)}) collective-permute-start(f32[264,128]{1,0:T(8,128)} %get-tuple-element.41), channel_id=1, source_target_pairs={{0,4},{1,5},{2,6},{3,7},{4,0},{5,1},{6,2},{7,3},{8,12},{9,13},{10,... | collective-permute-start | bytes 405512 | tf_op jit(solution)/shard_map/ppermute | solution.py:43
  5.4 0.9 copy-start.6
  6.3 0.7 copy-start.9
  7.7 23.8 %all-to-all-start = ((f32[32,16,128]{2,1,0:T(8,128)}), f32[32,16,128]{2,1,0:T(8,128)S(1)}, u32[]{:S(2)}, u32[]{:S(2)}) async-start(f32[32,16,128]{2,1,0:T(8,128)} %chip_forward.1), calls=%async_computation | async-start | bytes 524288 | tf_op jit(solution)/shard_map/all_to_all | solution.py:366
  24.3 7.3 %copy-start.11 = (f32[256,2560]{1,0:T(8,128)S(1)}, f32[256,2560]{1,0:T(8,128)}, u32[]{:S(2)}) copy-start(f32[256,2560]{1,0:T(8,128)} %get-tuple-element.56) | copy-start | bytes 7864324
  24.3 7.3 %copy-start.4 = (f32[256,128]{1,0:T(8,128)S(1)}, f32[256,128]{1,0:T(8,128)}, u32[]{:S(2)}) copy-start(f32[256,128]{1,0:T(8,128)} %get-tuple-element.48.refs_1_) | copy-start | bytes 393220
  24.3 7.3 %copy-start.10 = (f32[8,128]{1,0:T(8,128)S(1)}, f32[8,128]{1,0:T(8,128)}, u32[]{:S(2)}) copy-start(f32[8,128]{1,0:T(8,128)} %get-tuple-element.42.refs_2_.refs_3_) | copy-start | bytes 12292
  24.3 5.0 %collective-permute-start.1 = (f32[256,128]{1,0:T(8,128)}, f32[256,128]{1,0:T(8,128)S(1)}, u32[]{:S(2)}, u32[]{:S(2)}) collective-permute-start(f32[256,128]{1,0:T(8,128)} %get-tuple-element.44), channel_id=1, source_target_pairs={{0,4},{1,5},{2,6},{3,7},{4,0},{5,1},{6,2},{7,3},{8,12},{9,13},{10,... | collective-permute-start | bytes 393224 | tf_op jit(solution)/shard_map/ppermute | solution.py:43
  29.3 22.8 %copy-start.7 = (f32[256,128]{1,0:T(8,128)S(1)}, f32[256,128]{1,0:T(8,128)}, u32[]{:S(2)}) copy-start(f32[256,128]{1,0:T(8,128)} %get-tuple-element.40.refs_0_.refs_1_) | copy-start | bytes 393220
  31.6 24.7 %collective-permute-start.4 = (f32[256,2560]{1,0:T(8,128)S(1)}, f32[256,2560]{1,0:T(8,128)S(1)}, u32[]{:S(2)}, u32[]{:S(2)}) collective-permute-start(f32[256,2560]{1,0:T(8,128)S(1)} %copy-done.11), channel_id=1, source_target_pairs={{0,4},{1,5},{2,6},{3,7},{4,0},{5,1},{6,2},{7,3},{8,12},{9,13},{10,... | collective-permute-start | bytes 7864328 | tf_op jit(solution)/shard_map/ppermute | solution.py:43
  31.7 21.9 %copy-start.2 = (bf16[1,256,128]{2,1,0:T(8,128)(2,1)S(1)}, bf16[1,256,128]{2,1,0:T(8,128)(2,1)}, u32[]{:S(2)}) copy-start(bf16[1,256,128]{2,1,0:T(8,128)(2,1)} %param.9) | copy-start | bytes 196612
  31.7 21.9 %copy-start.3 = (f32[256,1024]{1,0:T(8,128)S(1)}, f32[256,1024]{1,0:T(8,128)}, u32[]{:S(2)}) copy-start(f32[256,1024]{1,0:T(8,128)} %intra_forward.1.refs_3_) | copy-start | bytes 3145732
  52.2 2.5 %copy-start.5 = (f32[256,128]{1,0:T(8,128)}, f32[256,128]{1,0:T(8,128)S(1)}, u32[]{:S(2)}) copy-start(f32[256,128]{1,0:T(8,128)S(1)} %get-tuple-element.50.refs_0_.refs_6_) | copy-start | bytes 393220
  52.2 1.4 %collective-permute-start.2 = (f32[256,128]{1,0:T(8,128)S(1)}, f32[256,128]{1,0:T(8,128)S(1)}, u32[]{:S(2)}, u32[]{:S(2)}) collective-permute-start(f32[256,128]{1,0:T(8,128)S(1)} %get-tuple-element.51), channel_id=1, source_target_pairs={{0,4},{1,5},{2,6},{3,7},{4,0},{5,1},{6,2},{7,3},{8,12},{9,13},{10,... | collective-permute-start | bytes 393224 | tf_op jit(solution)/shard_map/ppermute | solution.py:43
  53.6 1.1 %copy-start.1 = (f32[256,128]{1,0:T(8,128)}, f32[256,128]{1,0:T(8,128)S(1)}, u32[]{:S(2)}) copy-start(f32[256,128]{1,0:T(8,128)S(1)} %collective-permute-done.2.refs_1_.refs_7_) | copy-start | bytes 393220
  53.6 2.6 %copy-start = (bf16[1,256,2560]{2,1,0:T(8,128)(2,1)S(1)}, bf16[1,256,2560]{2,1,0:T(8,128)(2,1)}, u32[]{:S(2)}) copy-start(bf16[1,256,2560]{2,1,0:T(8,128)(2,1)} %param.13) | copy-start | bytes 3932164
  54.7 1.5 %collective-permute-start.3 = (f32[256,256]{1,0:T(8,128)S(1)}, f32[256,256]{1,0:T(8,128)S(1)}, u32[]{:S(2)}, u32[]{:S(2)}) collective-permute-start(f32[256,256]{1,0:T(8,128)S(1)} %get-tuple-element.55), channel_id=1, source_target_pairs={{0,4},{1,5},{2,6},{3,7},{4,0},{5,1},{6,2},{7,3},{8,12},{9,13},{10,... | collective-permute-start | bytes 786440 | tf_op jit(solution)/shard_map/ppermute | solution.py:43
  57.9 19.4 %collective-permute-start.6 = (f32[4,64,640]{2,1,0:T(8,128)S(1)}, f32[4,64,640]{2,1,0:T(8,128)S(1)}, u32[]{:S(2)}, u32[]{:S(2)}) collective-permute-start(f32[4,64,640]{2,1,0:T(8,128)S(1)} %get-tuple-element.59), channel_id=1, source_target_pairs={{0,2},{1,3},{2,0},{3,1},{4,20},{5,21},{6,22},{7,23},{8,10},{9,11},... | collective-permute-start | bytes 1966088 | tf_op jit(solution)/shard_map/ppermute | solution.py:43
  61.2 16.2 %collective-permute-start.7 = (f32[4,64,640]{2,1,0:T(8,128)S(1)}, f32[4,64,640]{2,1,0:T(8,128)S(1)}, u32[]{:S(2)}, u32[]{:S(2)}) collective-permute-start(f32[4,64,640]{2,1,0:T(8,128)S(1)} %get-tuple-element.60), channel_id=1, source_target_pairs={{0,3},{1,0},{2,1},{3,2},{4,28},{5,29},{6,30},{7,31},{8,11},{9,8},{... | collective-permute-start | bytes 1966088 | tf_op jit(solution)/shard_map/ppermute | solution.py:43
  62.4 15.1 %collective-permute-start.5 = (f32[4,64,640]{2,1,0:T(8,128)S(1)}, f32[4,64,640]{2,1,0:T(8,128)S(1)}, u32[]{:S(2)}, u32[]{:S(2)}) collective-permute-start(f32[4,64,640]{2,1,0:T(8,128)S(1)} %get-tuple-element.58), channel_id=1, source_target_pairs={{0,1},{1,2},{2,3},{3,0},{4,12},{5,13},{6,14},{7,15},{8,9},{9,10},{... | collective-permute-start | bytes 1966088 | tf_op jit(solution)/shard_map/ppermute | solution.py:43
  77.6 6.9 %collective-permute-start.8 = (f32[64,640]{1,0:T(8,128)S(1)}, f32[64,640]{1,0:T(8,128)S(1)}, u32[]{:S(2)}, u32[]{:S(2)}) collective-permute-start(f32[64,640]{1,0:T(8,128)S(1)} %get-tuple-element.75), channel_id=1, source_target_pairs={{0,16},{1,17},{2,18},{3,19},{4,6},{5,7},{6,4},{7,5},{8,24},{9,25},... | collective-permute-start | bytes 491528 | tf_op jit(solution)/shard_map/ppermute | solution.py:43
  78.8 6.1 %collective-permute-start.10 = (f32[64,640]{1,0:T(8,128)S(1)}, f32[64,640]{1,0:T(8,128)S(1)}, u32[]{:S(2)}, u32[]{:S(2)}) collective-permute-start(f32[64,640]{1,0:T(8,128)S(1)} %get-tuple-element.76), channel_id=1, source_target_pairs={{0,24},{1,25},{2,26},{3,27},{4,7},{5,4},{6,5},{7,6},{8,0},{9,1},{1... | collective-permute-start | bytes 491528 | tf_op jit(solution)/shard_map/ppermute | solution.py:43
  80.9 6.5 %collective-permute-start.9 = (f32[64,640]{1,0:T(8,128)S(1)}, f32[64,640]{1,0:T(8,128)S(1)}, u32[]{:S(2)}, u32[]{:S(2)}) collective-permute-start(f32[64,640]{1,0:T(8,128)S(1)} %get-tuple-element.77), channel_id=1, source_target_pairs={{0,8},{1,9},{2,10},{3,11},{4,5},{5,6},{6,7},{7,4},{8,16},{9,17},{1... | collective-permute-start | bytes 491528 | tf_op jit(solution)/shard_map/ppermute | solution.py:43
  81.0 0.6 copy-start.8
  81.6 10.5 %collective-permute-start.11 = (f32[256,128]{1,0:T(8,128)S(1)}, f32[256,128]{1,0:T(8,128)S(1)}, u32[]{:S(2)}, u32[]{:S(2)}) collective-permute-start(f32[256,128]{1,0:T(8,128)S(1)} %get-tuple-element.69), channel_id=1, source_target_pairs={{0,4},{1,5},{2,6},{3,7},{4,0},{5,1},{6,2},{7,3},{8,12},{9,13},{10,... | collective-permute-start | bytes 393224 | tf_op jit(solution)/shard_map/ppermute | solution.py:43
  88.2 12.6 %all-to-all-start.3 = ((f32[8,8,640]{2,1,0:T(8,128)}), f32[8,8,640]{2,1,0:T(8,128)S(1)}, u32[]{:S(2)}, u32[]{:S(2)}) async-start(f32[8,8,640]{2,1,0:T(8,128)} %fusion.3), calls=%async_computation.3 | async-start | bytes 327680 | tf_op jit(solution)/shard_map/all_to_all | solution.py:366
  92.1 0.7 copy-start.12
  100.7 3.9 %collective-permute-start.14 = (f32[8,640]{1,0:T(8,128)S(1)}, f32[8,640]{1,0:T(8,128)S(1)}, u32[]{:S(2)}, u32[]{:S(2)}) collective-permute-start(f32[8,640]{1,0:T(8,128)S(1)} %reduce_sum.9.refs_0_), channel_id=1, source_target_pairs={{0,3},{1,0},{2,1},{3,2},{4,7},{5,4},{6,5},{7,6},{8,11},{9,8},{10,9... | collective-permute-start | bytes 61448 | tf_op jit(solution)/shard_map/ppermute | solution.py:43
  102.7 5.3 %collective-permute-start.13 = (f32[8,640]{1,0:T(8,128)S(1)}, f32[8,640]{1,0:T(8,128)S(1)}, u32[]{:S(2)}, u32[]{:S(2)}) collective-permute-start(f32[8,640]{1,0:T(8,128)S(1)} %reduce_sum.9.refs_0_), channel_id=1, source_target_pairs={{0,2},{1,3},{2,0},{3,1},{4,6},{5,7},{6,4},{7,5},{8,10},{9,11},{10,... | collective-permute-start | bytes 61448 | tf_op jit(solution)/shard_map/ppermute | solution.py:43
  103.6 5.0 %collective-permute-start.12 = (f32[8,640]{1,0:T(8,128)S(1)}, f32[8,640]{1,0:T(8,128)S(1)}, u32[]{:S(2)}, u32[]{:S(2)}) collective-permute-start(f32[8,640]{1,0:T(8,128)S(1)} %reduce_sum.9.refs_0_), channel_id=1, source_target_pairs={{0,1},{1,2},{2,3},{3,0},{4,5},{5,6},{6,7},{7,4},{8,9},{9,10},{10,1... | collective-permute-start | bytes 61448 | tf_op jit(solution)/shard_map/ppermute | solution.py:43

commit v4 on v3

--- a/solution.py
+++ b/solution.py
@@ -64,11 +64,11 @@
     return at >> 3, (at >> 1) & 3, at & 1, lax.axis_index("dp")
 
 
-def rate_lanes(rate_ref, width):
-    lane = lax.broadcasted_iota(jnp.int32, (1, width), 1) // (width // HEADS)
-    rates = jnp.zeros((1, width), f32)
+def rate_rows(rate_ref):
+    head = lax.broadcasted_iota(jnp.int32, (HEADS, 1), 0)
+    rates = jnp.zeros((HEADS, 1), f32)
     for h in range(HEADS):
-        rates = jnp.where(lane == h, rate_ref[h] * RATE_UNIT, rates)
+        rates = jnp.where(head == h, rate_ref[h] * RATE_UNIT, rates)
     return rates
 
 
@@ -81,11 +81,23 @@
     return jnp.where(plus, 1.0, jnp.where(minus, -1.0, 0.0)).astype(f32)
 
 
-def step_lanes(cum, dt_lanes):
-    ones = jnp.ones((8, TOK // 2), f32)
-    start = -lax.dot_general(ones, dt_lanes[:, : TOK // 2], NT, precision=HI, preferred_element_type=f32)[:1]
-    row = lax.broadcasted_iota(jnp.int32, (TOK, CH), 0)
-    return jnp.where(row == 0, cum - start, cum - pltpu.roll(cum, 1, 0)), start
+def row_sums(dt):
+    return lax.dot_general(dt, signed_tri(), NT, precision=HI, preferred_element_type=f32)
+
+
+def column_sums(dt):
+    return lax.dot_general(signed_tri(), dt, NT, precision=HI, preferred_element_type=f32)
+
+
+def before_first(dt):
+    return -jnp.sum(dt[:, : TOK // 2], axis=1, keepdims=True)
+
+
+def spread(rows):
+    head = lax.broadcasted_iota(jnp.int32, (HEADS, CH), 0)
+    lane = lax.broadcasted_iota(jnp.int32, (HEADS, CH), 1) // HEAD_DIM
+    pick = jnp.where(head == lane, 1.0, 0.0).astype(f32)
+    return lax.dot_general(rows, pick, TN, precision=HI, preferred_element_type=f32)
 
 
 def gate(v):
@@ -95,48 +107,37 @@
     return jnp.sqrt(jnp.where(v < 0.25, v * s, 1.0 - jnp.exp(-v)))
 
 
-def lanes_of(dt):
-    return jnp.broadcast_to(dt[:, None, :], (HEADS, HEAD_DIM, TOK)).reshape(CH, TOK)
-
-
-def local_forward(rate_ref, dt_ref, x_ref, b_ref, mine_ref, send_ref, tot_ref):
+def local_forward(rate_ref, dt_ref, x_ref, b_ref, mine_ref, send_ref):
     core = place_of()[2]
     dt = dt_ref[...].astype(f32)
-    rate = rate_lanes(rate_ref, CH)
-    dt_lanes = lanes_of(dt)
-    cum = lax.dot_general(signed_tri(), dt_lanes, NT, precision=HI, preferred_element_type=f32)
-    w = gate(step_lanes(cum, dt_lanes)[0] * (2.0 * rate))
-    xt = (x_ref[...].astype(f32) * w * jnp.exp((cum - cum[TOK - 1:]) * rate)).astype(bf16)
+    rate = rate_rows(rate_ref)
+    cum = row_sums(dt)
+    tail = jnp.exp((cum - cum[:, TOK - 1:]) * rate)
+    xt = (x_ref[...].astype(f32) * spread(gate(dt * (2.0 * rate)) * tail)).astype(bf16)
     own = mm(xt, b_ref[...], TN)
-    head = lax.broadcasted_iota(jnp.int32, (HEADS, 1), 0)
-    rate_col = jnp.zeros((HEADS, 1), f32)
-    for h in range(HEADS):
-        rate_col = jnp.where(head == h, rate_ref[h] * RATE_UNIT, rate_col)
-    tot = jnp.broadcast_to(-(jnp.sum(dt, axis=1, keepdims=True) * rate_col), (HEADS, STATE))
-    tot_ref[...] = tot
+    tot = jnp.broadcast_to(-(jnp.sum(dt, axis=1, keepdims=True) * rate), (HEADS, STATE))
+    mine_ref[HALF:, :] = tot
     send_ref[HALF:, :] = tot
 
     @pl.when(core == 0)
     def _():
-        mine_ref[...] = own[:HALF]
+        mine_ref[:HALF, :] = own[:HALF]
         send_ref[:HALF, :] = own[HALF:]
 
     @pl.when(core == 1)
     def _():
-        mine_ref[...] = own[HALF:]
+        mine_ref[:HALF, :] = own[HALF:]
         send_ref[:HALF, :] = own[:HALF]
 
 
 def local_backward(rate_ref, dt_ref, c_ref, g_ref, w_ref, mine_ref, send_ref, gy_ref, wide_ref):
     core = place_of()[2]
-    rate = rate_lanes(rate_ref, CH)
-    dt_lanes = lanes_of(dt_ref[...].astype(f32))
-    cum = lax.dot_general(signed_tri(), dt_lanes, NT, precision=HI, preferred_element_type=f32)
-    decay = jnp.exp((step_lanes(cum, dt_lanes)[1] - cum) * rate)
+    dt = dt_ref[...].astype(f32)
+    decay = spread(jnp.exp((before_first(dt) - row_sums(dt)) * rate_rows(rate_ref)))
     g = g_ref[...]
+    wide_ref[...] = g.astype(f32)
     gy = mm(g, w_ref[...], NT).astype(bf16)
     gy_ref[...] = gy
-    wide_ref[...] = g.astype(f32)
     adj = mm((gy.astype(f32) * decay).astype(bf16), c_ref[...], TN)
 
     @pl.when(core == 0)
@@ -159,50 +160,54 @@
     return jnp.broadcast_to(rows[:, None, :], (HEADS // 2, HEAD_DIM, STATE)).reshape(HALF, STATE)
 
 
-def chip_forward(mine_ref, peer_ref, tot_ref, out_ref):
-    core = place_of()[2]
-    own = my_heads(core, tot_ref[...])
+def chip_forward(mine_ref, peer_ref, out_ref):
+    core = place_of()[2]
+    own = my_heads(core, mine_ref[HALF:, :])
     other = my_heads(core, peer_ref[HALF:, :])
-    mine, peer = mine_ref[...], peer_ref[:HALF, :]
+    mine, peer = mine_ref[:HALF, :], peer_ref[:HALF, :]
     second = decay_rows(jnp.where(core == 0, other, own))
     chip = jnp.where(core == 0, mine, peer) * second + jnp.where(core == 0, peer, mine)
-    out_ref[:, :PIECE, :] = chip.reshape(CHIPS, PIECE, STATE)
-    tots = jnp.broadcast_to((own + other)[:, None, None, :], (HEADS // 2, CHIPS // (HEADS // 2), PIECE, STATE))
-    out_ref[:, PIECE:, :] = tots.reshape(CHIPS, PIECE, STATE)
-
-
-def scan_forward(in_ref, mine_ref, peer_ref, tot_ref, fpeer_ref, out_ref):
-    core = place_of()[2]
-    first = decay_rows(my_heads(core, jnp.where(core == 0, tot_ref[...], fpeer_ref[HALF:, :])))
+    rows = chip.reshape(CHIPS, PIECE, STATE)
+    for r in range(PIECE):
+        out_ref[:, 0, r * STATE:(r + 1) * STATE] = rows[:, r, :]
+    tots = jnp.broadcast_to((own + other)[:, None, :], (HEADS // 2, CHIPS // (HEADS // 2), STATE))
+    out_ref[:, 0, PIECE * STATE:] = tots.reshape(CHIPS, STATE)
+
+
+def scan_forward(in_ref, mine_ref, peer_ref, fmine_ref, fpeer_ref, out_ref):
+    core = place_of()[2]
+    first = decay_rows(my_heads(core, jnp.where(core == 0, fmine_ref[HALF:, :], fpeer_ref[HALF:, :])))
     mine, peer = mine_ref[...], peer_ref[...]
     chip = jnp.where(core == 0, mine, peer) + jnp.where(core == 0, peer, mine) * first
     out_ref[:, PIECE:, :] = chip.reshape(CHIPS, PIECE, STATE)
-    acc = jnp.zeros((PIECE, STATE), f32)
+    acc = [jnp.zeros((1, STATE), f32)] * PIECE
     for k in range(CHIPS):
-        out_ref[k, :PIECE, :] = acc
-        acc = acc * jnp.exp(in_ref[k, PIECE:, :]) + in_ref[k, :PIECE, :]
+        keep = jnp.exp(in_ref[k, :, PIECE * STATE:])
+        for r in range(PIECE):
+            out_ref[k, r:r + 1, :] = acc[r]
+            acc[r] = acc[r] * keep + in_ref[k, :, r * STATE:(r + 1) * STATE]
 
 
 def scan_backward(dec_ref, in_ref, out_ref):
     acc = jnp.zeros((PIECE, STATE), f32)
     for k in range(CHIPS - 1, -1, -1):
         out_ref[k] = acc
-        acc = acc * jnp.exp(dec_ref[k, PIECE:, :]) + in_ref[k, PIECE:, :]
-
-
-def core_forward(got_ref, mine_ref, peer_ref, tot_ref, keep_ref, send_ref):
+        acc = acc * jnp.exp(dec_ref[k, :, PIECE * STATE:]) + in_ref[k, PIECE:, :]
+
+
+def core_forward(got_ref, mine_ref, peer_ref, keep_ref, send_ref):
     core = place_of()[2]
     into = got_ref[:, :PIECE, :].reshape(HALF, STATE)
-    first = decay_rows(my_heads(core, jnp.where(core == 0, tot_ref[...], peer_ref[HALF:, :])))
-    after = into * first + jnp.where(core == 0, mine_ref[...], peer_ref[:HALF, :])
+    first = decay_rows(my_heads(core, jnp.where(core == 0, mine_ref[HALF:, :], peer_ref[HALF:, :])))
+    after = into * first + jnp.where(core == 0, mine_ref[:HALF, :], peer_ref[:HALF, :])
     keep_ref[...] = jnp.where(core == 0, into, after)
     send_ref[...] = jnp.where(core == 0, after, into)
 
 
-def core_backward(got_ref, mine_ref, peer_ref, tot_ref, fpeer_ref, keep_ref, send_ref):
+def core_backward(got_ref, mine_ref, peer_ref, fmine_ref, fpeer_ref, keep_ref, send_ref):
     core = place_of()[2]
     after = got_ref[...].reshape(HALF, STATE)
-    second = decay_rows(my_heads(core, jnp.where(core == 0, fpeer_ref[HALF:, :], tot_ref[...])))
+    second = decay_rows(my_heads(core, jnp.where(core == 0, fpeer_ref[HALF:, :], fmine_ref[HALF:, :])))
     into = after * second + jnp.where(core == 0, peer_ref[...], mine_ref[...])
     keep_ref[...] = jnp.where(core == 0, into, after)
     send_ref[...] = jnp.where(core == 0, after, into)
@@ -214,27 +219,20 @@
     return jnp.concatenate([low, high], axis=0).astype(bf16)
 
 
-def head_masks(rate_ref, dt, cum):
-    cum_rows = lax.dot_general(dt, signed_tri(), NT, precision=HI, preferred_element_type=f32)
+def intra_forward(rate_ref, dt_ref, x_ref, b_ref, c_ref, out_ref):
+    dt = dt_ref[...].astype(f32)
+    rate = rate_rows(rate_ref)
+    rows, cols = row_sums(dt), column_sums(dt)
+    xw = (x_ref[...].astype(f32) * spread(gate(dt * (2.0 * rate)))).astype(bf16)
+    scores = mm(c_ref[...], b_ref[...], NT)
     i = lax.broadcasted_iota(jnp.int32, (TOK, TOK), 0)
     j = lax.broadcasted_iota(jnp.int32, (TOK, TOK), 1)
     for h in range(HEADS):
-        gap = cum_rows[h:h + 1, :] - cum[:, h * HEAD_DIM:h * HEAD_DIM + 1]
-        mask = jnp.exp(jnp.where(i >= j, gap * (rate_ref[h] * RATE_UNIT), -jnp.inf))
-        yield slice(h * HEAD_DIM, (h + 1) * HEAD_DIM), mask
-
-
-def intra_forward(rate_ref, dt_ref, x_ref, b_ref, c_ref, out_ref):
-    dt = dt_ref[...].astype(f32)
-    rate = rate_lanes(rate_ref, CH)
-    dt_lanes = lanes_of(dt)
-    cum = lax.dot_general(signed_tri(), dt_lanes, NT, precision=HI, preferred_element_type=f32)
-    steps, start = step_lanes(cum, dt_lanes)
-    xw = (x_ref[...].astype(f32) * gate(steps * (2.0 * rate))).astype(bf16)
-    scores = mm(c_ref[...], b_ref[...], NT)
-    for lanes, mask in head_masks(rate_ref, dt, cum):
+        lanes = slice(h * HEAD_DIM, (h + 1) * HEAD_DIM)
+        gap = (rows[h:h + 1, :] - cols[:, h:h + 1]) * (rate_ref[h] * RATE_UNIT)
+        mask = jnp.exp(jnp.where(i >= j, gap, -jnp.inf))
         out_ref[:, lanes] = mm((mask * scores).astype(bf16), xw[:, lanes], NN)
-    out_ref[:, CH:] = jnp.exp((start - cum) * rate)
+    out_ref[:, CH:] = spread(jnp.exp((before_first(dt) - rows) * rate))
 
 
 def select_rows(core, y_at):
@@ -279,31 +277,34 @@
               gi_ref, gwr_ref, grd_ref):
     core = place_of()[2]
     dt = dt_ref[...].astype(f32)
-    rate = rate_lanes(rate_ref, CH)
-    dt_lanes = lanes_of(dt)
-    cum = lax.dot_general(signed_tri(), dt_lanes, NT, precision=HI, preferred_element_type=f32)
-    steps, start = step_lanes(cum, dt_lanes)
-    w = gate(steps * (2.0 * rate))
-    tail = jnp.exp((cum - cum[TOK - 1:]) * rate)
-    xw = x_ref[...].astype(f32) * w
-    xt = (xw * tail).astype(bf16)
-    xw = xw.astype(bf16)
+    rate = rate_rows(rate_ref)
+    rows, cols = row_sums(dt), column_sums(dt)
+    gates = gate(dt * (2.0 * rate))
+    w = spread(gates)
+    wt = spread(gates * jnp.exp((rows - rows[:, TOK - 1:]) * rate))
+    x = x_ref[...].astype(f32)
+    xw, xt = (x * w).astype(bf16), (x * wt).astype(bf16)
     gy = gy_ref[...]
-    gyd = (gy.astype(f32) * jnp.exp((start - cum) * rate)).astype(bf16)
+    gyd = (gy.astype(f32) * spread(jnp.exp((before_first(dt) - rows) * rate))).astype(bf16)
     b = b_ref[...]
     c = c_ref[...]
-    scores = mm(c, b, NT)
+    scores = mm(b, c, NT)
+    j = lax.broadcasted_iota(jnp.int32, (TOK, TOK), 0)
+    i = lax.broadcasted_iota(jnp.int32, (TOK, TOK), 1)
     state = both_halves(core, keep_ref[...], recv_ref[...])
     adj = both_halves(core, after_ref[...], recv2_ref[...])
-    inter = tail * mm(b, adj, NT)
+    inter = wt * mm(b, adj, NT)
     pairs = jnp.zeros((TOK, TOK), f32)
-    for lanes, mask in head_masks(rate_ref, dt, cum):
-        intra = mm((mask * scores).astype(bf16), gy[:, lanes], TN)
-        gi_ref[:, lanes] = (w[:, lanes] * (intra + inter[:, lanes])).astype(bf16)
-        pairs = pairs + mask * mm(gy[:, lanes], xw[:, lanes], NT)
+    for h in range(HEADS):
+        lanes = slice(h * HEAD_DIM, (h + 1) * HEAD_DIM)
+        gap = (cols[:, h:h + 1] - rows[h:h + 1, :]) * (rate_ref[h] * RATE_UNIT)
+        mask = jnp.exp(jnp.where(i >= j, gap, -jnp.inf))
+        intra = mm((mask * scores).astype(bf16), gy[:, lanes], NN)
+        gi_ref[:, lanes] = (w[:, lanes] * intra + inter[:, lanes]).astype(bf16)
+        pairs = pairs + mask * mm(xw[:, lanes], gy[:, lanes], NT)
     pairs = pairs.astype(bf16)
-    grd_ref[...] = (mm(pairs, b, NN) + mm(gyd, state, NN)).astype(bf16)
-    gwr_ref[...] = (mm(pairs, c, TN) + mm(xt, adj, NN)).astype(bf16)
+    grd_ref[...] = (mm(pairs, b, TN) + mm(gyd, state, NN)).astype(bf16)
+    gwr_ref[...] = (mm(pairs, c, NN) + mm(xt, adj, NN)).astype(bf16)
 
 
 def place(r0_ref, r1_ref, r2_ref, r3_ref, out_ref):
@@ -367,22 +368,24 @@
 
     half = ((HALF, STATE), f32)
     tokens, narrow = ((TOK, CH), bf16), ((TOK, STATE), bf16)
-    mine, send, tot = call(local_forward, [half, ((HALF + 8, STATE), f32), ((HEADS, STATE), f32)], 4,
-                           a_rate, dt, x, b, us=2)
+    both = ((HALF + 8, STATE), f32)
+    mine, send = call(local_forward, [both, both], 4, a_rate, dt, x, b, us=2)
     peer = permute(send, swap_core)
-    chip = call(chip_forward, [((CHIPS, 2 * PIECE, STATE), f32)], 0, mine, peer, tot)
+    chip = call(chip_forward, [((CHIPS, 1, (PIECE + 1) * STATE), f32)], 0, mine, peer)
     pieces = over(chip, chips)
 
-    g2, x2 = lax.optimization_barrier((g, x, chip))[:2]
+    g2 = lax.optimization_barrier((g, chip))[0]
     bmine, bsend, gy, g_wide = call(local_backward, [half, half, tokens, ((TOK, D), f32)], 5,
                                     a_rate, dt, c, g2, w_out, us=4)
     bpeer = permute(bsend, swap_core)
+    pieces, bpeer, g_wide = lax.optimization_barrier((pieces, bpeer, g_wide))
+    g_peer = permute(g_wide, swap_core)
+    back = call(scan_forward, [((CHIPS, 2 * PIECE, STATE), f32)], 0, pieces, bmine, bpeer, mine, peer)
+    got = over(back, chips)
+    x2 = lax.optimization_barrier((x, back))[0]
     y_in = call(intra_forward, [((TOK, 2 * CH), f32)], 5, a_rate, dt, x2, b, c, us=3)
-    pieces, bpeer, y_in, g_wide = lax.optimization_barrier((pieces, bpeer, y_in, g_wide))
-    g_peer = permute(g_wide, swap_core)
-
-    got = over(call(scan_forward, [((CHIPS, 2 * PIECE, STATE), f32)], 0, pieces, bmine, bpeer, tot, peer), chips)
-    keep, send = call(core_forward, [half, half], 0, got, mine, peer, tot)
+    got, y_in = lax.optimization_barrier((got, y_in))
+    keep, send = call(core_forward, [half, half], 0, got, mine, peer)
     recv = permute(send, swap_core)
     out, rows, send = call(
         forward_out, [tokens, ((HALF, TOK), bf16), ((HALF, TOK), f32)], 0, keep, recv, c, y_in, us=2)
@@ -393,11 +396,11 @@
     s1, s2, s3 = permute(s[1], first_axis(1)), permute(s[2], first_axis(2)), permute(s[3], first_axis(3))
     s1, s2, s3, back = lax.optimization_barrier((s1, s2, s3, back))
     s = s[0] + s2 + s1 + s3
-    after, send = call(core_backward, [half, half], 0, back, bmine, bpeer, tot, peer)
+    after, send = call(core_backward, [half, half], 0, back, bmine, bpeer, mine, peer)
     recv2 = permute(send, swap_core)
     s = s[0] + permute(s[2], second_axis(2)) + permute(s[1], second_axis(1)) + permute(s[3], second_axis(3))
     s = over(s.reshape(NZ, 8, BLK), depth)
-    gi, gwr, grd = call(gradients, [tokens, narrow, narrow], 5, a_rate, dt, x2, b, c, gy, keep, recv, after, recv2, us=5)
+    gi, gwr, grd = call(gradients, [tokens, narrow, narrow], 10, a_rate, dt, x2, b, c, gy, keep, recv, after, recv2, us=5)
     s, gi = lax.optimization_barrier((s, gi))
     s = jnp.sum(s, axis=0)
     grad_w_out = call(place, [((8, D), f32)], 0, s, permute(s, x_axis(1)), permute(s, x_axis(2)), permute(s, x_axis(3)))

time: 110 us -> 108 us (0.982)
  blocking collectives: 34.3 us -> 14.1 us
  waiting for transfers between devices: 17 us -> 29.2 us
  starting transfers between devices: 29.4 us -> 35.6 us
  local copies, waits for them, and re-layouts: 2.95 us -> 4.08 us
    all_to_all x2 -> x1, blocking collectives: 34.3 us -> 14.1 us  [over(): return lax.all_to_all(v, 'seq', 0, 0, axis_index_groups=groups, tiled=True)]
    all_to_all x2 -> x3, waiting for transfers between devices: 3.94 us -> 14.5 us  [over(): return lax.all_to_all(v, 'seq', 0, 0, axis_index_groups=groups, tiled=True)]
    all_to_all x2 -> x3, starting transfers between devices: 15.3 us -> 21.9 us  [over(): return lax.all_to_all(v, 'seq', 0, 0, axis_index_groups=groups, tiled=True)]
    ppermute x15, waiting for transfers between devices: 13.1 us -> 14.6 us  [permute(): return lax.ppermute(v, BOTH, pairs)]
    unnamed x26, local copies, waits for them, and re-layouts: 2.92 us -> 4.04 us
  transfers between devices with their start and end apart: 17 -> 18, of which waited for: 12 -> 13; matrix products, arithmetic and copies ran while one was open for 1% -> 1% of each run, Pallas kernels for 16% -> 15%
where the time goes in v4:
time: 108 us
  starting transfers between devices  35.6 us (33%)
  waiting for transfers between devices  29.2 us (27%)
  Pallas kernels  23.1 us (21%)
  blocking collectives  14.1 us (13%)
  local copies, waits for them, and re-layouts  4.08 us (4%)
    pallas_call x12, Pallas kernels, call(): pl.pallas_call(kernel, out_shape=shapes, in_specs=[pl.BlockSpec(memory_sp...  23.1 us
    all_to_all x3, starting transfers between devices, over(): return lax.all_to_all(v, 'seq', 0, 0, axis_index_groups=groups, tiled=True)  21.9 us
    ppermute x15, waiting for transfers between devices, permute(): return lax.ppermute(v, BOTH, pairs)  14.6 us
    all_to_all x3, waiting for transfers between devices, over(): return lax.all_to_all(v, 'seq', 0, 0, axis_index_groups=groups, tiled=True)  14.5 us
    all_to_all x1, blocking collectives, over(): return lax.all_to_all(v, 'seq', 0, 0, axis_index_groups=groups, tiled=True)  14.1 us
    ppermute x15, starting transfers between devices, permute(): return lax.ppermute(v, BOTH, pairs)  13.7 us
    unnamed x26, local copies, waits for them, and re-layouts  4.04 us
  transfers between devices with their start and end apart: 18, of which 13 were waited for; matrix products, arithmetic and copies ran while one was open for 1% of the time, Pallas kernels for 15%

profile of v4, /device:TPU:32, one launch (start us, length us, event | category | flops | bytes accessed | tf_op | source)
XLA Modules:
  0.0 107.8 jit_solution(102490825608194230)
XLA Ops:
  0.6 3.3 %local_forward.1 = (f32[264,128]{1,0:T(8,128)}, f32[264,128]{1,0:T(8,128)}) custom-call(f32[8]{0:T(128)} %refs_0_.7, s32[8,256]{1,0:T(8,128)} %bitcast.39, bf16[256,512]{1,0:T(8,128)(2,1)} %bitcast.33, bf16[256,128]{1,0:T(8,128)(2,1)} %bitcast.36), custom_call_target="tpu_custom_call" | custom-call | flops 2000000000 | bytes 606240 | tf_op jit(solution)/shard_map/local_forward/pallas_call | solution.py:347
  3.9 0.1 collective-permute-start
  4.0 1.6 %collective-permute-done.refs_1_.refs_4_.refs_2_ = f32[264,128]{1,0:T(8,128)S(1)} collective-permute-done((f32[264,128]{1,0:T(8,128)}, f32[264,128]{1,0:T(8,128)S(1)}, u32[]{:S(2)}, u32[]{:S(2)}) %collective-permute-start) | collective-permute-done | bytes 135200 | tf_op jit(solution)/shard_map/ppermute | solution.py:43
  5.5 0.9 copy-done.4
  6.5 0.8 chip_forward.1
  7.2 11.4 %all-to-all-start = ((f32[32,1,1152]{2,1,0:T(1,128)}), f32[32,1,1152]{2,1,0:T(1,128)S(1)}, u32[]{:S(2)}, u32[]{:S(2)}) async-start(f32[32,1,1152]{2,1,0:T(1,128)} %chip_forward.1), calls=%async_computation | async-start | bytes 294912 | tf_op jit(solution)/shard_map/all_to_all | solution.py:367
  18.6 0.0 copy-start.5
  18.6 5.3 %local_backward.1 = (f32[256,128]{1,0:T(8,128)}, f32[256,128]{1,0:T(8,128)}, bf16[256,512]{1,0:T(8,128)(2,1)}, f32[256,2560]{1,0:T(8,128)}) custom-call(f32[8]{0:T(128)} %refs_0_.7, s32[8,256]{1,0:T(8,128)} %bitcast.40, bf16[256,128]{1,0:T(8,128)(2,1)} %bitcast.29, bf16[256,2560]{1,0:T(8,128)(2,1)} %bitcast.27, bf16[512,2560]{1,0:T(8,128)(2,1)} %refs_4_.1), custom_call_target="tpu_custom_call" | custom-call | flops 4000000000 | bytes 7151648 | tf_op jit(solution)/shard_map/local_backward/pallas_call | solution.py:347
  23.9 0.1 collective-permute-start.1
  24.0 1.5 %collective-permute-done.1.refs_2_ = f32[256,128]{1,0:T(8,128)S(1)} collective-permute-done((f32[256,128]{1,0:T(8,128)}, f32[256,128]{1,0:T(8,128)S(1)}, u32[]{:S(2)}, u32[]{:S(2)}) %collective-permute-start.1) | collective-permute-done | bytes 131104 | tf_op jit(solution)/shard_map/ppermute | solution.py:43
  25.5 3.3 %all-to-all-done.refs_0_ = f32[32,1,1152]{2,1,0:T(1,128)S(1)} async-done(((f32[32,1,1152]{2,1,0:T(1,128)}), f32[32,1,1152]{2,1,0:T(1,128)S(1)}, u32[]{:S(2)}, u32[]{:S(2)}) %all-to-all-start) | async-done | bytes 147488 | tf_op jit(solution)/shard_map/all_to_all | solution.py:367
  28.8 0.0 collective-permute-start.4
  28.8 0.0 copy-done.5
  28.8 0.9 copy-done.8
  29.7 0.8 scan_forward.1
  30.6 6.7 %all-to-all-start.1 = ((f32[32,16,128]{2,1,0:T(8,128)}), f32[32,16,128]{2,1,0:T(8,128)S(1)}, u32[]{:S(2)}, u32[]{:S(2)}) async-start(f32[32,16,128]{2,1,0:T(8,128)} %scan_forward.1), calls=%async_computation.1 | async-start | bytes 524288 | tf_op jit(solution)/shard_map/all_to_all | solution.py:367
  37.2 4.2 %intra_forward.1.refs_3_ = f32[256,1024]{1,0:T(8,128)} custom-call(f32[8]{0:T(128)} %refs_0_.7, s32[8,256]{1,0:T(8,128)} %bitcast.41, bf16[256,512]{1,0:T(8,128)(2,1)} %bitcast.34, bf16[256,128]{1,0:T(8,128)(2,1)} %bitcast.37, bf16[256,128]{1,0:T(8,128)(2,1)} %bitcast.30), custom_call_target="tpu_custom_call" | custom-call | flops 3000000000 | bytes 1450016 | tf_op jit(solution)/shard_map/intra_forward/pallas_call | solution.py:347
  41.5 0.0 copy-start.2
  41.5 8.4 %all-to-all-done.1.refs_0_.refs_1_ = f32[32,16,128]{2,1,0:T(8,128)S(1)} async-done(((f32[32,16,128]{2,1,0:T(8,128)}), f32[32,16,128]{2,1,0:T(8,128)S(1)}, u32[]{:S(2)}, u32[]{:S(2)}) %all-to-all-start.1) | async-done | bytes 262176 | tf_op jit(solution)/shard_map/all_to_all | solution.py:367
  49.9 0.9 copy-done.6
  50.9 0.0 copy-start.11
  50.9 0.1 collective-permute-start.2
  51.0 1.3 %collective-permute-done.2.refs_1_.refs_7_ = f32[256,128]{1,0:T(8,128)S(1)} collective-permute-done((f32[256,128]{1,0:T(8,128)S(1)}, f32[256,128]{1,0:T(8,128)S(1)}, u32[]{:S(2)}, u32[]{:S(2)}) %collective-permute-start.2) | collective-permute-done | bytes 131104 | tf_op jit(solution)/shard_map/ppermute | solution.py:43
  52.3 0.0 copy-done.2
  52.3 0.0 copy-done.3
  52.3 1.1 forward_out.1
  53.4 0.0 copy-done.11
  53.4 0.0 copy-done.1
  53.4 0.1 collective-permute-start.3
  53.5 1.4 %collective-permute-done.3.refs_1_ = f32[256,256]{1,0:T(8,128)S(1)} collective-permute-done((f32[256,256]{1,0:T(8,128)S(1)}, f32[256,256]{1,0:T(8,128)S(1)}, u32[]{:S(2)}, u32[]{:S(2)}) %collective-permute-start.3) | collective-permute-done | bytes 262176 | tf_op jit(solution)/shard_map/ppermute | solution.py:43
  54.9 0.0 collective-permute-done.4.refs_3_
  54.9 0.0 copy-done
  54.9 1.7 %partial_grad.1 = (f32[4,64,640]{2,1,0:T(8,128)S(1)}, f32[4,64,640]{2,1,0:T(8,128)S(1)}, f32[4,64,640]{2,1,0:T(8,128)S(1)}, f32[4,64,640]{2,1,0:T(8,128)S(1)}) custom-call(bf16[256,256]{1,0:T(8,128)(2,1)S(1)} %get-tuple-element.54.refs_0_, f32[256,256]{1,0:T(8,128)S(1)} %collective-permute-done.3.refs_1_, bf16[256,2560]{1,0:T(8,128)(2,1)S(1)} %bitcast.28, ...), custom_call_target="tpu_custom_call" | custom-call | flops 4000000000 | bytes 6946816 | tf_op jit(solution)/shard_map/partial_grad/pallas_call | solution.py:347
  56.6 3.1 %collective-permute-start.6 = (f32[4,64,640]{2,1,0:T(8,128)S(1)}, f32[4,64,640]{2,1,0:T(8,128)S(1)}, u32[]{:S(2)}, u32[]{:S(2)}) collective-permute-start(f32[4,64,640]{2,1,0:T(8,128)S(1)} %get-tuple-element.59), channel_id=1, source_target_pairs={{0,2},{1,3},{2,0},{3,1},{4,20},{5,21},{6,22},{7,23},{8,10},{9,11},... | collective-permute-start | bytes 1966088 | tf_op jit(solution)/shard_map/ppermute | solution.py:43
  59.7 1.2 %collective-permute-start.7 = (f32[4,64,640]{2,1,0:T(8,128)S(1)}, f32[4,64,640]{2,1,0:T(8,128)S(1)}, u32[]{:S(2)}, u32[]{:S(2)}) collective-permute-start(f32[4,64,640]{2,1,0:T(8,128)S(1)} %get-tuple-element.60), channel_id=1, source_target_pairs={{0,3},{1,0},{2,1},{3,2},{4,28},{5,29},{6,30},{7,31},{8,11},{9,8},{... | collective-permute-start | bytes 1966088 | tf_op jit(solution)/shard_map/ppermute | solution.py:43
  60.9 0.9 collective-permute-start.5
  61.8 0.1 scan_backward.1
  61.8 0.0 copy-start.9
  61.8 14.1 %all_to_all.20.refs_0_ = f32[32,8,128]{2,1,0:T(8,128)S(1)} all-to-all(f32[32,8,128]{2,1,0:T(8,128)S(1)} %scan_backward.1), channel_id=1, replica_groups={{0,8,16,24,32,40,48,56,64,72,80,88,96,104,112,120,128,136,144,152,160,1..., dimensions={0} | all-to-all | bytes 262144 | tf_op jit(solution)/shard_map/all_to_all | solution.py:367
  76.0 0.0 collective-permute-done.6
  76.0 0.0 collective-permute-done.7
  76.0 0.0 collective-permute-done.5
  76.0 0.2 add_add_fusion
  76.2 1.2 %collective-permute-start.8 = (f32[64,640]{1,0:T(8,128)S(1)}, f32[64,640]{1,0:T(8,128)S(1)}, u32[]{:S(2)}, u32[]{:S(2)}) collective-permute-start(f32[64,640]{1,0:T(8,128)S(1)} %get-tuple-element.75), channel_id=1, source_target_pairs={{0,16},{1,17},{2,18},{3,19},{4,6},{5,7},{6,4},{7,5},{8,24},{9,25},... | collective-permute-start | bytes 491528 | tf_op jit(solution)/shard_map/ppermute | solution.py:43
  77.4 2.2 %collective-permute-start.10 = (f32[64,640]{1,0:T(8,128)S(1)}, f32[64,640]{1,0:T(8,128)S(1)}, u32[]{:S(2)}, u32[]{:S(2)}) collective-permute-start(f32[64,640]{1,0:T(8,128)S(1)} %get-tuple-element.76), channel_id=1, source_target_pairs={{0,24},{1,25},{2,26},{3,27},{4,7},{5,4},{6,5},{7,6},{8,0},{9,1},{1... | collective-permute-start | bytes 491528 | tf_op jit(solution)/shard_map/ppermute | solution.py:43
  79.6 0.0 collective-permute-start.9
  79.7 0.6 copy-done.10
  80.4 1.2 %collective-permute-start.11 = (f32[256,128]{1,0:T(8,128)S(1)}, f32[256,128]{1,0:T(8,128)S(1)}, u32[]{:S(2)}, u32[]{:S(2)}) collective-permute-start(f32[256,128]{1,0:T(8,128)S(1)} %get-tuple-element.69), channel_id=1, source_target_pairs={{0,4},{1,5},{2,6},{3,7},{4,0},{5,1},{6,2},{7,3},{8,12},{9,13},{10,... | collective-permute-start | bytes 393224 | tf_op jit(solution)/shard_map/ppermute | solution.py:43
  81.5 1.6 %collective-permute-done.8 = f32[64,640]{1,0:T(8,128)S(1)} collective-permute-done((f32[64,640]{1,0:T(8,128)S(1)}, f32[64,640]{1,0:T(8,128)S(1)}, u32[]{:S(2)}, u32[]{:S(2)}) %collective-permute-start.8) | collective-permute-done | bytes 163872 | tf_op jit(solution)/shard_map/ppermute | solution.py:43
  83.1 0.5 collective-permute-done.10
  83.6 2.6 %collective-permute-done.9 = f32[64,640]{1,0:T(8,128)S(1)} collective-permute-done((f32[64,640]{1,0:T(8,128)S(1)}, f32[64,640]{1,0:T(8,128)S(1)}, u32[]{:S(2)}, u32[]{:S(2)}) %collective-permute-start.9) | collective-permute-done | bytes 163872 | tf_op jit(solution)/shard_map/ppermute | solution.py:43
  86.2 0.7 fusion.3
  86.9 3.9 %all-to-all-start.3 = ((f32[8,8,640]{2,1,0:T(8,128)}), f32[8,8,640]{2,1,0:T(8,128)S(1)}, u32[]{:S(2)}, u32[]{:S(2)}) async-start(f32[8,8,640]{2,1,0:T(8,128)} %fusion.3), calls=%async_computation.3 | async-start | bytes 327680 | tf_op jit(solution)/shard_map/all_to_all | solution.py:367
  90.8 0.0 collective-permute-done.11.refs_9_
  90.8 0.6 copy-done.12
  91.5 5.1 %gradients.1 = (bf16[256,512]{1,0:T(8,128)(2,1)}, bf16[256,128]{1,0:T(8,128)(2,1)}, bf16[256,128]{1,0:T(8,128)(2,1)}) custom-call(f32[8]{0:T(128)} %refs_0_.7, s32[8,256]{1,0:T(8,128)} %bitcast.42, bf16[256,512]{1,0:T(8,128)(2,1)} %bitcast.35, bf16[256,128]{1,0:T(8,128)(2,1)} %bitcast.38, bf16[256,128]{1,0:T(8,128)(2,1)} %bitcast.31, ...), custom_call_target="tpu_custom_call" | custom-call | flops 5000000000 | bytes 1581088 | tf_op jit(solution)/shard_map/gradients/pallas_call | solution.py:347
  96.6 2.8 %all-to-all-done.3 = f32[8,8,640]{2,1,0:T(8,128)S(1)} async-done(((f32[8,8,640]{2,1,0:T(8,128)}), f32[8,8,640]{2,1,0:T(8,128)S(1)}, u32[]{:S(2)}, u32[]{:S(2)}) %all-to-all-start.3) | async-done | bytes 163872 | tf_op jit(solution)/shard_map/all_to_all | solution.py:367
  99.4 1.8 %collective-permute-start.14 = (f32[8,640]{1,0:T(8,128)S(1)}, f32[8,640]{1,0:T(8,128)S(1)}, u32[]{:S(2)}, u32[]{:S(2)}) collective-permute-start(f32[8,640]{1,0:T(8,128)S(1)} %reduce_sum.9.refs_0_), channel_id=1, source_target_pairs={{0,3},{1,0},{2,1},{3,2},{4,7},{5,4},{6,5},{7,6},{8,11},{9,8},{10,9... | collective-permute-start | bytes 61448 | tf_op jit(solution)/shard_map/ppermute | solution.py:43
  101.3 0.9 collective-permute-start.13
  102.1 0.8 collective-permute-start.12
  102.9 0.4 collective-permute-done.14.refs_3_
  103.3 3.2 %collective-permute-done.13.refs_2_ = f32[8,640]{1,0:T(8,128)S(1)} collective-permute-done((f32[8,640]{1,0:T(8,128)S(1)}, f32[8,640]{1,0:T(8,128)S(1)}, u32[]{:S(2)}, u32[]{:S(2)}) %collective-permute-start.13) | collective-permute-done | bytes 20512 | tf_op jit(solution)/shard_map/ppermute | solution.py:43
  106.5 0.6 collective-permute-done.12.refs_1_
  107.1 0.6 place.1
  (15 shorter events, 0.2 us)
Async XLA Ops:
  3.9 1.7 %collective-permute-start = (f32[264,128]{1,0:T(8,128)}, f32[264,128]{1,0:T(8,128)S(1)}, u32[]{:S(2)}, u32[]{:S(2)}) collective-permute-start(f32[264,128]{1,0:T(8,128)} %get-tuple-element.41), channel_id=1, source_target_pairs={{0,4},{1,5},{2,6},{3,7},{4,0},{5,1},{6,2},{7,3},{8,12},{9,13},{10,... | collective-permute-start | bytes 405512 | tf_op jit(solution)/shard_map/ppermute | solution.py:43
  5.5 0.9 copy-start.4
  7.2 21.6 %all-to-all-start = ((f32[32,1,1152]{2,1,0:T(1,128)}), f32[32,1,1152]{2,1,0:T(1,128)S(1)}, u32[]{:S(2)}, u32[]{:S(2)}) async-start(f32[32,1,1152]{2,1,0:T(1,128)} %chip_forward.1), calls=%async_computation | async-start | bytes 294912 | tf_op jit(solution)/shard_map/all_to_all | solution.py:367
  18.6 10.2 %copy-start.5 = (f32[264,128]{1,0:T(8,128)S(1)}, f32[264,128]{1,0:T(8,128)}, u32[]{:S(2)}) copy-start(f32[264,128]{1,0:T(8,128)} %get-tuple-element.40.refs_0_.refs_3_.refs_1_) | copy-start | bytes 405508
  23.9 1.6 %collective-permute-start.1 = (f32[256,128]{1,0:T(8,128)}, f32[256,128]{1,0:T(8,128)S(1)}, u32[]{:S(2)}, u32[]{:S(2)}) collective-permute-start(f32[256,128]{1,0:T(8,128)} %get-tuple-element.43), channel_id=1, source_target_pairs={{0,4},{1,5},{2,6},{3,7},{4,0},{5,1},{6,2},{7,3},{8,12},{9,13},{10,... | collective-permute-start | bytes 393224 | tf_op jit(solution)/shard_map/ppermute | solution.py:43
  28.8 26.1 %collective-permute-start.4 = (f32[256,2560]{1,0:T(8,128)}, f32[256,2560]{1,0:T(8,128)S(1)}, u32[]{:S(2)}, u32[]{:S(2)}) collective-permute-start(f32[256,2560]{1,0:T(8,128)} %get-tuple-element.56), channel_id=1, source_target_pairs={{0,4},{1,5},{2,6},{3,7},{4,0},{5,1},{6,2},{7,3},{8,12},{9,13},{10,... | collective-permute-start | bytes 7864328 | tf_op jit(solution)/shard_map/ppermute | solution.py:43
  28.8 0.9 copy-start.8
  30.6 19.3 %all-to-all-start.1 = ((f32[32,16,128]{2,1,0:T(8,128)}), f32[32,16,128]{2,1,0:T(8,128)S(1)}, u32[]{:S(2)}, u32[]{:S(2)}) async-start(f32[32,16,128]{2,1,0:T(8,128)} %scan_forward.1), calls=%async_computation.1 | async-start | bytes 524288 | tf_op jit(solution)/shard_map/all_to_all | solution.py:367
  41.5 10.9 %copy-start.2 = (bf16[1,256,128]{2,1,0:T(8,128)(2,1)S(1)}, bf16[1,256,128]{2,1,0:T(8,128)(2,1)}, u32[]{:S(2)}) copy-start(bf16[1,256,128]{2,1,0:T(8,128)(2,1)} %param.9) | copy-start | bytes 196612
  49.9 0.9 copy-start.6
  50.8 1.5 %copy-start.3 = (f32[256,1024]{1,0:T(8,128)S(1)}, f32[256,1024]{1,0:T(8,128)}, u32[]{:S(2)}) copy-start(f32[256,1024]{1,0:T(8,128)} %intra_forward.1.refs_3_) | copy-start | bytes 3145732
  50.9 2.5 %copy-start.11 = (f32[256,128]{1,0:T(8,128)}, f32[256,128]{1,0:T(8,128)S(1)}, u32[]{:S(2)}) copy-start(f32[256,128]{1,0:T(8,128)S(1)} %get-tuple-element.50.refs_0_.refs_6_) | copy-start | bytes 393220
  50.9 1.4 %collective-permute-start.2 = (f32[256,128]{1,0:T(8,128)S(1)}, f32[256,128]{1,0:T(8,128)S(1)}, u32[]{:S(2)}, u32[]{:S(2)}) collective-permute-start(f32[256,128]{1,0:T(8,128)S(1)} %get-tuple-element.51), channel_id=1, source_target_pairs={{0,4},{1,5},{2,6},{3,7},{4,0},{5,1},{6,2},{7,3},{8,12},{9,13},{10,... | collective-permute-start | bytes 393224 | tf_op jit(solution)/shard_map/ppermute | solution.py:43
  52.3 1.1 %copy-start.1 = (f32[256,128]{1,0:T(8,128)}, f32[256,128]{1,0:T(8,128)S(1)}, u32[]{:S(2)}) copy-start(f32[256,128]{1,0:T(8,128)S(1)} %collective-permute-done.2.refs_1_.refs_7_) | copy-start | bytes 393220
  52.3 2.6 %copy-start = (bf16[1,256,2560]{2,1,0:T(8,128)(2,1)S(1)}, bf16[1,256,2560]{2,1,0:T(8,128)(2,1)}, u32[]{:S(2)}) copy-start(bf16[1,256,2560]{2,1,0:T(8,128)(2,1)} %param.13) | copy-start | bytes 3932164
  53.4 1.5 %collective-permute-start.3 = (f32[256,256]{1,0:T(8,128)S(1)}, f32[256,256]{1,0:T(8,128)S(1)}, u32[]{:S(2)}, u32[]{:S(2)}) collective-permute-start(f32[256,256]{1,0:T(8,128)S(1)} %get-tuple-element.55), channel_id=1, source_target_pairs={{0,4},{1,5},{2,6},{3,7},{4,0},{5,1},{6,2},{7,3},{8,12},{9,13},{10,... | collective-permute-start | bytes 786440 | tf_op jit(solution)/shard_map/ppermute | solution.py:43
  56.6 19.3 %collective-permute-start.6 = (f32[4,64,640]{2,1,0:T(8,128)S(1)}, f32[4,64,640]{2,1,0:T(8,128)S(1)}, u32[]{:S(2)}, u32[]{:S(2)}) collective-permute-start(f32[4,64,640]{2,1,0:T(8,128)S(1)} %get-tuple-element.59), channel_id=1, source_target_pairs={{0,2},{1,3},{2,0},{3,1},{4,20},{5,21},{6,22},{7,23},{8,10},{9,11},... | collective-permute-start | bytes 1966088 | tf_op jit(solution)/shard_map/ppermute | solution.py:43
  59.7 16.2 %collective-permute-start.7 = (f32[4,64,640]{2,1,0:T(8,128)S(1)}, f32[4,64,640]{2,1,0:T(8,128)S(1)}, u32[]{:S(2)}, u32[]{:S(2)}) collective-permute-start(f32[4,64,640]{2,1,0:T(8,128)S(1)} %get-tuple-element.60), channel_id=1, source_target_pairs={{0,3},{1,0},{2,1},{3,2},{4,28},{5,29},{6,30},{7,31},{8,11},{9,8},{... | collective-permute-start | bytes 1966088 | tf_op jit(solution)/shard_map/ppermute | solution.py:43
  60.9 15.1 %collective-permute-start.5 = (f32[4,64,640]{2,1,0:T(8,128)S(1)}, f32[4,64,640]{2,1,0:T(8,128)S(1)}, u32[]{:S(2)}, u32[]{:S(2)}) collective-permute-start(f32[4,64,640]{2,1,0:T(8,128)S(1)} %get-tuple-element.58), channel_id=1, source_target_pairs={{0,1},{1,2},{2,3},{3,0},{4,12},{5,13},{6,14},{7,15},{8,9},{9,10},{... | collective-permute-start | bytes 1966088 | tf_op jit(solution)/shard_map/ppermute | solution.py:43
  61.8 17.8 %copy-start.7 = (f32[264,128]{1,0:T(8,128)S(1)}, f32[264,128]{1,0:T(8,128)}, u32[]{:S(2)}) copy-start(f32[264,128]{1,0:T(8,128)} %get-tuple-element.40.refs_0_.refs_3_.refs_1_) | copy-start | bytes 405508
  61.8 17.8 %copy-start.9 = (f32[256,128]{1,0:T(8,128)S(1)}, f32[256,128]{1,0:T(8,128)}, u32[]{:S(2)}) copy-start(f32[256,128]{1,0:T(8,128)} %get-tuple-element.46.refs_1_) | copy-start | bytes 393220
  76.2 6.9 %collective-permute-start.8 = (f32[64,640]{1,0:T(8,128)S(1)}, f32[64,640]{1,0:T(8,128)S(1)}, u32[]{:S(2)}, u32[]{:S(2)}) collective-permute-start(f32[64,640]{1,0:T(8,128)S(1)} %get-tuple-element.75), channel_id=1, source_target_pairs={{0,16},{1,17},{2,18},{3,19},{4,6},{5,7},{6,4},{7,5},{8,24},{9,25},... | collective-permute-start | bytes 491528 | tf_op jit(solution)/shard_map/ppermute | solution.py:43
  77.4 6.2 %collective-permute-start.10 = (f32[64,640]{1,0:T(8,128)S(1)}, f32[64,640]{1,0:T(8,128)S(1)}, u32[]{:S(2)}, u32[]{:S(2)}) collective-permute-start(f32[64,640]{1,0:T(8,128)S(1)} %get-tuple-element.76), channel_id=1, source_target_pairs={{0,24},{1,25},{2,26},{3,27},{4,7},{5,4},{6,5},{7,6},{8,0},{9,1},{1... | collective-permute-start | bytes 491528 | tf_op jit(solution)/shard_map/ppermute | solution.py:43
  79.6 6.5 %collective-permute-start.9 = (f32[64,640]{1,0:T(8,128)S(1)}, f32[64,640]{1,0:T(8,128)S(1)}, u32[]{:S(2)}, u32[]{:S(2)}) collective-permute-start(f32[64,640]{1,0:T(8,128)S(1)} %get-tuple-element.77), channel_id=1, source_target_pairs={{0,8},{1,9},{2,10},{3,11},{4,5},{5,6},{6,7},{7,4},{8,16},{9,17},{1... | collective-permute-start | bytes 491528 | tf_op jit(solution)/shard_map/ppermute | solution.py:43
  79.7 0.7 copy-start.10
  80.4 10.4 %collective-permute-start.11 = (f32[256,128]{1,0:T(8,128)S(1)}, f32[256,128]{1,0:T(8,128)S(1)}, u32[]{:S(2)}, u32[]{:S(2)}) collective-permute-start(f32[256,128]{1,0:T(8,128)S(1)} %get-tuple-element.69), channel_id=1, source_target_pairs={{0,4},{1,5},{2,6},{3,7},{4,0},{5,1},{6,2},{7,3},{8,12},{9,13},{10,... | collective-permute-start | bytes 393224 | tf_op jit(solution)/shard_map/ppermute | solution.py:43
  86.9 12.5 %all-to-all-start.3 = ((f32[8,8,640]{2,1,0:T(8,128)}), f32[8,8,640]{2,1,0:T(8,128)S(1)}, u32[]{:S(2)}, u32[]{:S(2)}) async-start(f32[8,8,640]{2,1,0:T(8,128)} %fusion.3), calls=%async_computation.3 | async-start | bytes 327680 | tf_op jit(solution)/shard_map/all_to_all | solution.py:367
  90.8 0.7 copy-start.12
  99.4 3.9 %collective-permute-start.14 = (f32[8,640]{1,0:T(8,128)S(1)}, f32[8,640]{1,0:T(8,128)S(1)}, u32[]{:S(2)}, u32[]{:S(2)}) collective-permute-start(f32[8,640]{1,0:T(8,128)S(1)} %reduce_sum.9.refs_0_), channel_id=1, source_target_pairs={{0,3},{1,0},{2,1},{3,2},{4,7},{5,4},{6,5},{7,6},{8,11},{9,8},{10,9... | collective-permute-start | bytes 61448 | tf_op jit(solution)/shard_map/ppermute | solution.py:43
  101.3 5.3 %collective-permute-start.13 = (f32[8,640]{1,0:T(8,128)S(1)}, f32[8,640]{1,0:T(8,128)S(1)}, u32[]{:S(2)}, u32[]{:S(2)}) collective-permute-start(f32[8,640]{1,0:T(8,128)S(1)} %reduce_sum.9.refs_0_), channel_id=1, source_target_pairs={{0,2},{1,3},{2,0},{3,1},{4,6},{5,7},{6,4},{7,5},{8,10},{9,11},{10,... | collective-permute-start | bytes 61448 | tf_op jit(solution)/shard_map/ppermute | solution.py:43
  102.1 5.0 %collective-permute-start.12 = (f32[8,640]{1,0:T(8,128)S(1)}, f32[8,640]{1,0:T(8,128)S(1)}, u32[]{:S(2)}, u32[]{:S(2)}) collective-permute-start(f32[8,640]{1,0:T(8,128)S(1)} %reduce_sum.9.refs_0_), channel_id=1, source_target_pairs={{0,1},{1,2},{2,3},{3,0},{4,5},{5,6},{6,7},{7,4},{8,9},{9,10},{10,1... | collective-permute-start | bytes 61448 | tf_op jit(solution)/shard_map/ppermute | solution.py:43

commit v5 on v4

--- a/solution.py
+++ b/solution.py
@@ -352,9 +352,9 @@
         out_specs=[pl.BlockSpec(memory_space=pltpu.VMEM)] * len(shapes),
         scratch_shapes=scratch,
         cost_estimate=pl.CostEstimate(flops=us * 1_000_000_000, bytes_accessed=moved, transcendentals=0),
-        compiler_params=pltpu.CompilerParams(vmem_limit_bytes=(54 << 20) if fetch else (8 << 20)),
+        compiler_params=pltpu.CompilerParams(vmem_limit_bytes=(12 << 20) if fetch else (4 << 20)),
         name=body.__name__,
-    )(*args)
+    )(*[pltpu.with_memory_space_constraint(a, pltpu.HBM) if n < fetch else a for n, a in enumerate(args)])
     return got if len(got) > 1 else got[0]
 
 
@@ -400,7 +400,7 @@
     recv2 = permute(send, swap_core)
     s = s[0] + permute(s[2], second_axis(2)) + permute(s[1], second_axis(1)) + permute(s[3], second_axis(3))
     s = over(s.reshape(NZ, 8, BLK), depth)
-    gi, gwr, grd = call(gradients, [tokens, narrow, narrow], 10, a_rate, dt, x2, b, c, gy, keep, recv, after, recv2, us=5)
+    gi, gwr, grd = call(gradients, [tokens, narrow, narrow], 5, a_rate, dt, x2, b, c, gy, keep, recv, after, recv2, us=5)
     s, gi = lax.optimization_barrier((s, gi))
     s = jnp.sum(s, axis=0)
     grad_w_out = call(place, [((8, D), f32)], 0, s, permute(s, x_axis(1)), permute(s, x_axis(2)), permute(s, x_axis(3)))

time: 108 us -> 106 us (0.981)
  waiting for transfers between devices: 29.2 us -> 31.5 us
  Pallas kernels: 23.1 us -> 21.2 us
  local copies, waits for them, and re-layouts: 4.08 us -> 2.66 us
  starting transfers between devices: 35.6 us -> 34.3 us
    all_to_all x3, waiting for transfers between devices: 14.5 us -> 16.7 us  [over(): return lax.all_to_all(v, 'seq', 0, 0, axis_index_groups=groups, tiled=True)]
    pallas_call x12, Pallas kernels: 23.1 us -> 21.2 us  [call(): pl.pallas_call(kernel, out_shape=shapes, in_specs=[pl.BlockSpec(memory_sp...]
    unnamed x26, local copies, waits for them, and re-layouts: 4.04 us -> 2.62 us
    all_to_all x3, starting transfers between devices: 21.9 us -> 20.6 us  [over(): return lax.all_to_all(v, 'seq', 0, 0, axis_index_groups=groups, tiled=True)]
  transfers between devices with their start and end apart: 18 -> 18, of which waited for: 13 -> 13; matrix products, arithmetic and copies ran while one was open for 1% -> 1% of each run, Pallas kernels for 15% -> 13%
where the time goes in v5:
time: 106 us; the launch traced here: 105 us
  starting transfers between devices  34.3 us (32%)
  waiting for transfers between devices  31.5 us (30%)
  Pallas kernels  21.2 us (20%)
  blocking collectives  14.1 us (13%)
  local copies, waits for them, and re-layouts  2.66 us (3%)
    pallas_call x12, Pallas kernels, call(): pl.pallas_call(kernel, out_shape=shapes, in_specs=[pl.BlockSpec(memory_sp...  21.2 us
    all_to_all x3, starting transfers between devices, over(): return lax.all_to_all(v, 'seq', 0, 0, axis_index_groups=groups, tiled=True)  20.6 us
    all_to_all x3, waiting for transfers between devices, over(): return lax.all_to_all(v, 'seq', 0, 0, axis_index_groups=groups, tiled=True)  16.7 us
    ppermute x15, waiting for transfers between devices, permute(): return lax.ppermute(v, BOTH, pairs)  14.8 us
    all_to_all x1, blocking collectives, over(): return lax.all_to_all(v, 'seq', 0, 0, axis_index_groups=groups, tiled=True)  14.1 us
    ppermute x15, starting transfers between devices, permute(): return lax.ppermute(v, BOTH, pairs)  13.7 us
    unnamed x26, local copies, waits for them, and re-layouts  2.62 us
  transfers between devices with their start and end apart: 18, of which 13 were waited for; matrix products, arithmetic and copies ran while one was open for 1% of the time, Pallas kernels for 13%

profile of v5, /device:TPU:32, one launch (start us, length us, event | category | flops | bytes accessed | tf_op | source)
XLA Modules:
  0.0 105.5 jit_solution(737964976198738829)
XLA Ops:
  0.6 2.6 %local_forward.1 = (f32[264,128]{1,0:T(8,128)S(1)}, f32[264,128]{1,0:T(8,128)S(1)}) custom-call(f32[8]{0:T(128)} %refs_0_.7, s32[8,256]{1,0:T(8,128)} %bitcast.39, bf16[256,512]{1,0:T(8,128)(2,1)} %bitcast.33, bf16[256,128]{1,0:T(8,128)(2,1)} %bitcast.36), custom_call_target="tpu_custom_call" | custom-call | flops 2000000000 | bytes 606240 | tf_op jit(solution)/shard_map/local_forward/pallas_call | solution.py:347
  3.2 0.0 copy-start.4
  3.2 0.1 collective-permute-start
  3.3 1.3 %collective-permute-done.refs_1_.refs_4_.refs_2_ = f32[264,128]{1,0:T(8,128)S(1)} collective-permute-done((f32[264,128]{1,0:T(8,128)S(1)}, f32[264,128]{1,0:T(8,128)S(1)}, u32[]{:S(2)}, u32[]{:S(2)}) %collective-permute-start) | collective-permute-done | bytes 135200 | tf_op jit(solution)/shard_map/ppermute | solution.py:43
  4.6 0.8 chip_forward.1
  5.4 11.4 %all-to-all-start = ((f32[32,1,1152]{2,1,0:T(1,128)}), f32[32,1,1152]{2,1,0:T(1,128)S(1)}, u32[]{:S(2)}, u32[]{:S(2)}) async-start(f32[32,1,1152]{2,1,0:T(1,128)} %chip_forward.1), calls=%async_computation | async-start | bytes 294912 | tf_op jit(solution)/shard_map/all_to_all | solution.py:367
  16.8 3.6 %local_backward.1 = (f32[256,128]{1,0:T(8,128)S(1)}, f32[256,128]{1,0:T(8,128)S(1)}, bf16[256,512]{1,0:T(8,128)(2,1)S(1)}, f32[256,2560]{1,0:T(8,128)S(1)}) custom-call(f32[8]{0:T(128)} %refs_0_.7, s32[8,256]{1,0:T(8,128)} %bitcast.40, bf16[256,128]{1,0:T(8,128)(2,1)} %bitcast.29, bf16[256,2560]{1,0:T(8,128)(2,1)} %bitcast.27, bf16[512,2560]{1,0:T(8,128)(2,1)} %refs_4_.1), custom_call_target="tpu_custom_call" | custom-call | flops 4000000000 | bytes 7151648 | tf_op jit(solution)/shard_map/local_backward/pallas_call | solution.py:347
  20.4 0.0 copy-start.11
  20.4 0.7 copy-done.11
  21.1 0.0 collective-permute-start.1
  21.1 1.3 %collective-permute-done.1.refs_2_ = f32[256,128]{1,0:T(8,128)S(1)} collective-permute-done((f32[256,128]{1,0:T(8,128)S(1)}, f32[256,128]{1,0:T(8,128)S(1)}, u32[]{:S(2)}, u32[]{:S(2)}) %collective-permute-start.1) | collective-permute-done | bytes 131104 | tf_op jit(solution)/shard_map/ppermute | solution.py:43
  22.4 4.6 %all-to-all-done.refs_0_ = f32[32,1,1152]{2,1,0:T(1,128)S(1)} async-done(((f32[32,1,1152]{2,1,0:T(1,128)}), f32[32,1,1152]{2,1,0:T(1,128)S(1)}, u32[]{:S(2)}, u32[]{:S(2)}) %all-to-all-start) | async-done | bytes 147488 | tf_op jit(solution)/shard_map/all_to_all | solution.py:367
  27.0 0.0 collective-permute-start.4
  27.0 0.0 copy-done.4
  27.0 0.8 scan_forward.1
  27.8 5.4 %all-to-all-start.1 = ((f32[32,16,128]{2,1,0:T(8,128)}), f32[32,16,128]{2,1,0:T(8,128)S(1)}, u32[]{:S(2)}, u32[]{:S(2)}) async-start(f32[32,16,128]{2,1,0:T(8,128)} %scan_forward.1), calls=%async_computation.1 | async-start | bytes 524288 | tf_op jit(solution)/shard_map/all_to_all | solution.py:367
  33.2 3.2 %intra_forward.1.refs_3_ = f32[256,1024]{1,0:T(8,128)S(1)} custom-call(f32[8]{0:T(128)} %refs_0_.7, s32[8,256]{1,0:T(8,128)} %bitcast.41, bf16[256,512]{1,0:T(8,128)(2,1)} %bitcast.34, bf16[256,128]{1,0:T(8,128)(2,1)} %bitcast.37, bf16[256,128]{1,0:T(8,128)(2,1)} %bitcast.30), custom_call_target="tpu_custom_call" | custom-call | flops 3000000000 | bytes 1450016 | tf_op jit(solution)/shard_map/intra_forward/pallas_call | solution.py:347
  36.4 0.0 copy-done.7
  36.5 0.0 copy-start.2
  36.5 1.0 copy-done.2
  37.4 8.4 %all-to-all-done.1.refs_0_.refs_1_ = f32[32,16,128]{2,1,0:T(8,128)S(1)} async-done(((f32[32,16,128]{2,1,0:T(8,128)}), f32[32,16,128]{2,1,0:T(8,128)S(1)}, u32[]{:S(2)}, u32[]{:S(2)}) %all-to-all-start.1) | async-done | bytes 262176 | tf_op jit(solution)/shard_map/all_to_all | solution.py:367
  45.9 0.9 copy-done.5
  46.8 0.0 copy-start.9
  46.9 0.1 collective-permute-start.2
  47.0 1.3 %collective-permute-done.2.refs_1_.refs_7_ = f32[256,128]{1,0:T(8,128)S(1)} collective-permute-done((f32[256,128]{1,0:T(8,128)S(1)}, f32[256,128]{1,0:T(8,128)S(1)}, u32[]{:S(2)}, u32[]{:S(2)}) %collective-permute-start.2) | collective-permute-done | bytes 131104 | tf_op jit(solution)/shard_map/ppermute | solution.py:43
  48.3 0.0 copy-done.1
  48.3 0.0 copy-done.3
  48.3 1.1 %forward_out.1 = (bf16[256,512]{1,0:T(8,128)(2,1)}, bf16[256,256]{1,0:T(8,128)(2,1)S(1)}, f32[256,256]{1,0:T(8,128)S(1)}) custom-call(f32[256,128]{1,0:T(8,128)S(1)} %get-tuple-element.50.refs_0_.refs_6_, f32[256,128]{1,0:T(8,128)S(1)} %collective-permute-done.2.refs_1_.refs_7_, bf16[256,128]{1,0:T(8,128)(2,1)S(1)} %bitcast.32, f32[256,1024]{1,0:T(8,128)S(1)} %copy-done.3), custom_call_target="tpu_custom_call" | custom-call | flops 2000000000 | bytes 2031616 | tf_op jit(solution)/shard_map/forward_out/pallas_call | solution.py:347
  49.4 0.0 copy-done.9
  49.4 0.1 collective-permute-start.3
  49.5 1.4 %collective-permute-done.3.refs_1_ = f32[256,256]{1,0:T(8,128)S(1)} collective-permute-done((f32[256,256]{1,0:T(8,128)S(1)}, f32[256,256]{1,0:T(8,128)S(1)}, u32[]{:S(2)}, u32[]{:S(2)}) %collective-permute-start.3) | collective-permute-done | bytes 262176 | tf_op jit(solution)/shard_map/ppermute | solution.py:43
  50.9 0.0 collective-permute-done.4.refs_3_
  50.9 3.4 %partial_grad.1 = (f32[4,64,640]{2,1,0:T(8,128)S(1)}, f32[4,64,640]{2,1,0:T(8,128)S(1)}, f32[4,64,640]{2,1,0:T(8,128)S(1)}, f32[4,64,640]{2,1,0:T(8,128)S(1)}) custom-call(bf16[256,256]{1,0:T(8,128)(2,1)S(1)} %get-tuple-element.54.refs_0_, f32[256,256]{1,0:T(8,128)S(1)} %collective-permute-done.3.refs_1_, bf16[256,2560]{1,0:T(8,128)(2,1)S(1)} %bitcast.28, ...), custom_call_target="tpu_custom_call" | custom-call | flops 4000000000 | bytes 6946816 | tf_op jit(solution)/shard_map/partial_grad/pallas_call | solution.py:347
  54.3 3.1 %collective-permute-start.6 = (f32[4,64,640]{2,1,0:T(8,128)S(1)}, f32[4,64,640]{2,1,0:T(8,128)S(1)}, u32[]{:S(2)}, u32[]{:S(2)}) collective-permute-start(f32[4,64,640]{2,1,0:T(8,128)S(1)} %get-tuple-element.59), channel_id=1, source_target_pairs={{0,2},{1,3},{2,0},{3,1},{4,20},{5,21},{6,22},{7,23},{8,10},{9,11},... | collective-permute-start | bytes 1966088 | tf_op jit(solution)/shard_map/ppermute | solution.py:43
  57.4 1.1 %collective-permute-start.7 = (f32[4,64,640]{2,1,0:T(8,128)S(1)}, f32[4,64,640]{2,1,0:T(8,128)S(1)}, u32[]{:S(2)}, u32[]{:S(2)}) collective-permute-start(f32[4,64,640]{2,1,0:T(8,128)S(1)} %get-tuple-element.60), channel_id=1, source_target_pairs={{0,3},{1,0},{2,1},{3,2},{4,28},{5,29},{6,30},{7,31},{8,11},{9,8},{... | collective-permute-start | bytes 1966088 | tf_op jit(solution)/shard_map/ppermute | solution.py:43
  58.6 0.9 collective-permute-start.5
  59.5 0.1 scan_backward.1
  59.5 14.1 %all_to_all.20.refs_0_ = f32[32,8,128]{2,1,0:T(8,128)S(1)} all-to-all(f32[32,8,128]{2,1,0:T(8,128)S(1)} %scan_backward.1), channel_id=1, replica_groups={{0,8,16,24,32,40,48,56,64,72,80,88,96,104,112,120,128,136,144,152,160,1..., dimensions={0} | all-to-all | bytes 262144 | tf_op jit(solution)/shard_map/all_to_all | solution.py:367
  73.7 0.0 collective-permute-done.6
  73.7 0.0 collective-permute-done.7
  73.7 0.0 collective-permute-done.5
  73.7 0.2 add_add_fusion
  73.9 0.0 copy-start.10
  73.9 1.2 %collective-permute-start.8 = (f32[64,640]{1,0:T(8,128)S(1)}, f32[64,640]{1,0:T(8,128)S(1)}, u32[]{:S(2)}, u32[]{:S(2)}) collective-permute-start(f32[64,640]{1,0:T(8,128)S(1)} %get-tuple-element.75), channel_id=1, source_target_pairs={{0,16},{1,17},{2,18},{3,19},{4,6},{5,7},{6,4},{7,5},{8,24},{9,25},... | collective-permute-start | bytes 491528 | tf_op jit(solution)/shard_map/ppermute | solution.py:43
  75.1 2.3 %collective-permute-start.10 = (f32[64,640]{1,0:T(8,128)S(1)}, f32[64,640]{1,0:T(8,128)S(1)}, u32[]{:S(2)}, u32[]{:S(2)}) collective-permute-start(f32[64,640]{1,0:T(8,128)S(1)} %get-tuple-element.76), channel_id=1, source_target_pairs={{0,24},{1,25},{2,26},{3,27},{4,7},{5,4},{6,5},{7,6},{8,0},{9,1},{1... | collective-permute-start | bytes 491528 | tf_op jit(solution)/shard_map/ppermute | solution.py:43
  77.4 0.0 collective-permute-start.9
  77.5 1.3 %collective-permute-start.11 = (f32[256,128]{1,0:T(8,128)S(1)}, f32[256,128]{1,0:T(8,128)S(1)}, u32[]{:S(2)}, u32[]{:S(2)}) collective-permute-start(f32[256,128]{1,0:T(8,128)S(1)} %get-tuple-element.69), channel_id=1, source_target_pairs={{0,4},{1,5},{2,6},{3,7},{4,0},{5,1},{6,2},{7,3},{8,12},{9,13},{10,... | collective-permute-start | bytes 393224 | tf_op jit(solution)/shard_map/ppermute | solution.py:43
  78.7 2.1 %collective-permute-done.8 = f32[64,640]{1,0:T(8,128)S(1)} collective-permute-done((f32[64,640]{1,0:T(8,128)S(1)}, f32[64,640]{1,0:T(8,128)S(1)}, u32[]{:S(2)}, u32[]{:S(2)}) %collective-permute-start.8) | collective-permute-done | bytes 163872 | tf_op jit(solution)/shard_map/ppermute | solution.py:43
  80.8 0.5 collective-permute-done.10
  81.3 2.6 %collective-permute-done.9 = f32[64,640]{1,0:T(8,128)S(1)} collective-permute-done((f32[64,640]{1,0:T(8,128)S(1)}, f32[64,640]{1,0:T(8,128)S(1)}, u32[]{:S(2)}, u32[]{:S(2)}) %collective-permute-start.9) | collective-permute-done | bytes 163872 | tf_op jit(solution)/shard_map/ppermute | solution.py:43
  83.9 0.7 fusion.3
  84.6 3.9 %all-to-all-start.3 = ((f32[8,8,640]{2,1,0:T(8,128)}), f32[8,8,640]{2,1,0:T(8,128)S(1)}, u32[]{:S(2)}, u32[]{:S(2)}) async-start(f32[8,8,640]{2,1,0:T(8,128)} %fusion.3), calls=%async_computation.3 | async-start | bytes 327680 | tf_op jit(solution)/shard_map/all_to_all | solution.py:367
  88.5 0.0 collective-permute-done.11.refs_9_
  88.5 0.0 copy-done.10
  88.5 0.0 copy-done.12
  88.5 4.9 %gradients.1 = (bf16[256,512]{1,0:T(8,128)(2,1)}, bf16[256,128]{1,0:T(8,128)(2,1)}, bf16[256,128]{1,0:T(8,128)(2,1)}) custom-call(f32[8]{0:T(128)} %refs_0_.7, s32[8,256]{1,0:T(8,128)} %bitcast.42, bf16[256,512]{1,0:T(8,128)(2,1)} %bitcast.35, bf16[256,128]{1,0:T(8,128)(2,1)} %bitcast.38, bf16[256,128]{1,0:T(8,128)(2,1)} %bitcast.31, ...), custom_call_target="tpu_custom_call" | custom-call | flops 5000000000 | bytes 1581088 | tf_op jit(solution)/shard_map/gradients/pallas_call | solution.py:347
  93.5 3.7 %all-to-all-done.3 = f32[8,8,640]{2,1,0:T(8,128)S(1)} async-done(((f32[8,8,640]{2,1,0:T(8,128)}), f32[8,8,640]{2,1,0:T(8,128)S(1)}, u32[]{:S(2)}, u32[]{:S(2)}) %all-to-all-start.3) | async-done | bytes 163872 | tf_op jit(solution)/shard_map/all_to_all | solution.py:367
  97.2 1.8 %collective-permute-start.14 = (f32[8,640]{1,0:T(8,128)S(1)}, f32[8,640]{1,0:T(8,128)S(1)}, u32[]{:S(2)}, u32[]{:S(2)}) collective-permute-start(f32[8,640]{1,0:T(8,128)S(1)} %reduce_sum.9.refs_0_), channel_id=1, source_target_pairs={{0,3},{1,0},{2,1},{3,2},{4,7},{5,4},{6,5},{7,6},{8,11},{9,8},{10,9... | collective-permute-start | bytes 61448 | tf_op jit(solution)/shard_map/ppermute | solution.py:43
  99.0 0.9 collective-permute-start.13
  99.8 0.8 collective-permute-start.12
  100.7 0.4 collective-permute-done.14.refs_3_
  101.0 3.2 %collective-permute-done.13.refs_2_ = f32[8,640]{1,0:T(8,128)S(1)} collective-permute-done((f32[8,640]{1,0:T(8,128)S(1)}, f32[8,640]{1,0:T(8,128)S(1)}, u32[]{:S(2)}, u32[]{:S(2)}) %collective-permute-start.13) | collective-permute-done | bytes 20512 | tf_op jit(solution)/shard_map/ppermute | solution.py:43
  104.3 0.6 collective-permute-done.12.refs_1_
  104.8 0.6 place.1
  (15 shorter events, 0.2 us)
Async XLA Ops:
  3.2 23.8 %copy-start.4 = (f32[264,128]{1,0:T(8,128)}, f32[264,128]{1,0:T(8,128)S(1)}, u32[]{:S(2)}) copy-start(f32[264,128]{1,0:T(8,128)S(1)} %get-tuple-element.40.refs_0_.refs_3_.refs_1_) | copy-start | bytes 405508
  3.2 1.4 %collective-permute-start = (f32[264,128]{1,0:T(8,128)S(1)}, f32[264,128]{1,0:T(8,128)S(1)}, u32[]{:S(2)}, u32[]{:S(2)}) collective-permute-start(f32[264,128]{1,0:T(8,128)S(1)} %get-tuple-element.41), channel_id=1, source_target_pairs={{0,4},{1,5},{2,6},{3,7},{4,0},{5,1},{6,2},{7,3},{8,12},{9,13},{10,... | collective-permute-start | bytes 405512 | tf_op jit(solution)/shard_map/ppermute | solution.py:43
  5.4 21.6 %all-to-all-start = ((f32[32,1,1152]{2,1,0:T(1,128)}), f32[32,1,1152]{2,1,0:T(1,128)S(1)}, u32[]{:S(2)}, u32[]{:S(2)}) async-start(f32[32,1,1152]{2,1,0:T(1,128)} %chip_forward.1), calls=%async_computation | async-start | bytes 294912 | tf_op jit(solution)/shard_map/all_to_all | solution.py:367
  20.4 0.7 copy-start.11
  21.1 15.4 %copy-start.7 = (f32[256,128]{1,0:T(8,128)}, f32[256,128]{1,0:T(8,128)S(1)}, u32[]{:S(2)}) copy-start(f32[256,128]{1,0:T(8,128)S(1)} %get-tuple-element.46.refs_1_) | copy-start | bytes 393220
  21.1 1.3 %collective-permute-start.1 = (f32[256,128]{1,0:T(8,128)S(1)}, f32[256,128]{1,0:T(8,128)S(1)}, u32[]{:S(2)}, u32[]{:S(2)}) collective-permute-start(f32[256,128]{1,0:T(8,128)S(1)} %get-tuple-element.43), channel_id=1, source_target_pairs={{0,4},{1,5},{2,6},{3,7},{4,0},{5,1},{6,2},{7,3},{8,12},{9,13},{10,... | collective-permute-start | bytes 393224 | tf_op jit(solution)/shard_map/ppermute | solution.py:43
  27.0 23.9 %collective-permute-start.4 = (f32[256,2560]{1,0:T(8,128)S(1)}, f32[256,2560]{1,0:T(8,128)}, u32[]{:S(2)}, u32[]{:S(2)}) collective-permute-start(f32[256,2560]{1,0:T(8,128)S(1)} %get-tuple-element.56), channel_id=1, source_target_pairs={{0,4},{1,5},{2,6},{3,7},{4,0},{5,1},{6,2},{7,3},{8,12},{9,13},{10,... | collective-permute-start | bytes 7864328 | tf_op jit(solution)/shard_map/ppermute | solution.py:43
  27.8 18.0 %all-to-all-start.1 = ((f32[32,16,128]{2,1,0:T(8,128)}), f32[32,16,128]{2,1,0:T(8,128)S(1)}, u32[]{:S(2)}, u32[]{:S(2)}) async-start(f32[32,16,128]{2,1,0:T(8,128)} %scan_forward.1), calls=%async_computation.1 | async-start | bytes 524288 | tf_op jit(solution)/shard_map/all_to_all | solution.py:367
  36.5 1.0 copy-start.2
  37.4 10.8 %copy-start.1 = (bf16[1,256,128]{2,1,0:T(8,128)(2,1)S(1)}, bf16[1,256,128]{2,1,0:T(8,128)(2,1)}, u32[]{:S(2)}) copy-start(bf16[1,256,128]{2,1,0:T(8,128)(2,1)} %param.9) | copy-start | bytes 196612
  45.9 0.9 copy-start.5
  46.8 1.5 %copy-start.3 = (f32[256,1024]{1,0:T(8,128)S(1)}, f32[256,1024]{1,0:T(8,128)}, u32[]{:S(2)}) copy-start(f32[256,1024]{1,0:T(8,128)} %copy-done.2) | copy-start | bytes 3145732
  46.8 2.5 %copy-start.9 = (f32[256,128]{1,0:T(8,128)}, f32[256,128]{1,0:T(8,128)S(1)}, u32[]{:S(2)}) copy-start(f32[256,128]{1,0:T(8,128)S(1)} %get-tuple-element.50.refs_0_.refs_6_) | copy-start | bytes 393220
  46.9 1.4 %collective-permute-start.2 = (f32[256,128]{1,0:T(8,128)S(1)}, f32[256,128]{1,0:T(8,128)S(1)}, u32[]{:S(2)}, u32[]{:S(2)}) collective-permute-start(f32[256,128]{1,0:T(8,128)S(1)} %get-tuple-element.51), channel_id=1, source_target_pairs={{0,4},{1,5},{2,6},{3,7},{4,0},{5,1},{6,2},{7,3},{8,12},{9,13},{10,... | collective-permute-start | bytes 393224 | tf_op jit(solution)/shard_map/ppermute | solution.py:43
  48.3 2.6 %copy-start = (bf16[1,256,2560]{2,1,0:T(8,128)(2,1)S(1)}, bf16[1,256,2560]{2,1,0:T(8,128)(2,1)}, u32[]{:S(2)}) copy-start(bf16[1,256,2560]{2,1,0:T(8,128)(2,1)} %param.13) | copy-start | bytes 3932164
  49.4 1.5 %collective-permute-start.3 = (f32[256,256]{1,0:T(8,128)S(1)}, f32[256,256]{1,0:T(8,128)S(1)}, u32[]{:S(2)}, u32[]{:S(2)}) collective-permute-start(f32[256,256]{1,0:T(8,128)S(1)} %get-tuple-element.55), channel_id=1, source_target_pairs={{0,4},{1,5},{2,6},{3,7},{4,0},{5,1},{6,2},{7,3},{8,12},{9,13},{10,... | collective-permute-start | bytes 786440 | tf_op jit(solution)/shard_map/ppermute | solution.py:43
  54.3 19.4 %collective-permute-start.6 = (f32[4,64,640]{2,1,0:T(8,128)S(1)}, f32[4,64,640]{2,1,0:T(8,128)S(1)}, u32[]{:S(2)}, u32[]{:S(2)}) collective-permute-start(f32[4,64,640]{2,1,0:T(8,128)S(1)} %get-tuple-element.59), channel_id=1, source_target_pairs={{0,2},{1,3},{2,0},{3,1},{4,20},{5,21},{6,22},{7,23},{8,10},{9,11},... | collective-permute-start | bytes 1966088 | tf_op jit(solution)/shard_map/ppermute | solution.py:43
  57.4 16.2 %collective-permute-start.7 = (f32[4,64,640]{2,1,0:T(8,128)S(1)}, f32[4,64,640]{2,1,0:T(8,128)S(1)}, u32[]{:S(2)}, u32[]{:S(2)}) collective-permute-start(f32[4,64,640]{2,1,0:T(8,128)S(1)} %get-tuple-element.60), channel_id=1, source_target_pairs={{0,3},{1,0},{2,1},{3,2},{4,28},{5,29},{6,30},{7,31},{8,11},{9,8},{... | collective-permute-start | bytes 1966088 | tf_op jit(solution)/shard_map/ppermute | solution.py:43
  58.6 15.1 %collective-permute-start.5 = (f32[4,64,640]{2,1,0:T(8,128)S(1)}, f32[4,64,640]{2,1,0:T(8,128)S(1)}, u32[]{:S(2)}, u32[]{:S(2)}) collective-permute-start(f32[4,64,640]{2,1,0:T(8,128)S(1)} %get-tuple-element.58), channel_id=1, source_target_pairs={{0,1},{1,2},{2,3},{3,0},{4,12},{5,13},{6,14},{7,15},{8,9},{9,10},{... | collective-permute-start | bytes 1966088 | tf_op jit(solution)/shard_map/ppermute | solution.py:43
  59.5 17.9 %copy-start.6 = (f32[264,128]{1,0:T(8,128)S(1)}, f32[264,128]{1,0:T(8,128)}, u32[]{:S(2)}) copy-start(f32[264,128]{1,0:T(8,128)} %copy-done.4) | copy-start | bytes 405508
  59.5 17.9 %copy-start.8 = (f32[256,128]{1,0:T(8,128)S(1)}, f32[256,128]{1,0:T(8,128)}, u32[]{:S(2)}) copy-start(f32[256,128]{1,0:T(8,128)} %copy-done.7) | copy-start | bytes 393220
  73.9 14.6 %copy-start.10 = (f32[256,128]{1,0:T(8,128)S(1)}, f32[256,128]{1,0:T(8,128)}, u32[]{:S(2)}) copy-start(f32[256,128]{1,0:T(8,128)} %copy-done.9) | copy-start | bytes 393220
  73.9 14.6 %copy-start.12 = (bf16[256,512]{1,0:T(8,128)(2,1)S(1)}, bf16[256,512]{1,0:T(8,128)(2,1)}, u32[]{:S(2)}) copy-start(bf16[256,512]{1,0:T(8,128)(2,1)} %copy-done.11) | copy-start | bytes 786436
  73.9 6.9 %collective-permute-start.8 = (f32[64,640]{1,0:T(8,128)S(1)}, f32[64,640]{1,0:T(8,128)S(1)}, u32[]{:S(2)}, u32[]{:S(2)}) collective-permute-start(f32[64,640]{1,0:T(8,128)S(1)} %get-tuple-element.75), channel_id=1, source_target_pairs={{0,16},{1,17},{2,18},{3,19},{4,6},{5,7},{6,4},{7,5},{8,24},{9,25},... | collective-permute-start | bytes 491528 | tf_op jit(solution)/shard_map/ppermute | solution.py:43
  75.1 6.2 %collective-permute-start.10 = (f32[64,640]{1,0:T(8,128)S(1)}, f32[64,640]{1,0:T(8,128)S(1)}, u32[]{:S(2)}, u32[]{:S(2)}) collective-permute-start(f32[64,640]{1,0:T(8,128)S(1)} %get-tuple-element.76), channel_id=1, source_target_pairs={{0,24},{1,25},{2,26},{3,27},{4,7},{5,4},{6,5},{7,6},{8,0},{9,1},{1... | collective-permute-start | bytes 491528 | tf_op jit(solution)/shard_map/ppermute | solution.py:43
  77.4 6.5 %collective-permute-start.9 = (f32[64,640]{1,0:T(8,128)S(1)}, f32[64,640]{1,0:T(8,128)S(1)}, u32[]{:S(2)}, u32[]{:S(2)}) collective-permute-start(f32[64,640]{1,0:T(8,128)S(1)} %get-tuple-element.77), channel_id=1, source_target_pairs={{0,8},{1,9},{2,10},{3,11},{4,5},{5,6},{6,7},{7,4},{8,16},{9,17},{1... | collective-permute-start | bytes 491528 | tf_op jit(solution)/shard_map/ppermute | solution.py:43
  77.5 11.1 %collective-permute-start.11 = (f32[256,128]{1,0:T(8,128)S(1)}, f32[256,128]{1,0:T(8,128)S(1)}, u32[]{:S(2)}, u32[]{:S(2)}) collective-permute-start(f32[256,128]{1,0:T(8,128)S(1)} %get-tuple-element.69), channel_id=1, source_target_pairs={{0,4},{1,5},{2,6},{3,7},{4,0},{5,1},{6,2},{7,3},{8,12},{9,13},{10,... | collective-permute-start | bytes 393224 | tf_op jit(solution)/shard_map/ppermute | solution.py:43
  84.6 12.5 %all-to-all-start.3 = ((f32[8,8,640]{2,1,0:T(8,128)}), f32[8,8,640]{2,1,0:T(8,128)S(1)}, u32[]{:S(2)}, u32[]{:S(2)}) async-start(f32[8,8,640]{2,1,0:T(8,128)} %fusion.3), calls=%async_computation.3 | async-start | bytes 327680 | tf_op jit(solution)/shard_map/all_to_all | solution.py:367
  97.2 3.9 %collective-permute-start.14 = (f32[8,640]{1,0:T(8,128)S(1)}, f32[8,640]{1,0:T(8,128)S(1)}, u32[]{:S(2)}, u32[]{:S(2)}) collective-permute-start(f32[8,640]{1,0:T(8,128)S(1)} %reduce_sum.9.refs_0_), channel_id=1, source_target_pairs={{0,3},{1,0},{2,1},{3,2},{4,7},{5,4},{6,5},{7,6},{8,11},{9,8},{10,9... | collective-permute-start | bytes 61448 | tf_op jit(solution)/shard_map/ppermute | solution.py:43
  99.0 5.3 %collective-permute-start.13 = (f32[8,640]{1,0:T(8,128)S(1)}, f32[8,640]{1,0:T(8,128)S(1)}, u32[]{:S(2)}, u32[]{:S(2)}) collective-permute-start(f32[8,640]{1,0:T(8,128)S(1)} %reduce_sum.9.refs_0_), channel_id=1, source_target_pairs={{0,2},{1,3},{2,0},{3,1},{4,6},{5,7},{6,4},{7,5},{8,10},{9,11},{10,... | collective-permute-start | bytes 61448 | tf_op jit(solution)/shard_map/ppermute | solution.py:43
  99.8 5.0 %collective-permute-start.12 = (f32[8,640]{1,0:T(8,128)S(1)}, f32[8,640]{1,0:T(8,128)S(1)}, u32[]{:S(2)}, u32[]{:S(2)}) collective-permute-start(f32[8,640]{1,0:T(8,128)S(1)} %reduce_sum.9.refs_0_), channel_id=1, source_target_pairs={{0,1},{1,2},{2,3},{3,0},{4,5},{5,6},{6,7},{7,4},{8,9},{9,10},{10,1... | collective-permute-start | bytes 61448 | tf_op jit(solution)/shard_map/ppermute | solution.py:43

commit v6 on v5

--- a/solution.py
+++ b/solution.py
@@ -328,7 +328,7 @@
         return self.buffer[at]
 
 
-def call(body, outs, fetch, *args, us=1):
+def call(body, outs, fetch, *args, us=1, grant=None):
     shapes = [jax.ShapeDtypeStruct(s, d) for s, d in outs]
     moved = sum(a.size * a.dtype.itemsize for a in args) + sum(s.size * s.dtype.itemsize for s in shapes)
     scratch = [(pltpu.SMEM if a.ndim == 1 else pltpu.VMEM)(a.shape, a.dtype) for a in args[:fetch]]
@@ -352,7 +352,7 @@
         out_specs=[pl.BlockSpec(memory_space=pltpu.VMEM)] * len(shapes),
         scratch_shapes=scratch,
         cost_estimate=pl.CostEstimate(flops=us * 1_000_000_000, bytes_accessed=moved, transcendentals=0),
-        compiler_params=pltpu.CompilerParams(vmem_limit_bytes=(12 << 20) if fetch else (4 << 20)),
+        compiler_params=pltpu.CompilerParams(vmem_limit_bytes=grant or (12 << 20 if fetch else 4 << 20)),
         name=body.__name__,
     )(*[pltpu.with_memory_space_constraint(a, pltpu.HBM) if n < fetch else a for n, a in enumerate(args)])
     return got if len(got) > 1 else got[0]
@@ -376,7 +376,7 @@
 
     g2 = lax.optimization_barrier((g, chip))[0]
     bmine, bsend, gy, g_wide = call(local_backward, [half, half, tokens, ((TOK, D), f32)], 5,
-                                    a_rate, dt, c, g2, w_out, us=4)
+                                    a_rate, dt, c, g2, w_out, us=4, grant=54 << 20)
     bpeer = permute(bsend, swap_core)
     pieces, bpeer, g_wide = lax.optimization_barrier((pieces, bpeer, g_wide))
     g_peer = permute(g_wide, swap_core)

time: 106 us -> 106 us (level)
  starting transfers between devices: 34.3 us -> 35.7 us
  waiting for transfers between devices: 31.5 us -> 30.4 us
    all_to_all x3, waiting for transfers between devices: 16.7 us -> 15.4 us  [over(): return lax.all_to_all(v, 'seq', 0, 0, axis_index_groups=groups, tiled=True)]
    all_to_all x3, starting transfers between devices: 20.6 us -> 21.9 us  [over(): return lax.all_to_all(v, 'seq', 0, 0, axis_index_groups=groups, tiled=True)]
    unnamed x26 -> x24, local copies, waits for them, and re-layouts: 2.62 us -> 2.83 us
  transfers between devices with their start and end apart: 18 -> 18, of which waited for: 13 -> 13; matrix products, arithmetic and copies ran while one was open for 1% -> 1% of each run, Pallas kernels for 13% -> 15%
where the time goes in v6:
time: 106 us
  starting transfers between devices  35.7 us (34%)
  waiting for transfers between devices  30.4 us (29%)
  Pallas kernels  21.1 us (20%)
  blocking collectives  14.1 us (13%)
  local copies, waits for them, and re-layouts  2.86 us (3%)
    all_to_all x3, starting transfers between devices, over(): return lax.all_to_all(v, 'seq', 0, 0, axis_index_groups=groups, tiled=True)  21.9 us
    pallas_call x12, Pallas kernels, call(): pl.pallas_call(kernel, out_shape=shapes, in_specs=[pl.BlockSpec(memory_sp...  21.1 us
    all_to_all x3, waiting for transfers between devices, over(): return lax.all_to_all(v, 'seq', 0, 0, axis_index_groups=groups, tiled=True)  15.4 us
    ppermute x15, waiting for transfers between devices, permute(): return lax.ppermute(v, BOTH, pairs)  15 us
    all_to_all x1, blocking collectives, over(): return lax.all_to_all(v, 'seq', 0, 0, axis_index_groups=groups, tiled=True)  14.1 us
    ppermute x15, starting transfers between devices, permute(): return lax.ppermute(v, BOTH, pairs)  13.8 us
    unnamed x24, local copies, waits for them, and re-layouts  2.83 us
  transfers between devices with their start and end apart: 18, of which 13 were waited for; matrix products, arithmetic and copies ran while one was open for 1% of the time, Pallas kernels for 15%

profile of v6, /device:TPU:32, one launch (start us, length us, event | category | flops | bytes accessed | tf_op | source)
XLA Modules:
  0.0 105.9 jit_solution(7407371155130490652)
XLA Ops:
  0.6 2.6 %local_forward.1 = (f32[264,128]{1,0:T(8,128)S(1)}, f32[264,128]{1,0:T(8,128)S(1)}) custom-call(f32[8]{0:T(128)} %refs_0_.7, s32[8,256]{1,0:T(8,128)} %bitcast.39, bf16[256,512]{1,0:T(8,128)(2,1)} %bitcast.33, bf16[256,128]{1,0:T(8,128)(2,1)} %bitcast.36), custom_call_target="tpu_custom_call" | custom-call | flops 2000000000 | bytes 606240 | tf_op jit(solution)/shard_map/local_forward/pallas_call | solution.py:347
  3.2 0.0 copy-start.4
  3.2 0.1 collective-permute-start
  3.3 1.3 %collective-permute-done.refs_1_.refs_4_.refs_2_ = f32[264,128]{1,0:T(8,128)S(1)} collective-permute-done((f32[264,128]{1,0:T(8,128)S(1)}, f32[264,128]{1,0:T(8,128)S(1)}, u32[]{:S(2)}, u32[]{:S(2)}) %collective-permute-start) | collective-permute-done | bytes 135200 | tf_op jit(solution)/shard_map/ppermute | solution.py:43
  4.6 0.8 chip_forward.1
  5.4 11.4 %all-to-all-start = ((f32[32,1,1152]{2,1,0:T(1,128)}), f32[32,1,1152]{2,1,0:T(1,128)S(1)}, u32[]{:S(2)}, u32[]{:S(2)}) async-start(f32[32,1,1152]{2,1,0:T(1,128)} %chip_forward.1), calls=%async_computation | async-start | bytes 294912 | tf_op jit(solution)/shard_map/all_to_all | solution.py:367
  16.8 5.3 %local_backward.1 = (f32[256,128]{1,0:T(8,128)}, f32[256,128]{1,0:T(8,128)}, bf16[256,512]{1,0:T(8,128)(2,1)}, f32[256,2560]{1,0:T(8,128)}) custom-call(f32[8]{0:T(128)} %refs_0_.7, s32[8,256]{1,0:T(8,128)} %bitcast.40, bf16[256,128]{1,0:T(8,128)(2,1)} %bitcast.29, bf16[256,2560]{1,0:T(8,128)(2,1)} %bitcast.27, bf16[512,2560]{1,0:T(8,128)(2,1)} %refs_4_.1), custom_call_target="tpu_custom_call" | custom-call | flops 4000000000 | bytes 7151648 | tf_op jit(solution)/shard_map/local_backward/pallas_call | solution.py:347
  22.1 0.1 collective-permute-start.1
  22.2 1.5 %collective-permute-done.1.refs_2_ = f32[256,128]{1,0:T(8,128)S(1)} collective-permute-done((f32[256,128]{1,0:T(8,128)}, f32[256,128]{1,0:T(8,128)S(1)}, u32[]{:S(2)}, u32[]{:S(2)}) %collective-permute-start.1) | collective-permute-done | bytes 131104 | tf_op jit(solution)/shard_map/ppermute | solution.py:43
  23.7 3.3 %all-to-all-done.refs_0_ = f32[32,1,1152]{2,1,0:T(1,128)S(1)} async-done(((f32[32,1,1152]{2,1,0:T(1,128)}), f32[32,1,1152]{2,1,0:T(1,128)S(1)}, u32[]{:S(2)}, u32[]{:S(2)}) %all-to-all-start) | async-done | bytes 147488 | tf_op jit(solution)/shard_map/all_to_all | solution.py:367
  27.0 0.0 collective-permute-start.4
  27.0 0.0 copy-done.4
  27.0 0.9 copy-done.7
  27.9 0.8 scan_forward.1
  28.8 6.6 %all-to-all-start.1 = ((f32[32,16,128]{2,1,0:T(8,128)}), f32[32,16,128]{2,1,0:T(8,128)S(1)}, u32[]{:S(2)}, u32[]{:S(2)}) async-start(f32[32,16,128]{2,1,0:T(8,128)} %scan_forward.1), calls=%async_computation.1 | async-start | bytes 524288 | tf_op jit(solution)/shard_map/all_to_all | solution.py:367
  35.4 3.2 %intra_forward.1.refs_3_ = f32[256,1024]{1,0:T(8,128)S(1)} custom-call(f32[8]{0:T(128)} %refs_0_.7, s32[8,256]{1,0:T(8,128)} %bitcast.41, bf16[256,512]{1,0:T(8,128)(2,1)} %bitcast.34, bf16[256,128]{1,0:T(8,128)(2,1)} %bitcast.37, bf16[256,128]{1,0:T(8,128)(2,1)} %bitcast.30), custom_call_target="tpu_custom_call" | custom-call | flops 3000000000 | bytes 1450016 | tf_op jit(solution)/shard_map/intra_forward/pallas_call | solution.py:347
  38.6 0.0 copy-start.2
  38.6 1.0 copy-done.2
  39.6 8.4 %all-to-all-done.1.refs_0_.refs_1_ = f32[32,16,128]{2,1,0:T(8,128)S(1)} async-done(((f32[32,16,128]{2,1,0:T(8,128)}), f32[32,16,128]{2,1,0:T(8,128)S(1)}, u32[]{:S(2)}, u32[]{:S(2)}) %all-to-all-start.1) | async-done | bytes 262176 | tf_op jit(solution)/shard_map/all_to_all | solution.py:367
  48.0 0.9 copy-done.5
  49.0 0.0 copy-start.9
  49.0 0.1 collective-permute-start.2
  49.1 1.3 %collective-permute-done.2.refs_1_.refs_7_ = f32[256,128]{1,0:T(8,128)S(1)} collective-permute-done((f32[256,128]{1,0:T(8,128)S(1)}, f32[256,128]{1,0:T(8,128)S(1)}, u32[]{:S(2)}, u32[]{:S(2)}) %collective-permute-start.2) | collective-permute-done | bytes 131104 | tf_op jit(solution)/shard_map/ppermute | solution.py:43
  50.5 0.0 copy-done.1
  50.5 0.0 copy-done.3
  50.5 1.1 %forward_out.1 = (bf16[256,512]{1,0:T(8,128)(2,1)}, bf16[256,256]{1,0:T(8,128)(2,1)S(1)}, f32[256,256]{1,0:T(8,128)S(1)}) custom-call(f32[256,128]{1,0:T(8,128)S(1)} %get-tuple-element.50.refs_0_.refs_6_, f32[256,128]{1,0:T(8,128)S(1)} %collective-permute-done.2.refs_1_.refs_7_, bf16[256,128]{1,0:T(8,128)(2,1)S(1)} %bitcast.32, f32[256,1024]{1,0:T(8,128)S(1)} %copy-done.3), custom_call_target="tpu_custom_call" | custom-call | flops 2000000000 | bytes 2031616 | tf_op jit(solution)/shard_map/forward_out/pallas_call | solution.py:347
  51.5 0.0 copy-done.9
  51.5 0.1 collective-permute-start.3
  51.7 1.4 %collective-permute-done.3.refs_1_ = f32[256,256]{1,0:T(8,128)S(1)} collective-permute-done((f32[256,256]{1,0:T(8,128)S(1)}, f32[256,256]{1,0:T(8,128)S(1)}, u32[]{:S(2)}, u32[]{:S(2)}) %collective-permute-start.3) | collective-permute-done | bytes 262176 | tf_op jit(solution)/shard_map/ppermute | solution.py:43
  53.1 0.0 collective-permute-done.4.refs_3_
  53.1 0.0 copy-done
  53.1 1.7 %partial_grad.1 = (f32[4,64,640]{2,1,0:T(8,128)S(1)}, f32[4,64,640]{2,1,0:T(8,128)S(1)}, f32[4,64,640]{2,1,0:T(8,128)S(1)}, f32[4,64,640]{2,1,0:T(8,128)S(1)}) custom-call(bf16[256,256]{1,0:T(8,128)(2,1)S(1)} %get-tuple-element.54.refs_0_, f32[256,256]{1,0:T(8,128)S(1)} %collective-permute-done.3.refs_1_, bf16[256,2560]{1,0:T(8,128)(2,1)S(1)} %bitcast.28, ...), custom_call_target="tpu_custom_call" | custom-call | flops 4000000000 | bytes 6946816 | tf_op jit(solution)/shard_map/partial_grad/pallas_call | solution.py:347
  54.7 3.1 %collective-permute-start.6 = (f32[4,64,640]{2,1,0:T(8,128)S(1)}, f32[4,64,640]{2,1,0:T(8,128)S(1)}, u32[]{:S(2)}, u32[]{:S(2)}) collective-permute-start(f32[4,64,640]{2,1,0:T(8,128)S(1)} %get-tuple-element.59), channel_id=1, source_target_pairs={{0,2},{1,3},{2,0},{3,1},{4,20},{5,21},{6,22},{7,23},{8,10},{9,11},... | collective-permute-start | bytes 1966088 | tf_op jit(solution)/shard_map/ppermute | solution.py:43
  57.9 1.2 %collective-permute-start.7 = (f32[4,64,640]{2,1,0:T(8,128)S(1)}, f32[4,64,640]{2,1,0:T(8,128)S(1)}, u32[]{:S(2)}, u32[]{:S(2)}) collective-permute-start(f32[4,64,640]{2,1,0:T(8,128)S(1)} %get-tuple-element.60), channel_id=1, source_target_pairs={{0,3},{1,0},{2,1},{3,2},{4,28},{5,29},{6,30},{7,31},{8,11},{9,8},{... | collective-permute-start | bytes 1966088 | tf_op jit(solution)/shard_map/ppermute | solution.py:43
  59.0 0.9 collective-permute-start.5
  59.9 0.1 scan_backward.1
  60.0 0.0 copy-start.8
  60.0 14.1 %all_to_all.20.refs_0_ = f32[32,8,128]{2,1,0:T(8,128)S(1)} all-to-all(f32[32,8,128]{2,1,0:T(8,128)S(1)} %scan_backward.1), channel_id=1, replica_groups={{0,8,16,24,32,40,48,56,64,72,80,88,96,104,112,120,128,136,144,152,160,1..., dimensions={0} | all-to-all | bytes 262144 | tf_op jit(solution)/shard_map/all_to_all | solution.py:367
  74.1 0.0 collective-permute-done.6
  74.1 0.0 collective-permute-done.7
  74.1 0.0 collective-permute-done.5
  74.1 0.2 add_add_fusion
  74.3 0.0 copy-start.10
  74.3 0.0 copy-start.11
  74.3 1.2 %collective-permute-start.8 = (f32[64,640]{1,0:T(8,128)S(1)}, f32[64,640]{1,0:T(8,128)S(1)}, u32[]{:S(2)}, u32[]{:S(2)}) collective-permute-start(f32[64,640]{1,0:T(8,128)S(1)} %get-tuple-element.75), channel_id=1, source_target_pairs={{0,16},{1,17},{2,18},{3,19},{4,6},{5,7},{6,4},{7,5},{8,24},{9,25},... | collective-permute-start | bytes 491528 | tf_op jit(solution)/shard_map/ppermute | solution.py:43
  75.6 2.2 %collective-permute-start.10 = (f32[64,640]{1,0:T(8,128)S(1)}, f32[64,640]{1,0:T(8,128)S(1)}, u32[]{:S(2)}, u32[]{:S(2)}) collective-permute-start(f32[64,640]{1,0:T(8,128)S(1)} %get-tuple-element.76), channel_id=1, source_target_pairs={{0,24},{1,25},{2,26},{3,27},{4,7},{5,4},{6,5},{7,6},{8,0},{9,1},{1... | collective-permute-start | bytes 491528 | tf_op jit(solution)/shard_map/ppermute | solution.py:43
  77.8 0.0 collective-permute-start.9
  77.8 0.0 copy-done.6
  77.9 1.3 %collective-permute-start.11 = (f32[256,128]{1,0:T(8,128)S(1)}, f32[256,128]{1,0:T(8,128)S(1)}, u32[]{:S(2)}, u32[]{:S(2)}) collective-permute-start(f32[256,128]{1,0:T(8,128)S(1)} %get-tuple-element.69), channel_id=1, source_target_pairs={{0,4},{1,5},{2,6},{3,7},{4,0},{5,1},{6,2},{7,3},{8,12},{9,13},{10,... | collective-permute-start | bytes 393224 | tf_op jit(solution)/shard_map/ppermute | solution.py:43
  79.1 2.1 %collective-permute-done.8 = f32[64,640]{1,0:T(8,128)S(1)} collective-permute-done((f32[64,640]{1,0:T(8,128)S(1)}, f32[64,640]{1,0:T(8,128)S(1)}, u32[]{:S(2)}, u32[]{:S(2)}) %collective-permute-start.8) | collective-permute-done | bytes 163872 | tf_op jit(solution)/shard_map/ppermute | solution.py:43
  81.3 0.5 collective-permute-done.10
  81.8 2.6 %collective-permute-done.9 = f32[64,640]{1,0:T(8,128)S(1)} collective-permute-done((f32[64,640]{1,0:T(8,128)S(1)}, f32[64,640]{1,0:T(8,128)S(1)}, u32[]{:S(2)}, u32[]{:S(2)}) %collective-permute-start.9) | collective-permute-done | bytes 163872 | tf_op jit(solution)/shard_map/ppermute | solution.py:43
  84.3 0.7 fusion.3
  85.0 3.9 %all-to-all-start.3 = ((f32[8,8,640]{2,1,0:T(8,128)}), f32[8,8,640]{2,1,0:T(8,128)S(1)}, u32[]{:S(2)}, u32[]{:S(2)}) async-start(f32[8,8,640]{2,1,0:T(8,128)} %fusion.3), calls=%async_computation.3 | async-start | bytes 327680 | tf_op jit(solution)/shard_map/all_to_all | solution.py:367
  89.0 0.0 collective-permute-done.11.refs_9_
  89.0 4.9 %gradients.1 = (bf16[256,512]{1,0:T(8,128)(2,1)}, bf16[256,128]{1,0:T(8,128)(2,1)}, bf16[256,128]{1,0:T(8,128)(2,1)}) custom-call(f32[8]{0:T(128)} %refs_0_.7, s32[8,256]{1,0:T(8,128)} %bitcast.42, bf16[256,512]{1,0:T(8,128)(2,1)} %bitcast.35, bf16[256,128]{1,0:T(8,128)(2,1)} %bitcast.38, bf16[256,128]{1,0:T(8,128)(2,1)} %bitcast.31, ...), custom_call_target="tpu_custom_call" | custom-call | flops 5000000000 | bytes 1581088 | tf_op jit(solution)/shard_map/gradients/pallas_call | solution.py:347
  93.9 3.7 %all-to-all-done.3 = f32[8,8,640]{2,1,0:T(8,128)S(1)} async-done(((f32[8,8,640]{2,1,0:T(8,128)}), f32[8,8,640]{2,1,0:T(8,128)S(1)}, u32[]{:S(2)}, u32[]{:S(2)}) %all-to-all-start.3) | async-done | bytes 163872 | tf_op jit(solution)/shard_map/all_to_all | solution.py:367
  97.6 1.8 %collective-permute-start.14 = (f32[8,640]{1,0:T(8,128)S(1)}, f32[8,640]{1,0:T(8,128)S(1)}, u32[]{:S(2)}, u32[]{:S(2)}) collective-permute-start(f32[8,640]{1,0:T(8,128)S(1)} %reduce_sum.9.refs_0_), channel_id=1, source_target_pairs={{0,3},{1,0},{2,1},{3,2},{4,7},{5,4},{6,5},{7,6},{8,11},{9,8},{10,9... | collective-permute-start | bytes 61448 | tf_op jit(solution)/shard_map/ppermute | solution.py:43
  99.4 0.9 collective-permute-start.13
  100.3 0.8 collective-permute-start.12
  101.1 0.4 collective-permute-done.14.refs_3_
  101.5 3.2 %collective-permute-done.13.refs_2_ = f32[8,640]{1,0:T(8,128)S(1)} collective-permute-done((f32[8,640]{1,0:T(8,128)S(1)}, f32[8,640]{1,0:T(8,128)S(1)}, u32[]{:S(2)}, u32[]{:S(2)}) %collective-permute-start.13) | collective-permute-done | bytes 20512 | tf_op jit(solution)/shard_map/ppermute | solution.py:43
  104.7 0.6 collective-permute-done.12.refs_1_
  105.3 0.6 place.1
  (13 shorter events, 0.2 us)
Async XLA Ops:
  3.2 23.8 %copy-start.4 = (f32[264,128]{1,0:T(8,128)}, f32[264,128]{1,0:T(8,128)S(1)}, u32[]{:S(2)}) copy-start(f32[264,128]{1,0:T(8,128)S(1)} %get-tuple-element.40.refs_0_.refs_3_.refs_1_) | copy-start | bytes 405508
  3.2 1.4 %collective-permute-start = (f32[264,128]{1,0:T(8,128)S(1)}, f32[264,128]{1,0:T(8,128)S(1)}, u32[]{:S(2)}, u32[]{:S(2)}) collective-permute-start(f32[264,128]{1,0:T(8,128)S(1)} %get-tuple-element.41), channel_id=1, source_target_pairs={{0,4},{1,5},{2,6},{3,7},{4,0},{5,1},{6,2},{7,3},{8,12},{9,13},{10,... | collective-permute-start | bytes 405512 | tf_op jit(solution)/shard_map/ppermute | solution.py:43
  5.4 21.6 %all-to-all-start = ((f32[32,1,1152]{2,1,0:T(1,128)}), f32[32,1,1152]{2,1,0:T(1,128)S(1)}, u32[]{:S(2)}, u32[]{:S(2)}) async-start(f32[32,1,1152]{2,1,0:T(1,128)} %chip_forward.1), calls=%async_computation | async-start | bytes 294912 | tf_op jit(solution)/shard_map/all_to_all | solution.py:367
  22.1 1.6 %collective-permute-start.1 = (f32[256,128]{1,0:T(8,128)}, f32[256,128]{1,0:T(8,128)S(1)}, u32[]{:S(2)}, u32[]{:S(2)}) collective-permute-start(f32[256,128]{1,0:T(8,128)} %get-tuple-element.43), channel_id=1, source_target_pairs={{0,4},{1,5},{2,6},{3,7},{4,0},{5,1},{6,2},{7,3},{8,12},{9,13},{10,... | collective-permute-start | bytes 393224 | tf_op jit(solution)/shard_map/ppermute | solution.py:43
  27.0 26.1 %collective-permute-start.4 = (f32[256,2560]{1,0:T(8,128)}, f32[256,2560]{1,0:T(8,128)S(1)}, u32[]{:S(2)}, u32[]{:S(2)}) collective-permute-start(f32[256,2560]{1,0:T(8,128)} %get-tuple-element.56), channel_id=1, source_target_pairs={{0,4},{1,5},{2,6},{3,7},{4,0},{5,1},{6,2},{7,3},{8,12},{9,13},{10,... | collective-permute-start | bytes 7864328 | tf_op jit(solution)/shard_map/ppermute | solution.py:43
  27.0 0.9 copy-start.7
  28.8 19.3 %all-to-all-start.1 = ((f32[32,16,128]{2,1,0:T(8,128)}), f32[32,16,128]{2,1,0:T(8,128)S(1)}, u32[]{:S(2)}, u32[]{:S(2)}) async-start(f32[32,16,128]{2,1,0:T(8,128)} %scan_forward.1), calls=%async_computation.1 | async-start | bytes 524288 | tf_op jit(solution)/shard_map/all_to_all | solution.py:367
  38.6 1.0 copy-start.2
  39.6 10.8 %copy-start.1 = (bf16[1,256,128]{2,1,0:T(8,128)(2,1)S(1)}, bf16[1,256,128]{2,1,0:T(8,128)(2,1)}, u32[]{:S(2)}) copy-start(bf16[1,256,128]{2,1,0:T(8,128)(2,1)} %param.9) | copy-start | bytes 196612
  48.0 0.9 copy-start.5
  49.0 1.5 %copy-start.3 = (f32[256,1024]{1,0:T(8,128)S(1)}, f32[256,1024]{1,0:T(8,128)}, u32[]{:S(2)}) copy-start(f32[256,1024]{1,0:T(8,128)} %copy-done.2) | copy-start | bytes 3145732
  49.0 2.5 %copy-start.9 = (f32[256,128]{1,0:T(8,128)}, f32[256,128]{1,0:T(8,128)S(1)}, u32[]{:S(2)}) copy-start(f32[256,128]{1,0:T(8,128)S(1)} %get-tuple-element.50.refs_0_.refs_6_) | copy-start | bytes 393220
  49.0 1.4 %collective-permute-start.2 = (f32[256,128]{1,0:T(8,128)S(1)}, f32[256,128]{1,0:T(8,128)S(1)}, u32[]{:S(2)}, u32[]{:S(2)}) collective-permute-start(f32[256,128]{1,0:T(8,128)S(1)} %get-tuple-element.51), channel_id=1, source_target_pairs={{0,4},{1,5},{2,6},{3,7},{4,0},{5,1},{6,2},{7,3},{8,12},{9,13},{10,... | collective-permute-start | bytes 393224 | tf_op jit(solution)/shard_map/ppermute | solution.py:43
  50.5 2.6 %copy-start = (bf16[1,256,2560]{2,1,0:T(8,128)(2,1)S(1)}, bf16[1,256,2560]{2,1,0:T(8,128)(2,1)}, u32[]{:S(2)}) copy-start(bf16[1,256,2560]{2,1,0:T(8,128)(2,1)} %param.13) | copy-start | bytes 3932164
  51.5 1.5 %collective-permute-start.3 = (f32[256,256]{1,0:T(8,128)S(1)}, f32[256,256]{1,0:T(8,128)S(1)}, u32[]{:S(2)}, u32[]{:S(2)}) collective-permute-start(f32[256,256]{1,0:T(8,128)S(1)} %get-tuple-element.55), channel_id=1, source_target_pairs={{0,4},{1,5},{2,6},{3,7},{4,0},{5,1},{6,2},{7,3},{8,12},{9,13},{10,... | collective-permute-start | bytes 786440 | tf_op jit(solution)/shard_map/ppermute | solution.py:43
  54.7 19.4 %collective-permute-start.6 = (f32[4,64,640]{2,1,0:T(8,128)S(1)}, f32[4,64,640]{2,1,0:T(8,128)S(1)}, u32[]{:S(2)}, u32[]{:S(2)}) collective-permute-start(f32[4,64,640]{2,1,0:T(8,128)S(1)} %get-tuple-element.59), channel_id=1, source_target_pairs={{0,2},{1,3},{2,0},{3,1},{4,20},{5,21},{6,22},{7,23},{8,10},{9,11},... | collective-permute-start | bytes 1966088 | tf_op jit(solution)/shard_map/ppermute | solution.py:43
  57.9 16.2 %collective-permute-start.7 = (f32[4,64,640]{2,1,0:T(8,128)S(1)}, f32[4,64,640]{2,1,0:T(8,128)S(1)}, u32[]{:S(2)}, u32[]{:S(2)}) collective-permute-start(f32[4,64,640]{2,1,0:T(8,128)S(1)} %get-tuple-element.60), channel_id=1, source_target_pairs={{0,3},{1,0},{2,1},{3,2},{4,28},{5,29},{6,30},{7,31},{8,11},{9,8},{... | collective-permute-start | bytes 1966088 | tf_op jit(solution)/shard_map/ppermute | solution.py:43
  59.0 15.1 %collective-permute-start.5 = (f32[4,64,640]{2,1,0:T(8,128)S(1)}, f32[4,64,640]{2,1,0:T(8,128)S(1)}, u32[]{:S(2)}, u32[]{:S(2)}) collective-permute-start(f32[4,64,640]{2,1,0:T(8,128)S(1)} %get-tuple-element.58), channel_id=1, source_target_pairs={{0,1},{1,2},{2,3},{3,0},{4,12},{5,13},{6,14},{7,15},{8,9},{9,10},{... | collective-permute-start | bytes 1966088 | tf_op jit(solution)/shard_map/ppermute | solution.py:43
  60.0 17.8 %copy-start.6 = (f32[264,128]{1,0:T(8,128)S(1)}, f32[264,128]{1,0:T(8,128)}, u32[]{:S(2)}) copy-start(f32[264,128]{1,0:T(8,128)} %copy-done.4) | copy-start | bytes 405508
  60.0 17.8 %copy-start.8 = (f32[256,128]{1,0:T(8,128)S(1)}, f32[256,128]{1,0:T(8,128)}, u32[]{:S(2)}) copy-start(f32[256,128]{1,0:T(8,128)} %get-tuple-element.46.refs_1_) | copy-start | bytes 393220
  74.3 14.6 %copy-start.10 = (f32[256,128]{1,0:T(8,128)S(1)}, f32[256,128]{1,0:T(8,128)}, u32[]{:S(2)}) copy-start(f32[256,128]{1,0:T(8,128)} %copy-done.9) | copy-start | bytes 393220
  74.3 14.6 %copy-start.11 = (bf16[256,512]{1,0:T(8,128)(2,1)S(1)}, bf16[256,512]{1,0:T(8,128)(2,1)}, u32[]{:S(2)}) copy-start(bf16[256,512]{1,0:T(8,128)(2,1)} %get-tuple-element.66.refs_5_) | copy-start | bytes 786436
  74.3 6.9 %collective-permute-start.8 = (f32[64,640]{1,0:T(8,128)S(1)}, f32[64,640]{1,0:T(8,128)S(1)}, u32[]{:S(2)}, u32[]{:S(2)}) collective-permute-start(f32[64,640]{1,0:T(8,128)S(1)} %get-tuple-element.75), channel_id=1, source_target_pairs={{0,16},{1,17},{2,18},{3,19},{4,6},{5,7},{6,4},{7,5},{8,24},{9,25},... | collective-permute-start | bytes 491528 | tf_op jit(solution)/shard_map/ppermute | solution.py:43
  75.6 6.2 %collective-permute-start.10 = (f32[64,640]{1,0:T(8,128)S(1)}, f32[64,640]{1,0:T(8,128)S(1)}, u32[]{:S(2)}, u32[]{:S(2)}) collective-permute-start(f32[64,640]{1,0:T(8,128)S(1)} %get-tuple-element.76), channel_id=1, source_target_pairs={{0,24},{1,25},{2,26},{3,27},{4,7},{5,4},{6,5},{7,6},{8,0},{9,1},{1... | collective-permute-start | bytes 491528 | tf_op jit(solution)/shard_map/ppermute | solution.py:43
  77.8 6.5 %collective-permute-start.9 = (f32[64,640]{1,0:T(8,128)S(1)}, f32[64,640]{1,0:T(8,128)S(1)}, u32[]{:S(2)}, u32[]{:S(2)}) collective-permute-start(f32[64,640]{1,0:T(8,128)S(1)} %get-tuple-element.77), channel_id=1, source_target_pairs={{0,8},{1,9},{2,10},{3,11},{4,5},{5,6},{6,7},{7,4},{8,16},{9,17},{1... | collective-permute-start | bytes 491528 | tf_op jit(solution)/shard_map/ppermute | solution.py:43
  77.9 11.1 %collective-permute-start.11 = (f32[256,128]{1,0:T(8,128)S(1)}, f32[256,128]{1,0:T(8,128)S(1)}, u32[]{:S(2)}, u32[]{:S(2)}) collective-permute-start(f32[256,128]{1,0:T(8,128)S(1)} %get-tuple-element.69), channel_id=1, source_target_pairs={{0,4},{1,5},{2,6},{3,7},{4,0},{5,1},{6,2},{7,3},{8,12},{9,13},{10,... | collective-permute-start | bytes 393224 | tf_op jit(solution)/shard_map/ppermute | solution.py:43
  85.0 12.5 %all-to-all-start.3 = ((f32[8,8,640]{2,1,0:T(8,128)}), f32[8,8,640]{2,1,0:T(8,128)S(1)}, u32[]{:S(2)}, u32[]{:S(2)}) async-start(f32[8,8,640]{2,1,0:T(8,128)} %fusion.3), calls=%async_computation.3 | async-start | bytes 327680 | tf_op jit(solution)/shard_map/all_to_all | solution.py:367
  97.6 3.9 %collective-permute-start.14 = (f32[8,640]{1,0:T(8,128)S(1)}, f32[8,640]{1,0:T(8,128)S(1)}, u32[]{:S(2)}, u32[]{:S(2)}) collective-permute-start(f32[8,640]{1,0:T(8,128)S(1)} %reduce_sum.9.refs_0_), channel_id=1, source_target_pairs={{0,3},{1,0},{2,1},{3,2},{4,7},{5,4},{6,5},{7,6},{8,11},{9,8},{10,9... | collective-permute-start | bytes 61448 | tf_op jit(solution)/shard_map/ppermute | solution.py:43
  99.4 5.3 %collective-permute-start.13 = (f32[8,640]{1,0:T(8,128)S(1)}, f32[8,640]{1,0:T(8,128)S(1)}, u32[]{:S(2)}, u32[]{:S(2)}) collective-permute-start(f32[8,640]{1,0:T(8,128)S(1)} %reduce_sum.9.refs_0_), channel_id=1, source_target_pairs={{0,2},{1,3},{2,0},{3,1},{4,6},{5,7},{6,4},{7,5},{8,10},{9,11},{10,... | collective-permute-start | bytes 61448 | tf_op jit(solution)/shard_map/ppermute | solution.py:43
  100.3 5.0 %collective-permute-start.12 = (f32[8,640]{1,0:T(8,128)S(1)}, f32[8,640]{1,0:T(8,128)S(1)}, u32[]{:S(2)}, u32[]{:S(2)}) collective-permute-start(f32[8,640]{1,0:T(8,128)S(1)} %reduce_sum.9.refs_0_), channel_id=1, source_target_pairs={{0,1},{1,2},{2,3},{3,0},{4,5},{5,6},{6,7},{7,4},{8,9},{9,10},{10,1... | collective-permute-start | bytes 61448 | tf_op jit(solution)/shard_map/ppermute | solution.py:43
